TPU v7x, 32 devices: a whole 2x2x4 slice. The times are simulated.
32 devices in a mesh: dp: 4 (over y, x), row: 2 (over core), col: 4 (over z).
Axes of the slice: x: 2, y: 2, z: 4, core: 2. Of those that a mesh axis runs over, the one named last changes fastest.
Arguments:
- tokens: bfloat16 [16384, 1024], P(('dp', 'row'), 'col'), may hold values from -6 to 6
- segment_ids: int32 [16, 1024], P(('dp', 'row')), may hold values from 0 to 3, never falling along the last dimension, each value on 1 to 768 neighbouring positions
- w_qkv: bfloat16 [1024, 3, 1024], P('row', None, 'col'), may hold values from -0.25 to 0.25
- b_qv: bfloat16 [2, 1024], P(None, 'col'), may hold values from -3 to 3
- w_out: bfloat16 [1024, 1024], P('col', 'row'), may hold values from -0.75 to 0.75
- b_out: bfloat16 [1024], P('col'), may hold values from -3 to 3
- norm1_gain: bfloat16 [1024], P('col'), may hold values from 0.25 to 1.75
- norm1_shift: bfloat16 [1024], P('col'), may hold values from -3 to 3
- w_up: bfloat16 [1024, 4096], P('row', 'col'), may hold values from -0.1875 to 0.1875
- b_up: bfloat16 [4096], P('col'), may hold values from -3 to 3
- w_down: bfloat16 [4096, 1024], P('col', 'row'), may hold values from -0.09375 to 0.09375
- b_down: bfloat16 [1024], P('col'), may hold values from -3 to 3
- norm2_gain: bfloat16 [1024], P('col'), may hold values from 0.25 to 1.75
- norm2_shift: bfloat16 [1024], P('col'), may hold values from -3 to 3
- out_grad: bfloat16 [16384, 1024], P(('dp', 'row'), 'col'), may hold values from -6 to 6
Outputs:
- output: bfloat16 [16384, 1024], P(('dp', 'row'), 'col')
- in_grad: float32 [16384, 1024], P(('dp', 'row'), 'col')
- grad_w_qkv: float32 [1024, 3, 1024], P(('dp', 'row'), None, 'col')
- grad_b_qv: float32 [2, 1024], P(None, 'col')
- grad_w_out: float32 [1024, 1024], P('col', ('dp', 'row'))
- grad_b_out: float32 [1024], P('col')
- grad_norm1_gain: float32 [1024], P('col')
- grad_norm1_shift: float32 [1024], P('col')
- grad_w_up: float32 [1024, 4096], P(('dp', 'row'), 'col')
- grad_b_up: float32 [4096], P('col')
- grad_w_down: float32 [4096, 1024], P('col', ('dp', 'row'))
- grad_b_down: float32 [1024], P('col')
- grad_norm2_gain: float32 [1024], P('col')
- grad_norm2_shift: float32 [1024], P('col')
Inputs may be any that keep to these rules, and one draw needn't show every extreme that they name: `segment_ids`: document numbers never fall along a sequence; a document holds at most 768 positions, and some document holds exactly that many.
All inputs are finite; a program needn't handle non-finite values.
Results may differ from a plain program's by a relative error of at most 0.013.
Values may be sent and summed in bfloat16 or wider, within the bound.
A program may use at most 128 MiB of HBM per device.

v0:
```python
from functools import partial
import math

import jax
import jax.numpy as jnp
from jax import lax
from jax.sharding import PartitionSpec as P

HEAD_DIM = 64


NORM_EPSILON = 1e-05
CONTRACT_LAST = (((1,), (1,)), ((), ()))
CONTRACT_FIRST = (((0,), (0,)), ((), ()))


def gather_width(values):
    return lax.all_gather(values, "col", axis=1, tiled=True)


def sum_width(partial_terms):
    return lax.psum_scatter(partial_terms, "col", scatter_dimension=1, tiled=True)


def normalize(residual, norm_gain, norm_shift):
    feature_count = residual.shape[1] * lax.axis_size("col")
    row_mean = lax.psum(jnp.sum(residual, axis=1, keepdims=True), "col") / feature_count
    centered = residual - row_mean
    row_var = lax.psum(jnp.sum(centered * centered, axis=1, keepdims=True), "col") / feature_count
    inverse = lax.rsqrt(row_var + NORM_EPSILON)
    normed = centered * inverse
    return (normed * norm_gain + norm_shift, normed, inverse)


def normalize_back(incoming, normed, inverse, norm_gain):
    feature_count = incoming.shape[1] * lax.axis_size("col")
    scaled = incoming * norm_gain
    first_sum, second_sum = lax.psum(
        (jnp.sum(scaled, axis=1, keepdims=True), jnp.sum(scaled * normed, axis=1, keepdims=True)),
        "col",
    )
    resid_grad = inverse * (
        scaled - first_sum / feature_count - normed * (second_sum / feature_count)
    )
    return (resid_grad, jnp.sum(incoming * normed, axis=0), jnp.sum(incoming, axis=0))


def expand(left_rows, weight):
    zero_sum = jnp.zeros((left_rows.shape[0], weight.shape[1]), jnp.float32)
    weight_piece = lax.all_gather(weight, "row", axis=0, tiled=True)
    left_cols = lax.dynamic_slice_in_dim(left_rows, jnp.int32(0), weight_piece.shape[0], 1)
    return zero_sum + jnp.dot(left_cols, weight_piece, preferred_element_type=jnp.float32)


def project(left_rows, weight):
    return jnp.dot(
        left_rows,
        lax.all_gather(weight, "row", axis=1, tiled=True),
        preferred_element_type=jnp.float32,
    )


def project_back(grad_rows, weight):
    zero_sum = jnp.zeros((grad_rows.shape[0], weight.shape[0]), jnp.float32)
    weight_piece = lax.all_gather(weight, "row", axis=1, tiled=True)
    grad_cols = lax.dynamic_slice_in_dim(grad_rows, jnp.int32(0), weight_piece.shape[1], 1)
    return zero_sum + lax.dot_general(
        grad_cols, weight_piece, CONTRACT_LAST, preferred_element_type=jnp.float32
    )


def expand_back(grad_rows, weight):
    return lax.dot_general(
        grad_rows,
        lax.all_gather(weight, "row", axis=0, tiled=True),
        CONTRACT_LAST,
        preferred_element_type=jnp.float32,
    )


def block_scores(query_block, key_rows, segments, block_start, score_scale):
    block_rows = query_block.shape[0]
    scores = (
        jnp.einsum("qhd,khd->hqk", query_block, key_rows, preferred_element_type=jnp.float32)
        * score_scale
    )
    same_doc = (
        lax.dynamic_slice_in_dim(segments, block_start, block_rows, 0)[:, None] == segments[None, :]
    )
    return jnp.where(same_doc[None], scores, -1000000000.0)


def attend(queries, key_rows, value_rows, segments, score_scale):
    seq_len = queries.shape[0]
    block_rows = min(512, seq_len)
    context_blocks = []
    total_blocks = []
    for block_start in range(0, seq_len, block_rows):
        query_block = queries[block_start : block_start + block_rows]
        scores = block_scores(query_block, key_rows, segments, block_start, score_scale)
        row_max = jnp.max(scores, axis=-1, keepdims=True)
        exp_terms = jnp.exp(scores - row_max)
        row_total = jnp.sum(exp_terms, axis=-1, keepdims=True)
        attn_prob = exp_terms / row_total
        prob_low = attn_prob.astype(jnp.bfloat16)
        context = jnp.einsum(
            "hqk,khd->qhd", prob_low, value_rows, preferred_element_type=jnp.float32
        )
        context_blocks.append(context.astype(jnp.bfloat16))
        total_blocks.append((row_max + jnp.log(row_total))[..., 0])
    return (jnp.concatenate(context_blocks, axis=0), jnp.concatenate(total_blocks, axis=1))


def attend_back(queries, key_rows, value_rows, segments, log_total, context_grad, score_scale):
    seq_len = queries.shape[0]
    block_rows = min(512, seq_len)
    key_grad = jnp.zeros(key_rows.shape, jnp.float32)
    value_grad = jnp.zeros(value_rows.shape, jnp.float32)
    query_blocks = []
    for block_start in range(0, seq_len, block_rows):
        query_block = queries[block_start : block_start + block_rows]
        grad_block = context_grad[block_start : block_start + block_rows]
        scores = block_scores(query_block, key_rows, segments, block_start, score_scale)
        attn_prob = jnp.exp(scores - log_total[:, block_start : block_start + block_rows, None])
        prob_grad = jnp.einsum(
            "qhd,khd->hqk", grad_block, value_rows, preferred_element_type=jnp.float32
        )
        delta_rows = jnp.sum(attn_prob * prob_grad, axis=-1, keepdims=True)
        score_grad = (attn_prob * (prob_grad - delta_rows)).astype(jnp.bfloat16)
        query_blocks.append(
            jnp.einsum("hqk,khd->qhd", score_grad, key_rows, preferred_element_type=jnp.float32)
            * score_scale
        )
        key_grad = (
            key_grad
            + jnp.einsum(
                "hqk,qhd->khd", score_grad, query_block, preferred_element_type=jnp.float32
            )
            * score_scale
        )
        value_grad = value_grad + jnp.einsum(
            "hqk,qhd->khd",
            attn_prob.astype(jnp.bfloat16),
            grad_block,
            preferred_element_type=jnp.float32,
        )
    return (jnp.concatenate(query_blocks, axis=0), key_grad, value_grad)


def on_device(
    tokens,
    segment_ids,
    w_qkv,
    b_qv,
    w_out,
    b_out,
    norm1_gain,
    norm1_shift,
    w_up,
    b_up,
    w_down,
    b_down,
    norm2_gain,
    norm2_shift,
    out_grad,
):
    token_rows, width_part = tokens.shape
    seqs_here, seq_len = segment_ids.shape
    heads_here = width_part // HEAD_DIM
    score_scale = 1.0 / math.sqrt(HEAD_DIM)
    qkv_flat = w_qkv.reshape(w_qkv.shape[0], 3 * width_part)
    token_whole = gather_width(tokens)
    projected = expand(token_whole, qkv_flat)
    queries = (projected[:, :width_part] + b_qv[0]).astype(jnp.bfloat16)
    key_rows = projected[:, width_part : 2 * width_part].astype(jnp.bfloat16)
    value_rows = (projected[:, 2 * width_part :] + b_qv[1]).astype(jnp.bfloat16)
    split_shape = (seqs_here, seq_len, heads_here, HEAD_DIM)
    query_split = queries.reshape(split_shape)
    key_split = key_rows.reshape(split_shape)
    value_split = value_rows.reshape(split_shape)
    context_split, log_total = lax.map(
        lambda packed: attend(packed[0], packed[1], packed[2], packed[3], score_scale),
        (query_split, key_split, value_split, segment_ids),
    )
    context = context_split.reshape(token_rows, width_part)
    attn_term = sum_width(project(context, w_out))
    residual_one = tokens.astype(jnp.float32) + attn_term + b_out
    hidden_one, normed_one, inverse_one = normalize(residual_one, norm1_gain, norm1_shift)
    hidden_low = hidden_one.astype(jnp.bfloat16)
    hidden_whole = gather_width(hidden_low)
    up_proj = expand(hidden_whole, w_up) + b_up
    activated_full, gelu_pull = jax.vjp(partial(jax.nn.gelu, approximate=False), up_proj)
    activated = activated_full.astype(jnp.bfloat16)
    residual_two = hidden_one + sum_width(project(activated, w_down)) + b_down
    output, normed_two, inverse_two = normalize(residual_two, norm2_gain, norm2_shift)
    resid_two_grad, gain_two_grad, shift_two_grad = normalize_back(
        out_grad.astype(jnp.float32), normed_two, inverse_two, norm2_gain
    )
    mix_low = resid_two_grad.astype(jnp.bfloat16)
    mix_whole = gather_width(mix_low)
    down_wgrad = lax.dot_general(
        activated, mix_whole, CONTRACT_FIRST, preferred_element_type=jnp.float32
    )
    activated_grad = project_back(mix_whole, w_down)
    up_grad = gelu_pull(activated_grad)[0]
    up_low = up_grad.astype(jnp.bfloat16)
    up_wgrad = lax.dot_general(
        hidden_whole, up_low, CONTRACT_FIRST, preferred_element_type=jnp.float32
    )
    hidden_grad = sum_width(expand_back(up_low, w_up)) + resid_two_grad
    resid_one_grad, gain_one_grad, shift_one_grad = normalize_back(
        hidden_grad, normed_one, inverse_one, norm1_gain
    )
    attn_low = resid_one_grad.astype(jnp.bfloat16)
    attn_whole = gather_width(attn_low)
    out_wgrad = lax.dot_general(
        context, attn_whole, CONTRACT_FIRST, preferred_element_type=jnp.float32
    )
    down_share, out_share = (
        lax.psum_scatter(down_wgrad, ("dp", "row"), scatter_dimension=1, tiled=True),
        lax.psum_scatter(out_wgrad, ("dp", "row"), scatter_dimension=1, tiled=True),
    )
    context_grad = project_back(attn_whole, w_out).astype(jnp.bfloat16)
    query_grad, key_grad, value_grad = lax.map(
        lambda packed: attend_back(
            packed[0], packed[1], packed[2], packed[3], packed[4], packed[5], score_scale
        ),
        (
            query_split,
            key_split,
            value_split,
            segment_ids,
            log_total,
            context_grad.reshape(split_shape),
        ),
    )
    query_grad = query_grad.reshape(token_rows, width_part)
    key_grad = key_grad.reshape(token_rows, width_part)
    value_grad = value_grad.reshape(token_rows, width_part)
    qkv_low = jnp.concatenate(
        [
            query_grad.astype(jnp.bfloat16),
            key_grad.astype(jnp.bfloat16),
            value_grad.astype(jnp.bfloat16),
        ],
        axis=1,
    )
    qkv_wgrad = lax.dot_general(
        token_whole, qkv_low, CONTRACT_FIRST, preferred_element_type=jnp.float32
    )
    in_grad = sum_width(expand_back(qkv_low, qkv_flat)) + resid_one_grad
    qkv_share, up_share = (
        lax.psum_scatter(qkv_wgrad, ("dp", "row"), scatter_dimension=0, tiled=True),
        lax.psum_scatter(up_wgrad, ("dp", "row"), scatter_dimension=0, tiled=True),
    )
    bias_qv_grad = jnp.stack([jnp.sum(query_grad, axis=0), jnp.sum(value_grad, axis=0)])
    small_sums = lax.psum(
        (
            bias_qv_grad,
            jnp.sum(resid_one_grad, axis=0),
            gain_one_grad,
            shift_one_grad,
            jnp.sum(up_grad, axis=0),
            jnp.sum(resid_two_grad, axis=0),
            gain_two_grad,
            shift_two_grad,
        ),
        ("dp", "row"),
    )
    return (
        output.astype(jnp.bfloat16),
        in_grad,
        qkv_share.reshape(qkv_share.shape[0], 3, width_part),
        small_sums[0],
        out_share,
        small_sums[1],
        small_sums[2],
        small_sums[3],
        up_share,
        small_sums[4],
        down_share,
        small_sums[5],
        small_sums[6],
        small_sums[7],
    )


def solution(mesh):
    return jax.shard_map(
        on_device,
        mesh=mesh,
        in_specs=(
            P(("dp", "row"), "col"),
            P(("dp", "row"), None),
            P("row", None, "col"),
            P(None, "col"),
            P("col", "row"),
            P("col"),
            P("col"),
            P("col"),
            P("row", "col"),
            P("col"),
            P("col", "row"),
            P("col"),
            P("col"),
            P("col"),
            P(("dp", "row"), "col"),
        ),
        out_specs=(
            P(("dp", "row"), "col"),
            P(("dp", "row"), "col"),
            P(("dp", "row"), None, "col"),
            P(None, "col"),
            P("col", ("dp", "row")),
            P("col"),
            P("col"),
            P("col"),
            P(("dp", "row"), "col"),
            P("col"),
            P("col", ("dp", "row")),
            P("col"),
            P("col"),
            P("col"),
        ),
        check_vma=False,
    )
```

profile of v0, /device:TPU:9, one launch (start us, length us, event | category | flops | bytes accessed | tf_op | source)
XLA Modules:
  0.0 1456.2 jit_solution(11667290038889355418)
XLA Ops:
  14.8 7.1 all-gather.10.cloned.1.call-done
  21.8 79.7 %all-gather.8.cloned.1.call-done = bf16[2048,1024]{1,0:T(8,128)(2,1)} async-done(((bf16[2048,256]{1,0:T(8,128)(2,1)}), bf16[2048,1024]{1,0:T(8,128)(2,1)}) %all-gather.8.cloned.1.call-update) | async-done | bytes 4194320 | tf_op jit(solution)/shard_map/all_gather | solution.py:18
  101.5 5.7 fusion.114
  124.0 31.2 %while.26 = (s32[]{:T(128)}, bf16[2,1024,4,64]{1,3,2,0:T(8,128)(2,1)}, f32[2,4,1024]{2,1,0:T(4,128)S(1)}, bf16[2,1024,4,64]{1,3,2,0:T(8,128)(2,1)S(1)}, s32[2,10...) while((s32[]{:T(128)}, ...), condition=%wide.region_5.6_spmd, body=%wide.region_0.5_spmd.sunk | while | flops 1126432768 | bytes 67300040 | solution.py:181
  164.1 144.7 %reduce-scatter.9.cloned.1.call-done = f32[2048,256]{1,0:T(8,128)} async-done(((f32[2048,1024]{1,0:T(8,128)}), f32[2048,256]{1,0:T(8,128)}) %reduce-scatter.9.cloned.1.call-update) | async-done | bytes 2097168 | tf_op jit(solution)/shard_map/reduce_scatter | solution.py:22
  312.2 8.6 psum.112
  323.1 8.6 psum.113
  335.2 80.4 %all-gather.12.cloned.1.call-done = bf16[2048,1024]{1,0:T(8,128)(2,1)} async-done(((bf16[2048,256]{1,0:T(8,128)(2,1)}), bf16[2048,1024]{1,0:T(8,128)(2,1)}) %all-gather.12.cloned.1.call-update) | async-done | bytes 4194320 | tf_op jit(solution)/shard_map/all_gather | solution.py:18
  415.6 26.2 %multiply_convert_fusion.2 = (bf16[2048,1024]{1,0:T(8,128)(2,1)}, f32[2048,1024]{1,0:T(8,128)}, f32[2048,1024]{1,0:T(8,128)}) fusion(f32[1024]{0:T(1024)S(1)} %convert_element_type.116, bf16[2048,1024]{1,0:T(8,128)(2,1)} %all-gather.12.cloned.1.call-done, bf16[1024,1024]{1,0:T(8,128)(2,1)} %all-gather.14.cloned.1.call-done), kind=kOutput, calls=%fused_computation.114 | convolution fusion | flops 4433379328 | bytes 27267072 | tf_op jit(solution)/shard_map/dot_general | solution.py:52
  441.8 10.6 fusion.116
  453.1 144.7 %reduce-scatter.11.cloned.1.call-done = f32[2048,256]{1,0:T(8,128)} async-done(((f32[2048,1024]{1,0:T(8,128)}), f32[2048,256]{1,0:T(8,128)}) %reduce-scatter.11.cloned.1.call-update) | async-done | bytes 2097168 | tf_op jit(solution)/shard_map/reduce_scatter | solution.py:22
  601.4 8.1 psum.114
  611.7 8.7 psum.115
  623.7 10.5 all-reduce.2
  641.7 86.7 %all-gather.18.cloned.1.call-done = bf16[2048,1024]{1,0:T(8,128)(2,1)} async-done(((bf16[2048,256]{1,0:T(8,128)(2,1)}), bf16[2048,1024]{1,0:T(8,128)(2,1)}) %all-gather.18.cloned.1.call-update) | async-done | bytes 4194320 | tf_op jit(solution)/shard_map/all_gather | solution.py:18
  728.4 14.0 fusion.106
  744.4 6.9 fusion.101
  751.4 145.4 %reduce-scatter.13.cloned.1.call-done = f32[2048,256]{1,0:T(8,128)} async-done(((f32[2048,1024]{1,0:T(8,128)}), f32[2048,256]{1,0:T(8,128)}) %reduce-scatter.13.cloned.1.call-update) | async-done | bytes 2097168 | tf_op jit(solution)/shard_map/reduce_scatter | solution.py:22
  901.6 11.7 all-reduce.1
  920.1 82.9 %all-gather.20.cloned.1.call-done = bf16[2048,1024]{1,0:T(8,128)(2,1)} async-done(((bf16[2048,256]{1,0:T(8,128)(2,1)}), bf16[2048,1024]{1,0:T(8,128)(2,1)}) %all-gather.20.cloned.1.call-update) | async-done | bytes 4194320 | tf_op jit(solution)/shard_map/all_gather | solution.py:18
  1016.1 72.8 %while.27 = (s32[]{:T(128)}, f32[2,1024,4,64]{1,3,2,0:T(8,128)}, bf16[2,1024,4,64]{1,3,2,0:T(8,128)(2,1)}, f32[2,1024,4,64]{1,3,2,0:T(8,128)}, bf16[2,1024,4,64]...) while((s32[]{:T(128)}, f32[2,1024,4,64]{1,3,2,0:T(8,128)}, ...), condition=%wide.region_28.29_spmd, body=%wide.region_25.28_spmd.sunk | while | flops 2749624320 | bytes 174243632 | solution.py:224
  1030.9 5.3 multiply_reduce_fusion.10
  1036.2 8.3 multiply_convert_fusion.4
  1072.3 8.3 multiply_convert_fusion.4
  1105.3 7.7 fusion.117
  1113.2 10.7 fusion.99
  1123.9 10.0 fusion.119
  1139.9 21.8 %all-reduce = (f32[2,256]{1,0:T(2,128)}, f32[256]{0:T(256)}, f32[256]{0:T(256)}, f32[256]{0:T(256)}, f32[1024]{0:T(1024)}, /*index=5*/f32[256]{0:T(256)}, f32[256]{0:T(256)}, f32[256]{0:T(256)}) all-reduce(f32[2,256]{1,0:T(2,128)S(1)} %pad_maximum_fusion, ...), channel_id=1, replica_groups=mesh['dp'=4,'row'=2,'col'=4] {'dp','row'}, use_global_device_ids=true, to_apply=%region_33.34 | all-reduce | flops 3072 | bytes 24576 | tf_op jit(solution)/shard_map/psum | solution.py:257
  1163.7 135.4 %reduce-scatter.15.cloned.1.call-done = f32[2048,256]{1,0:T(8,128)} async-done(((f32[2048,1024]{1,0:T(8,128)}), f32[2048,256]{1,0:T(8,128)}) %reduce-scatter.15.cloned.1.call-update) | async-done | bytes 2097168 | tf_op jit(solution)/shard_map/reduce_scatter | solution.py:22
  1302.3 52.9 %reduce-scatter.21.cloned.1.call-done = f32[128,1024]{1,0:T(8,128)} async-done(((f32[1024,1024]{1,0:T(8,128)}), f32[128,1024]{1,0:T(8,128)}) %reduce-scatter.21.cloned.1.call-update) | async-done | bytes 524304 | tf_op jit(solution)/shard_map/reduce_scatter | solution.py:254
  1355.2 54.9 %reduce-scatter.23.cloned.1.call-done = f32[1024,128]{1,0:T(8,128)} async-done(((f32[1024,1024]{1,0:T(8,128)}), f32[1024,128]{1,0:T(8,128)}) %reduce-scatter.23.cloned.1.call-update) | async-done | bytes 524304 | tf_op jit(solution)/shard_map/reduce_scatter | solution.py:220
  1410.0 39.4 %reduce-scatter.19.cloned.1.call-done = f32[256,128]{1,0:T(8,128)} async-done(((f32[256,1024]{1,0:T(8,128)}), f32[256,128]{1,0:T(8,128)}) %reduce-scatter.19.cloned.1.call-update) | async-done | bytes 131088 | tf_op jit(solution)/shard_map/reduce_scatter | solution.py:221
  (239 shorter events, 194.5 us)
Async XLA Ops:
  7.2 7.6 copy-start.24
  7.2 14.6 %all-gather.10.cloned.1.call-start = ((), (), s32[]{:S(2)}) async-start(), calls=%async_computation.9 | async-start | bytes 2359296 | tf_op jit(solution)/shard_map/all_gather | solution.py:50
  9.6 91.9 %all-gather.8.cloned.1.call-start = ((), (), s32[]{:S(2)}) async-start(), calls=%async_computation.8 | async-start | bytes 5242880 | tf_op jit(solution)/shard_map/all_gather | solution.py:18
  10.3 298.5 %reduce-scatter.9.cloned.1.call-start = ((), (), s32[]{:S(2)}) async-start(), calls=%async_computation.10 | async-start | bytes 10485760 | tf_op jit(solution)/shard_map/reduce_scatter | solution.py:22
  111.8 7.5 copy-start.6
  116.3 7.7 copy-start.15
  151.3 2.9 copy-start.10
  155.2 3.6 copy-start.7
  163.4 171.8 %all-gather.14.cloned.1.call-start = ((), (), s32[]{:S(2)}) async-start(), calls=%async_computation.12 | async-start | bytes 3145728 | tf_op jit(solution)/shard_map/all_gather | solution.py:50
  164.0 251.6 %all-gather.12.cloned.1.call-start = ((), (), s32[]{:S(2)}) async-start(), calls=%async_computation.11 | async-start | bytes 5242880 | tf_op jit(solution)/shard_map/all_gather | solution.py:18
  312.2 22.9 %copy-start.25 = (bf16[1024]{0:T(1024)(128)(2,1)S(1)}, bf16[1024]{0:T(1024)(128)(2,1)}, u32[]{:S(2)}) copy-start(bf16[1024]{0:T(1024)(128)(2,1)} %param.28) | copy-start | bytes 6148
  334.5 107.3 %all-gather.16.cloned.1.call-start = ((), (), s32[]{:S(2)}) async-start(), calls=%async_computation.13 | async-start | bytes 3145728 | tf_op jit(solution)/shard_map/all_gather | solution.py:58
  335.1 262.7 %reduce-scatter.11.cloned.1.call-start = ((), (), s32[]{:S(2)}) async-start(), calls=%async_computation.14 | async-start | bytes 10485760 | tf_op jit(solution)/shard_map/reduce_scatter | solution.py:22
  452.4 275.9 %all-gather.18.cloned.1.call-start = ((), (), s32[]{:S(2)}) async-start(), calls=%async_computation.15 | async-start | bytes 5242880 | tf_op jit(solution)/shard_map/all_gather | solution.py:18
  641.7 255.1 %reduce-scatter.13.cloned.1.call-start = ((), (), s32[]{:S(2)}) async-start(), calls=%async_computation.16 | async-start | bytes 10485760 | tf_op jit(solution)/shard_map/reduce_scatter | solution.py:22
  728.4 16.0 %copy-start.27 = (bf16[1024,1024]{1,0:T(8,128)(2,1)S(1)}, bf16[1024,1024]{1,0:T(8,128)(2,1)}, u32[]{:S(2)}) copy-start(bf16[1024,1024]{1,0:T(8,128)(2,1)} %all-gather.14.cloned.1.call-done) | copy-start | bytes 6291460
  751.3 251.7 %all-gather.20.cloned.1.call-start = ((), (), s32[]{:S(2)}) async-start(), calls=%async_computation.17 | async-start | bytes 5242880 | tf_op jit(solution)/shard_map/all_gather | solution.py:18
  920.0 241.6 %reduce-scatter.17.cloned.1.call-start = ((), (), s32[]{:S(2)}) async-start(), calls=%async_computation.19 | async-start | bytes 3538944 | tf_op jit(solution)/shard_map/reduce_scatter | solution.py:253
  1096.7 3.3 copy-start.26
  1100.0 5.3 copy-start.28
  1105.2 193.8 %reduce-scatter.15.cloned.1.call-start = ((), (), s32[]{:S(2)}) async-start(), calls=%async_computation.18 | async-start | bytes 10485760 | tf_op jit(solution)/shard_map/reduce_scatter | solution.py:22
  1113.0 242.2 %reduce-scatter.21.cloned.1.call-start = ((), (), s32[]{:S(2)}) async-start(), calls=%async_computation.21 | async-start | bytes 4718592 | tf_op jit(solution)/shard_map/reduce_scatter | solution.py:254
  1123.9 286.1 %reduce-scatter.23.cloned.1.call-start = ((), (), s32[]{:S(2)}) async-start(), calls=%async_computation.22 | async-start | bytes 4718592 | tf_op jit(solution)/shard_map/reduce_scatter | solution.py:220
  1134.0 5.8 copy-start.17
  1134.0 5.8 copy-start.18
  1134.0 5.8 copy-start.19
  1134.0 5.8 copy-start.20
  1134.0 5.8 copy-start.21
  1134.0 5.8 copy-start.22
  1134.0 5.8 copy-start.23
  1134.1 165.0 %copy-start.1 = (f32[2048,256]{1,0:T(8,128)S(1)}, f32[2048,256]{1,0:T(8,128)}, u32[]{:S(2)}) copy-start(f32[2048,256]{1,0:T(8,128)} %copy-done) | copy-start | bytes 6291460
  1134.1 315.4 %reduce-scatter.19.cloned.1.call-start = ((), (), s32[]{:S(2)}) async-start(), calls=%async_computation.20 | async-start | bytes 1179648 | tf_op jit(solution)/shard_map/reduce_scatter | solution.py:221
  (26 other events, 33.1 us)
Sparse Core Ops, SparseCore 0:
  10.1 11.6 all-gather.9
  23.4 78.0 all-gather.7
  163.5 145.2 reduce-scatter.8
  310.2 12.3 all-gather.13
  334.6 80.8 all-gather.11
  417.0 12.3 all-gather.15
  452.6 145.2 reduce-scatter.10
  641.8 86.5 all-gather.17
  751.4 145.2 reduce-scatter.12
  920.2 82.8 all-gather.19
  1105.4 47.2 reduce-scatter.16
  1154.9 144.1 reduce-scatter.14
  1303.0 52.1 reduce-scatter.20
  1359.0 51.0 reduce-scatter.22
  1413.6 35.7 reduce-scatter.18
where the time goes:
time: 1460 us
  waiting for transfers between devices  1060 us (73%)
  matrix products  176 us (12%)
  blocking collectives  82.4 us (6%)
  other arithmetic  71.2 us (5%)
  local copies, waits for them, and re-layouts  54.2 us (4%)
  between operations  14.7 us (1%)
    reduce_scatter x4, waiting for transfers between devices, sum_width(): lax.psum_scatter(partial_terms, 'col', scatter_dimension=1, tiled=True)  570 us
    all_gather x4, waiting for transfers between devices, gather_width(): return lax.all_gather(values, 'col', axis=1, tiled=True)  330 us
    reduce_scatter x1, waiting for transfers between devices, on_device(): lax.psum_scatter(down_wgrad, ('dp', 'row'), scatter_dimension=1, tiled=True)  54.9 us
    reduce_scatter x1, waiting for transfers between devices, on_device(): lax.psum_scatter(up_wgrad, ('dp', 'row'), scatter_dimension=0, tiled=True)  52.9 us
    reduce_scatter x1, waiting for transfers between devices, on_device(): lax.psum_scatter(out_wgrad, ('dp', 'row'), scatter_dimension=1, tiled=True)  39.4 us
    dot_general x2, matrix products, expand(): jnp.dot(left_cols, weight_piece, preferred_element_type=jnp.float32)  31.9 us
  transfers between devices with their start and end apart: 15, of which 12 were waited for; matrix products, arithmetic and copies ran while one was open for 5% of the time, Pallas kernels for 0%

commit v1 on v0

v1 whole, which is shorter than its diff:
```python
from functools import partial
import math

import jax
import jax.numpy as jnp
from jax import lax
from jax.experimental import pallas as pl
from jax.experimental.pallas import tpu as pltpu
from jax.sharding import Mesh, PartitionSpec as P

HEAD_DIM = 64
NORM_EPSILON = 1e-05
MESH = pl.DeviceIdType.MESH
LOG2E = math.log2(math.e)
BF = jnp.bfloat16
F32 = jnp.float32
CONTRACT_LAST = (((1,), (1,)), ((), ()))
CONTRACT_FIRST = (((0,), (0,)), ((), ()))
VMEM_LIMIT = 62 * 2**20


def wait_for(ref, sem):
    pltpu.make_async_copy(ref, ref, sem).wait()


def ds(start, size, multiple=128):
    return pl.ds(pl.multiple_of(start, multiple), size)


def gather_kernel(
    tok, og, par, wq, wo, wu, wd,
    xf, ogh, parf, wqf, wof, wuf, wdf,
    send_a, recv_a, send_b, recv_b, recv_l, send_l, send_t, recv_t, send_m, recv_m, send_g, recv_g, send_p, recv_p,
):
    d, r, c = lax.axis_index("dp"), lax.axis_index("core"), lax.axis_index("col")
    owner, j0 = c // 2, lax.rem(c, 2)
    half = tok.shape[0] // 4
    barrier = pltpu.get_barrier_semaphore()
    for s in range(4):
        for o in range(2):
            if s or o:
                target = {"core": lax.rem(r + o, 2), "col": lax.rem(c + s, 4)}
                pl.semaphore_signal(barrier, inc=1, device_id=target, device_id_type=MESH)
    peers = [lax.bitwise_xor(d, p) for p in (1, 2, 3)]
    for p in peers:
        pl.semaphore_signal(barrier, inc=1, device_id={"dp": p}, device_id_type=MESH)
    pl.semaphore_wait(barrier, 10)

    source, dest = (wq, wo, wu, wd), (wqf, wof, wuf, wdf)

    def whole(w, rr, j):
        rows, cols = source[w].shape
        if w in (0, 2):
            return dest[w].at[ds(rr * rows, rows), ds(j * cols, cols)]
        return dest[w].at[ds(j * rows, rows), ds(rr * cols, cols)]

    def piece(w, rr, dd, j):
        rows, cols = source[w].shape
        part = rows // 4
        if w in (0, 2):
            return dest[w].at[ds(rr * rows + dd * part, part, 64), ds(j * cols, cols)]
        return dest[w].at[ds(j * rows + dd * part, part, 64), ds(rr * cols, cols)]

    def a_copy(w, s):
        part = source[w].shape[0] // 4
        return pltpu.make_async_remote_copy(
            source[w].at[ds(d * part, part, 64)], piece(w, r, d, j0), send_a.at[w, s - 1], recv_a.at[w, j0 * 2 + r],
            device_id={"core": owner, "col": lax.rem(c + s, 4)}, device_id_type=MESH)

    def mate_part(w):
        return pltpu.make_async_remote_copy(
            source[w], whole(w, r, j0), send_l.at[w], recv_l.at[w], device_id={"core": 1 - r}, device_id_type=MESH)

    def start_a(w):
        for s in (2, 1, 3):
            a_copy(w, s).start()

        @pl.when(r == owner)
        def _():
            pltpu.make_async_copy(source[w], whole(w, r, j0), send_l.at[w]).start()

        @pl.when(r != owner)
        def _():
            mate_part(w).start()

    def token_copy(which, k, h, wait):
        src, dst = ((tok, xf), (og, ogh))[which]
        ssem = (send_t, send_g)[which].at[k * 2 + h]
        rsem = (recv_t, recv_g)[which].at[c]
        sref = src.at[pl.ds(k * 2 * half + h * half, half)]
        dref = dst.at[pl.ds(0, half), ds(c * 256, 256)]
        z = 2 * r + k
        me = jnp.logical_and(z == c, r == h)
        remote = pltpu.make_async_remote_copy(
            sref, dref, ssem, rsem, device_id={"core": h, "col": z}, device_id_type=MESH)
        if not wait:
            @pl.when(me)
            def _():
                pltpu.make_async_copy(sref, dref, rsem).start()

        @pl.when(jnp.logical_not(me))
        def _():
            remote.wait_send() if wait else remote.start()

    def mate_copy(q):
        src = xf.at[pl.ds(0, half), pl.ds(q * 256, 256)]
        dst = xf.at[pl.ds(half, half), pl.ds(q * 256, 256)]
        return pltpu.make_async_remote_copy(
            src, dst, send_m.at[q], recv_m.at[q], device_id={"core": 1 - r}, device_id_type=MESH)

    def par_copy(s):
        return pltpu.make_async_remote_copy(
            par, parf.at[:, ds(c * 256, 256)], send_p.at[s], recv_p.at[c],
            device_id={"col": lax.rem(c + s, 4)}, device_id_type=MESH)

    def b_copy(w, j, rr, p):
        ref = piece(w, rr, d, j)
        return pltpu.make_async_remote_copy(
            ref, ref, send_b.at[w, j * 2 + rr, p], recv_b.at[w, j * 2 + rr, p],
            device_id={"dp": peers[p]}, device_id_type=MESH)

    def b_step(w, j, rr):
        @pl.when(2 * r + j != c)
        def _():
            wait_for(piece(w, rr, d, j), recv_a.at[w, j * 2 + rr])
            for p in (2, 0, 1):
                b_copy(w, j, rr, p).start()

    start_a(0)
    for s in range(1, 4):
        par_copy(s).start()
    pltpu.make_async_copy(par, parf.at[:, ds(c * 256, 256)], recv_p.at[c]).start()
    for k in range(2):
        for h in range(2):
            token_copy(0, k, h, False)
    for j in range(2):
        for rr in range(2):
            b_step(0, j, rr)
    start_a(1)
    start_a(2)
    for q in range(4):
        wait_for(xf.at[pl.ds(0, half), pl.ds(q * 256, 256)], recv_t.at[q])
        mate_copy(q).start()
    start_a(3)
    for k in range(2):
        for h in range(2):
            token_copy(1, k, h, False)
    for w in (1, 2, 3):
        for j in range(2):
            for rr in range(2):
                b_step(w, j, rr)
    for s in range(1, 4):
        par_copy(s).wait_send()
    for q in range(4):
        wait_for(parf.at[:, pl.ds(q * 256, 256)], recv_p.at[q])
        mate_copy(q).wait_send()
        wait_for(xf.at[pl.ds(half, half), pl.ds(q * 256, 256)], recv_m.at[q])
        wait_for(ogh.at[:, pl.ds(q * 256, 256)], recv_g.at[q])
    for which in range(2):
        for k in range(2):
            for h in range(2):
                token_copy(which, k, h, True)
    for w in range(4):
        for s in (1, 2, 3):
            a_copy(w, s).wait_send()

        @pl.when(r == owner)
        def _():
            pltpu.make_async_copy(source[w], whole(w, r, j0), send_l.at[w]).wait()
            wait_for(whole(w, 1 - r, j0), recv_l.at[w])

        @pl.when(r != owner)
        def _():
            mate_part(w).wait_send()

        for j in range(2):
            @pl.when(2 * r + j != c)
            def _():
                for rr in range(2):
                    for p in range(3):
                        b_copy(w, j, rr, p).wait_send()
                        wait_for(piece(w, rr, peers[p], j), recv_b.at[w, j * 2 + rr, p])


def gather(tok, og, par, weights):
    dma = pltpu.SemaphoreType.DMA
    vmem, anywhere = pl.BlockSpec(memory_space=pltpu.VMEM), pl.BlockSpec(memory_space=pl.ANY)
    half, width = tok.shape[0] // 4, tok.shape[1] * 4
    out = [(2 * half, width), (half, width), (par.shape[0], width)]
    for w, weight in enumerate(weights):
        out.append((weight.shape[0] * 2, weight.shape[1] * 2))
    return pl.pallas_call(
        gather_kernel,
        out_shape=[jax.ShapeDtypeStruct(s, BF) for s in out],
        in_specs=[vmem] * 7,
        out_specs=[anywhere] * 7,
        scratch_shapes=[
            dma((4, 3)), dma((4, 4)), dma((4, 4, 3)), dma((4, 4, 3)), dma((4,)), dma((4,)), dma((4,)), dma((4,)),
            dma((4,)), dma((4,)), dma((4,)), dma((4,)), dma((4,)), dma((4,)),
        ],
        compiler_params=pltpu.CompilerParams(collective_id=0, has_side_effects=True, vmem_limit_bytes=VMEM_LIMIT),
        name="gather",
    )(tok, og, par, *weights)


def attend_kernel(q_ref, k_ref, v_ref, segq_ref, segk_ref, ctx_ref, lse_ref, *, scale):
    rows = 256
    length = q_ref.shape[0]
    seg_k = segk_ref[0:1, :]
    for h in range(2):
        lanes = slice(h * HEAD_DIM, (h + 1) * HEAD_DIM)
        k, v = k_ref[:, lanes], v_ref[:, lanes]
        for start in range(0, length, rows):
            q = q_ref[start : start + rows, lanes]
            s = lax.dot_general(q, k, CONTRACT_LAST, preferred_element_type=F32) * (scale * LOG2E)
            s = jnp.where(segq_ref[start : start + rows, 0:1] == seg_k, s, -1e9 * LOG2E)
            top = jnp.max(s, axis=1, keepdims=True)
            e = jnp.exp2(s - top)
            total = jnp.sum(e, axis=1, keepdims=True)
            ctx = jnp.dot(e.astype(BF), v, preferred_element_type=F32) / total
            ctx_ref[start : start + rows, lanes] = ctx.astype(BF)
            lse = top + jnp.log2(total)
            lse_ref[0, h : h + 1, start : start + rows] = jnp.transpose(jnp.broadcast_to(lse, (rows, 128)))[0:1, :]


def attend(qkv, seg_col, seg_row, scale):
    length = qkv.shape[0]
    pairs = qkv.shape[1] // 3 // 128
    per = pairs // 2

    def block(kind):
        return pl.BlockSpec((length, 128), lambda i: (0, (i // per) * 3 * per + kind * per + i % per))

    return pl.pallas_call(
        partial(attend_kernel, scale=scale),
        grid=(pairs,),
        out_shape=[jax.ShapeDtypeStruct((length, pairs * 128), BF), jax.ShapeDtypeStruct((pairs, 2, length), F32)],
        in_specs=[block(0), block(1), block(2), pl.BlockSpec((length, 128), lambda i: (0, 0)), pl.BlockSpec((8, length), lambda i: (0, 0))],
        out_specs=[pl.BlockSpec((length, 128), lambda i: (0, i)), pl.BlockSpec((1, 2, length), lambda i: (i, 0, 0))],
        compiler_params=pltpu.CompilerParams(vmem_limit_bytes=VMEM_LIMIT),
        name="attend",
    )(qkv, qkv, qkv, seg_col, seg_row)


def attend_back_kernel(q_ref, k_ref, v_ref, do_ref, ctx_ref, lse_ref, segk_ref, segq_ref, dq_ref, dk_ref, dv_ref, bq_ref, bv_ref, *, scale):
    rows = 256
    length = q_ref.shape[0]
    seg_q = segq_ref[0:1, :]
    prod = jnp.transpose(do_ref[...].astype(F32) * ctx_ref[...].astype(F32))
    for h in range(2):
        lanes = slice(h * HEAD_DIM, (h + 1) * HEAD_DIM)
        q, do = q_ref[:, lanes], do_ref[:, lanes]
        delta = jnp.sum(prod[h * HEAD_DIM : (h + 1) * HEAD_DIM], axis=0, keepdims=True)
        lse = lse_ref[0, h : h + 1, :]
        dqt = jnp.zeros((HEAD_DIM, length), F32)
        vsum = jnp.zeros((1, HEAD_DIM), F32)
        for start in range(0, length, rows):
            k = k_ref[start : start + rows, lanes]
            v = v_ref[start : start + rows, lanes]
            s = lax.dot_general(k, q, CONTRACT_LAST, preferred_element_type=F32) * (scale * LOG2E)
            s = jnp.where(segk_ref[start : start + rows, 0:1] == seg_q, s, -1e9 * LOG2E)
            p = jnp.exp2(s - lse)
            dp = lax.dot_general(v, do, CONTRACT_LAST, preferred_element_type=F32)
            g = (p * (dp - delta)).astype(BF)
            dk = jnp.dot(g, q, preferred_element_type=F32) * scale
            dk_ref[start : start + rows, lanes] = dk.astype(BF)
            dv = jnp.dot(p.astype(BF), do, preferred_element_type=F32)
            dv_ref[start : start + rows, lanes] = dv.astype(BF)
            vsum += jnp.sum(dv, axis=0, keepdims=True)
            dqt += jnp.dot(jnp.transpose(k), g, preferred_element_type=F32)
        dq = jnp.transpose(dqt) * scale
        dq_ref[:, lanes] = dq.astype(BF)
        bq_ref[0, :, lanes] = jnp.broadcast_to(jnp.sum(dq, axis=0, keepdims=True), (8, HEAD_DIM))
        bv_ref[0, :, lanes] = jnp.broadcast_to(vsum, (8, HEAD_DIM))


def attend_back(qkv, do, ctx, lse, seg_col, seg_row, scale):
    length = qkv.shape[0]
    pairs = qkv.shape[1] // 3 // 128
    per = pairs // 2

    def block(kind):
        return pl.BlockSpec((length, 128), lambda i: (0, (i // per) * 3 * per + kind * per + i % per))

    one = pl.BlockSpec((length, 128), lambda i: (0, i))
    small = pl.BlockSpec((1, 8, 128), lambda i: (i, 0, 0))
    return pl.pallas_call(
        partial(attend_back_kernel, scale=scale),
        grid=(pairs,),
        out_shape=[jax.ShapeDtypeStruct((length, pairs * 128), BF)] * 3 + [jax.ShapeDtypeStruct((pairs, 8, 128), F32)] * 2,
        in_specs=[
            block(0), block(1), block(2), one, one, pl.BlockSpec((1, 2, length), lambda i: (i, 0, 0)),
            pl.BlockSpec((length, 128), lambda i: (0, 0)), pl.BlockSpec((8, length), lambda i: (0, 0)),
        ],
        out_specs=[one, one, one, small, small],
        compiler_params=pltpu.CompilerParams(vmem_limit_bytes=VMEM_LIMIT),
        name="attend_back",
    )(qkv, qkv, qkv, do, ctx, lse, seg_col, seg_row)


def scatter_kernel(
    out_half, in_half, gq, go, gu, gd,
    outp, inp, rq, ro, ru, rd,
    r1q, r1o, r1u, r1d, s2q, s2o, s2u, s2d, r2q, r2o, r2u, r2d, s3q, s3o, s3u, s3d, r3q, r3o, r3u, r3d,
    send1, recv1, send2, recv2, send3, recv3, send_y, recv_y, send_i, recv_i,
):
    d, r, c = lax.axis_index("dp"), lax.axis_index("core"), lax.axis_index("col")
    a, b = d // 2, lax.rem(d, 2)
    barrier = pltpu.get_barrier_semaphore()
    for s in range(4):
        for o in range(2):
            if s or o:
                target = {"core": lax.rem(r + o, 2), "col": lax.rem(c + s, 4)}
                pl.semaphore_signal(barrier, inc=1, device_id=target, device_id_type=MESH)
    x_peer, y_peer = lax.bitwise_xor(d, 1), lax.bitwise_xor(d, 2)
    for p in (x_peer, y_peer):
        pl.semaphore_signal(barrier, inc=1, device_id={"dp": p}, device_id_type=MESH)
    pl.semaphore_wait(barrier, 9)

    grads = (gq, go, gu, gd)
    first, second = (r1q, r1o, r1u, r1d), (r2q, r2o, r2u, r2d)
    out2, out3 = (s2q, s2o, s2u, s2d), (s3q, s3o, s3u, s3d)
    third, result = (r3q, r3o, r3u, r3d), (rq, ro, ru, rd)
    by_rows = (True, False, True, False)

    def local(w, j, slab):
        rows, cols = grads[w].shape
        if by_rows[w]:
            return grads[w].at[ds(slab * (rows // 4), rows // 4), pl.ds(j * (cols // 2), cols // 2)]
        return grads[w].at[pl.ds(j * (rows // 2), rows // 2), ds(slab * (cols // 4), cols // 4)]

    def slab_of(j, i, mine):
        if j == 0:
            return i * 2 + (b if mine else 1 - b)
        return (a if mine else 1 - a) * 2 + i

    def copy1(w, j, i):
        return pltpu.make_async_remote_copy(
            local(w, j, slab_of(j, i, False)), first[w].at[j, i], send1.at[w, j, i], recv1.at[w, j, i],
            device_id={"dp": x_peer if j == 0 else y_peer}, device_id_type=MESH)

    def copy2(w, j):
        return pltpu.make_async_remote_copy(
            out2[w].at[j], second[w].at[j], send2.at[w, j], recv2.at[w, j],
            device_id={"dp": y_peer if j == 0 else x_peer}, device_id_type=MESH)

    def part3(w, j, rr):
        if by_rows[w]:
            return out3[w].at[j, pl.ds(rr * 128, 128), :]
        return out3[w].at[j, :, pl.ds(rr * 128, 128)]

    def copy3(w, j, rr, wait):
        dst = third[w].at[c]
        z = 2 * r + j
        me = jnp.logical_and(z == c, r == rr)
        remote = pltpu.make_async_remote_copy(
            part3(w, j, rr), dst, send3.at[w, j, rr], recv3.at[w, c],
            device_id={"core": rr, "col": z}, device_id_type=MESH)
        if not wait:
            @pl.when(me)
            def _():
                pltpu.make_async_copy(part3(w, j, rr), dst, recv3.at[w, c]).start()

        @pl.when(jnp.logical_not(me))
        def _():
            remote.wait_send() if wait else remote.start()

    def keep(j):
        return a if j == 0 else b

    def step2(w, j):
        give = 1 - keep(j)
        for i in range(2):
            wait_for(first[w].at[j, i], recv1.at[w, j, i])
        n = first[w].shape[2]
        src = local(w, j, slab_of(j, give, True))

        def body(t, carry):
            rows = ds(t * 64, 64, 64)
            out2[w][j, rows, :] = (src[rows, :].astype(F32) + first[w][j, give, rows, :].astype(F32)).astype(BF)
            return carry
        lax.fori_loop(0, n // 64, body, 0)
        copy2(w, j).start()

    def step3(w, j):
        wait_for(second[w].at[j], recv2.at[w, j])
        n = first[w].shape[2]
        src = local(w, j, slab_of(j, keep(j), True))

        def body(t, carry):
            rows = ds(t * 64, 64, 64)
            value = src[rows, :].astype(F32) + first[w][j, keep(j), rows, :].astype(F32) + second[w][j, rows, :].astype(F32)
            out3[w][j, rows, :] = value.astype(BF)
            return carry
        lax.fori_loop(0, n // 64, body, 0)
        for rr in range(2):
            copy3(w, j, rr, False)

    def finish(w):
        for z in range(4):
            wait_for(third[w].at[z], recv3.at[w, z])
        n = third[w].shape[1]

        def body(t, carry):
            rows = ds(t * 64, 64, 64)
            value = (third[w][0, rows, :].astype(F32) + third[w][1, rows, :].astype(F32)) + (
                third[w][2, rows, :].astype(F32) + third[w][3, rows, :].astype(F32))
            result[w][rows, :] = value
            return carry
        lax.fori_loop(0, n // 64, body, 0)

    half = out_half.shape[0]

    def token_copy(which, q, wait):
        src, dst = ((out_half, outp), (in_half, inp))[which]
        ssem, rsem = ((send_y, recv_y), (send_i, recv_i))[which]
        rr, k = c // 2, lax.rem(c, 2)
        sref = src.at[:, pl.ds(q * 256, 256)]
        dref = dst.at[ds(k * 2 * half + r * half, half)]
        sem = rsem.at[k * 2 + r]
        me = jnp.logical_and(rr == r, q == c)
        remote = pltpu.make_async_remote_copy(
            sref, dref, ssem.at[q], sem, device_id={"core": rr, "col": q}, device_id_type=MESH)
        if not wait:
            @pl.when(me)
            def _():
                pltpu.make_async_copy(sref, dref, sem).start()

        @pl.when(jnp.logical_not(me))
        def _():
            remote.wait_send() if wait else remote.start()

    order = (3, 2, 1, 0)
    for w in order:
        for i in range(2):
            for j in range(2):
                copy1(w, j, i).start()
    for q in range(4):
        token_copy(0, q, False)
        token_copy(1, q, False)
    for w in order:
        for j in range(2):
            step2(w, j)
        if w < 3:
            for j in range(2):
                step3(w + 1, j)
    for j in range(2):
        step3(0, j)
    for w in order:
        finish(w)
    for w in order:
        for j in range(2):
            for i in range(2):
                copy1(w, j, i).wait_send()
                copy3(w, j, i, True)
            copy2(w, j).wait_send()
    for which in range(2):
        for q in range(4):
            token_copy(which, q, True)
            dst, rsem = ((outp, recv_y), (inp, recv_i))[which]
            wait_for(dst.at[pl.ds(q * half, half)], rsem.at[q])


def scatter(out_half, in_half, grads):
    dma = pltpu.SemaphoreType.DMA
    vmem = pl.BlockSpec(memory_space=pltpu.VMEM)
    half, width = out_half.shape
    out, r1, r2, r3 = [((4 * half, width // 4), BF)] * 2, [], [], []
    for w, g in enumerate(grads):
        rows, cols = g.shape
        if w in (0, 2):
            out.append(((rows // 8, cols // 2), F32))
            r1.append((2, 2, rows // 4, cols // 2))
            r2.append((2, rows // 4, cols // 2))
            r3.append((4, rows // 8, cols // 2))
        else:
            out.append(((rows // 2, cols // 8), F32))
            r1.append((2, 2, rows // 2, cols // 4))
            r2.append((2, rows // 2, cols // 4))
            r3.append((4, rows // 2, cols // 8))
    return pl.pallas_call(
        scatter_kernel,
        out_shape=[jax.ShapeDtypeStruct(s, t) for s, t in out],
        in_specs=[vmem] * 6,
        out_specs=[vmem] * 6,
        scratch_shapes=[pltpu.VMEM(s, BF) for s in r1 + r2 + r2 + r2 + r3]
        + [dma((4, 2, 2)), dma((4, 2, 2)), dma((4, 2)), dma((4, 2)), dma((4, 2, 2)), dma((4, 4)), dma((4,)), dma((4,)), dma((4,)), dma((4,))],
        compiler_params=pltpu.CompilerParams(collective_id=1, has_side_effects=True, vmem_limit_bytes=VMEM_LIMIT),
        name="scatter",
    )(out_half, in_half, *grads)


def swap(values):
    return lax.ppermute(values, "core", [(0, 1), (1, 0)])


def both(own):
    return jnp.concatenate([own, swap(own)], axis=0)


def normalize(residual, gain, shift):
    mean = jnp.mean(residual, axis=1, keepdims=True)
    centered = residual - mean
    inverse = lax.rsqrt(jnp.mean(centered * centered, axis=1, keepdims=True) + NORM_EPSILON)
    normed = centered * inverse
    return normed * gain + shift, normed, inverse


def normalize_back(incoming, normed, inverse, gain):
    scaled = incoming * gain
    first = jnp.mean(scaled, axis=1, keepdims=True)
    second = jnp.mean(scaled * normed, axis=1, keepdims=True)
    grad = inverse * (scaled - first - normed * second)
    return grad, jnp.sum(incoming * normed, axis=0), jnp.sum(incoming, axis=0)


def mm(left, right, dims=(((1,), (0,)), ((), ()))):
    return lax.dot_general(left, right, dims, preferred_element_type=F32)


def join_rows(values, groups):
    if groups == 1:
        return values
    rows, cols = values.shape
    return values.reshape(2, groups, rows // (2 * groups), cols).transpose(1, 0, 2, 3).reshape(rows, cols)


def part_rows(values, groups):
    if groups == 1:
        return values
    rows, cols = values.shape
    return values.reshape(4, groups, 2, rows // (8 * groups), cols).transpose(0, 2, 1, 3, 4).reshape(rows, cols)


def on_device(
    tokens, segment_ids, w_qkv, b_qv, w_out, b_out, norm1_gain, norm1_shift,
    w_up, b_up, w_down, b_down, norm2_gain, norm2_shift, out_grad,
):
    groups = lax.axis_size("rh")
    core, col = lax.axis_index("core"), lax.axis_index("col")
    part = tokens.shape[1]
    length = segment_ids.shape[1]
    half = length // 2
    scale = 1.0 / math.sqrt(HEAD_DIM)
    wq, wo, wu, wd = w_qkv.reshape(w_qkv.shape[0], 3 * part), w_out, w_up, w_down
    if groups > 1:
        wq, wu = (lax.all_gather(w, "rh", axis=0, tiled=True) for w in (wq, wu))
        wo, wd = (lax.all_gather(w, "rh", axis=1, tiled=True) for w in (wo, wd))
    par = jnp.concatenate(
        [b_qv, b_out[None], norm1_gain[None], norm1_shift[None], b_down[None], norm2_gain[None], norm2_shift[None],
         b_up.reshape(4, part), jnp.zeros((4, part), BF)], axis=0)
    x, og, params, wq, wo, wu, wd = gather(tokens, out_grad, par, (wq, wo, wu, wd))
    wq, wu = join_rows(wq, groups), join_rows(wu, groups)
    wo, wd = join_rows(wo.T, groups).T if groups > 1 else wo, join_rows(wd.T, groups).T if groups > 1 else wd
    wo_mate = swap(wo)
    params = params.astype(F32)
    mine = lax.dynamic_slice_in_dim(params, core * 2 * part, 2 * part, 1)
    zeros = jnp.zeros((part,), F32)
    bias_qkv = jnp.concatenate([mine[0, :part], zeros, mine[1, :part], mine[0, part:], zeros, mine[1, part:]])
    bias_up = mine[8:12].reshape(4, 2, part).transpose(1, 0, 2).reshape(-1)
    bias_out, gain1, shift1, bias_down, gain2, shift2 = (params[i] for i in range(2, 8))

    seqs = lax.all_gather(segment_ids, "core", axis=0, tiled=True)
    seg = lax.dynamic_index_in_dim(seqs, col, 0, False)
    seg = jnp.concatenate([lax.dynamic_slice_in_dim(seg, core * half, half), lax.dynamic_slice_in_dim(seg, (1 - core) * half, half)])
    seg_col = jnp.broadcast_to(seg[:, None], (length, 128))
    seg_row = jnp.broadcast_to(seg[None], (8, length))

    qkv = (mm(x, wq) + bias_qkv).astype(BF)
    ctx, lse = attend(qkv, seg_col, seg_row, scale)
    ctx_mate = swap(ctx[half:])
    residual_one = x[:half].astype(F32) + (mm(ctx[:half], wo) + mm(ctx_mate, wo_mate)) + bias_out
    hidden_one, normed_one, inverse_one = normalize(residual_one, gain1, shift1)
    hidden = both(hidden_one.astype(BF))
    up_proj = mm(hidden, wu) + bias_up
    gate = 0.5 * (1.0 + lax.erf(up_proj * math.sqrt(0.5)))
    activated = (up_proj * gate).astype(BF)
    down = mm(activated, wd)
    residual_two = hidden_one + (down[:half] + swap(down[half:])) + bias_down
    output, normed_two, inverse_two = normalize(residual_two, gain2, shift2)
    two_grad, gain2_grad, shift2_grad = normalize_back(og.astype(F32), normed_two, inverse_two, gain2)
    mix = both(two_grad.astype(BF))
    down_wgrad = mm(activated, mix, CONTRACT_FIRST).astype(BF)
    slope = gate + up_proj * (math.sqrt(0.5 / math.pi) * jnp.exp(-0.5 * up_proj * up_proj))
    up_grad = mm(mix, wd, CONTRACT_LAST) * slope
    up_low = up_grad.astype(BF)
    up_bias_grad = jnp.sum(up_grad, axis=0)
    up_wgrad = mm(hidden, up_low, CONTRACT_FIRST).astype(BF)
    hidden_grad = mm(up_low, wu, CONTRACT_LAST)
    hidden_grad = hidden_grad[:half] + swap(hidden_grad[half:]) + two_grad
    one_grad, gain1_grad, shift1_grad = normalize_back(hidden_grad, normed_one, inverse_one, gain1)
    attn = both(one_grad.astype(BF))
    out_wgrad = mm(ctx, attn, CONTRACT_FIRST).astype(BF)
    ctx_grad = mm(attn, wo, CONTRACT_LAST).astype(BF)
    dq, dk, dv, bq, bv = attend_back(qkv, ctx_grad, ctx, lse, seg_col, seg_row, scale)
    low = jnp.concatenate([dq[:, :part], dk[:, :part], dv[:, :part], dq[:, part:], dk[:, part:], dv[:, part:]], axis=1)
    qkv_wgrad = mm(x, low, CONTRACT_FIRST).astype(BF)
    in_part = mm(low, wq, CONTRACT_LAST)
    in_half = (in_part[:half] + swap(in_part[half:]) + one_grad).astype(BF)

    qkv_wgrad, up_wgrad = part_rows(qkv_wgrad, groups), part_rows(up_wgrad, groups)
    if groups > 1:
        out_wgrad, down_wgrad = part_rows(out_wgrad.T, groups).T, part_rows(down_wgrad.T, groups).T
    output, in_grad, qkv_share, out_share, up_share, down_share = scatter(
        output.astype(BF), in_half, (qkv_wgrad, out_wgrad, up_wgrad, down_wgrad))
    if groups > 1:
        qkv_share, up_share = (lax.psum_scatter(g, "rh", scatter_dimension=0, tiled=True) for g in (qkv_share, up_share))
        out_share, down_share = (lax.psum_scatter(g, "rh", scatter_dimension=1, tiled=True) for g in (out_share, down_share))

    full = jnp.stack([jnp.sum(one_grad, axis=0), gain1_grad, shift1_grad, jnp.sum(two_grad, axis=0), gain2_grad, shift2_grad])
    owned = jnp.concatenate([bq[:, 0].reshape(1, -1), bv[:, 0].reshape(1, -1), up_bias_grad.reshape(2, 4, part).transpose(1, 0, 2).reshape(4, -1)], axis=0)
    owned = lax.dynamic_update_slice_in_dim(jnp.zeros((6, 4 * part), F32), owned, core * 2 * part, 1)
    sums = lax.psum(jnp.concatenate([full, owned], axis=0), ("dp", "rh", "core", "col"))
    sums = lax.dynamic_slice_in_dim(sums, col * part, part, 1)
    return (
        output,
        in_grad.astype(F32),
        qkv_share.reshape(qkv_share.shape[0], 3, part),
        sums[6:8],
        out_share,
        sums[0],
        sums[1],
        sums[2],
        up_share,
        sums[8:12].reshape(-1),
        down_share,
        sums[3],
        sums[4],
        sums[5],
    )


def solution(mesh):
    dp, row, col = (mesh.shape[name] for name in ("dp", "row", "col"))
    fine = Mesh(mesh.devices.reshape(dp, row // 2, 2, col), ("dp", "rh", "core", "col"))
    row, every = ("rh", "core"), ("dp", "rh", "core")
    return jax.shard_map(
        on_device,
        mesh=fine,
        in_specs=(
            P(every, "col"), P(every, None), P(row, None, "col"), P(None, "col"), P("col", row), P("col"), P("col"), P("col"),
            P(row, "col"), P("col"), P("col", row), P("col"), P("col"), P("col"), P(every, "col"),
        ),
        out_specs=(
            P(every, "col"), P(every, "col"), P(every, None, "col"), P(None, "col"), P("col", every), P("col"), P("col"),
            P("col"), P(every, "col"), P("col"), P("col", every), P("col"), P("col"), P("col"),
        ),
        check_vma=False,
    )
```

time: 1460 us -> 559 us (0.38)
  waiting for transfers between devices: 1060 us -> 13.5 us
  Pallas kernels: 0 us -> 360 us
  matrix products: 176 us -> 72.9 us
  other arithmetic: 71.2 us -> 13.3 us
  local copies, waits for them, and re-layouts: 54.2 us -> 30.6 us
  blocking collectives: 82.4 us -> 62.7 us
    reduce_scatter x8 -> x0, waiting for transfers between devices: 717 us -> none  [the longest x4 570 us: sum_width(): lax.psum_scatter(partial_terms, 'col', scatter_dimension=1, tiled=True)]
    pallas_call x0 -> x4, Pallas kernels: none -> 360 us  [the longest x1 164 us: scatter(): pl.pallas_call(scatter_kernel, out_shape=[jax.ShapeDtypeStruct(s, t) for...]
    all_gather x7 -> x0, waiting for transfers between devices: 337 us -> none  [the longest x4 330 us: gather_width(): return lax.all_gather(values, 'col', axis=1, tiled=True)]
    dot_general x40 -> x13, matrix products: 176 us -> 72.9 us  [mm(): return lax.dot_general(left, right, dims, preferred_element_type=F32)]
    reduce_sum x11 -> x7, other arithmetic: 41.9 us -> 6.45 us  [the longest x2 2.43 us: normalize_back(): return (grad, jnp.sum(incoming * normed, axis=0), jnp.sum(incoming, axis=0))]
    while x33 -> x0, local copies, waits for them, and re-layouts: 22 us -> none  [the longest x4 9.46 us: on_device(): lax.map(lambda packed: attend(packed[0], packed[1], packed[2], packed[3],...]
    psum x7 -> x1, blocking collectives: 78 us -> 60.5 us  [on_device(): lax.psum(jnp.concatenate([full, owned], axis=0), ('dp', 'rh', 'core', 'co...]
    convert_element_type x13 -> x6, other arithmetic: 22.9 us -> 6.81 us  [the longest x1 2.81 us: on_device(): in_grad.astype(F32)]
  transfers between devices with their start and end apart: 15 -> 8, of which waited for: 12 -> 4; matrix products, arithmetic and copies ran while one was open for 5% -> 8% of each run, Pallas kernels for 0% -> 4%
where the time goes in v1:
time: 559 us; the launch traced here: 556 us
  Pallas kernels  360 us (64%)
  matrix products  72.9 us (13%)
  blocking collectives  62.7 us (11%)
  local copies, waits for them, and re-layouts  30.6 us (5%)
  waiting for transfers between devices  13.5 us (2%)
  other arithmetic  13.3 us (2%)
    pallas_call x1, Pallas kernels, scatter(): pl.pallas_call(scatter_kernel, out_shape=[jax.ShapeDtypeStruct(s, t) for...  164 us
    pallas_call x1, Pallas kernels, gather(): pl.pallas_call(gather_kernel, out_shape=[jax.ShapeDtypeStruct(s, BF) for...  146 us
    dot_general x13, matrix products, mm(): return lax.dot_general(left, right, dims, preferred_element_type=F32)  72.9 us
    psum x1, blocking collectives, on_device(): lax.psum(jnp.concatenate([full, owned], axis=0), ('dp', 'rh', 'core', 'co...  60.5 us
    pallas_call x1, Pallas kernels, attend_back(): pl.pallas_call(partial(attend_back_kernel, scale=scale), grid=(pairs,), o...  27.7 us
    pallas_call x1, Pallas kernels, attend(): pl.pallas_call(partial(attend_kernel, scale=scale), grid=(pairs,), out_sh...  21.8 us
    unnamed x88, local copies, waits for them, and re-layouts  15 us
    ppermute x8, waiting for transfers between devices, swap(): return lax.ppermute(values, 'core', [(0, 1), (1, 0)])  13.5 us
  transfers between devices with their start and end apart: 8, of which 4 were waited for; matrix products, arithmetic and copies ran while one was open for 8% of the time, Pallas kernels for 4%

profile of v1, /device:TPU:9, one launch (start us, length us, event | category | flops | bytes accessed | tf_op | source)
XLA Modules:
  0.0 556.2 jit_solution(6731339839327726955)
XLA Ops:
  5.3 1.4 copy.36
  9.1 146.2 %gather.1 = (bf16[1024,1024]{1,0:T(8,128)(2,1)}, bf16[512,1024]{1,0:T(8,128)(2,1)}, bf16[16,1024]{1,0:T(8,128)(2,1)}, bf16[1024,1536]{1,0:T(8,128)(2,1)}, bf16[5...) custom-call(bf16[2048,256]{1,0:T(8,128)(2,1)} %tok.1, bf16[2048,256]{1,0:T(8,128)(2,1)} %og.1, ...), custom_call_target="tpu_custom_call" | custom-call | tf_op jit(solution)/shard_map/gather/pallas_call | solution.py:192
  157.0 2.2 all-gather
  159.4 7.6 %add_convert_fusion.q_ref.k_ref.v_ref = bf16[1024,1536]{1,0:T(8,128)(2,1)} fusion(bf16[1024,1024]{1,0:T(8,128)(2,1)} %get-tuple-element.34, bf16[1024,1536]{1,0:T(8,128)(2,1)} %get-tuple-element.35, f32[1536]{0:T(1024)S(1)} %constant_dynamic-update-slice_fusion.1), kind=kOutput, calls=%fused_computation.8 | convolution fusion | flops 3224371200 | bytes 8394752 | tf_op jit(solution)/shard_map/dot_general | solution.py:518
  168.6 21.8 %attend.1 = (bf16[1024,512]{1,0:T(8,128)(2,1)}, f32[4,2,1024]{2,1,0:T(2,128)}) custom-call(bf16[1024,1536]{1,0:T(8,128)(2,1)} %add_convert_fusion.q_ref.k_ref.v_ref, bf16[1024,1536]{1,0:T(8,128)(2,1)} %add_convert_fusion.q_ref.k_ref.v_ref, bf16[1024,1536]{1,0:T(8,128)(2,1)} %add_convert_fusion.q_ref.k_ref.v_ref, ...), custom_call_target="tpu_custom_call" | custom-call | tf_op jit(solution)/shard_map/attend/pallas_call | solution.py:234
  192.0 1.9 fusion.22
  193.9 2.1 fusion.40
  196.4 1.4 fusion.20
  198.0 2.9 collective-permute-done.2
  200.8 10.6 %multiply_convert_fusion = (bf16[1024,2048]{1,0:T(8,128)(2,1)S(1)}, f32[1024,2048]{1,0:T(8,128)}) fusion(f32[2048]{0:T(1024)S(1)} %bitcast.83, bf16[1024,2048]{1,0:T(8,128)(2,1)} %get-tuple-element.39, bf16[512,1024]{1,0:T(8,128)(2,1)} %collective-permute-done.2, bf16[512,1024]{1,0:T(8,128)(2,1)} %fusion.20), kind=kOutput, calls=%fused_computation.6 | convolution fusion | flops 4311744512 | bytes 18882560 | tf_op jit(solution)/shard_map/dot_general | solution.py:518
  211.5 4.5 fusion.42
  216.4 4.0 collective-permute-done.3
  223.4 1.8 fusion.30
  225.6 2.5 collective-permute-done.4
  228.1 11.1 %fusion.41 = (f32[2048]{0:T(1024)S(1)}, bf16[1024,2048]{1,0:T(8,128)(2,1)S(1)}) fusion(f32[1024,2048]{1,0:T(8,128)} %get-tuple-element.133, f32[2048]{0:T(1024)S(1)} %bitcast.84, bf16[2048,1024]{1,0:T(8,128)(2,1)S(1)} %copy-done.26, bf16[512,1024]{1,0:T(8,128)(2,1)S(1)} %collective-permute-done.4, bf16[512,1024]{1,0:T(8,128)(2,1)S(1)} %convert_element_type.58), kind=kOutput, calls=%fused_computation.95 | convolution fusion | flops 4324325376 | bytes 18890752 | tf_op jit(solution)/shard_map/dot_general | solution.py:518
  239.3 4.5 fusion.18
  244.3 4.0 collective-permute-done.5
  248.4 1.5 multiply_reduce_fusion
  250.5 1.3 copy-done
  252.2 9.6 %convolution_convert_fusion.2.gu = bf16[1024,2048]{1,0:T(8,128)(2,1)} fusion(bf16[1024,2048]{1,0:T(8,128)(2,1)} %copy-done.33, bf16[512,1024]{1,0:T(8,128)(2,1)} %collective-permute-done.2, bf16[512,1024]{1,0:T(8,128)(2,1)} %fusion.20), kind=kOutput, calls=%fused_computation.11 | convolution fusion | flops 4301258752 | bytes 10485760 | tf_op jit(solution)/shard_map/dot_general | solution.py:518
  261.8 2.3 convolution_convert_fusion.4.do_ref
  264.1 27.7 %attend_back.1 = (bf16[1024,512]{1,0:T(8,128)(2,1)}, bf16[1024,512]{1,0:T(8,128)(2,1)}, bf16[1024,512]{1,0:T(8,128)(2,1)}, f32[4,8,128]{2,1,0:T(8,128)}, f32[4,8,128]{2,1,0:T(8,128)}) custom-call(bf16[1024,1536]{1,0:T(8,128)(2,1)} %add_convert_fusion.q_ref.k_ref.v_ref, bf16[1024,1536]{1,0:T(8,128)(2,1)} %add_convert_fusion.q_ref.k_ref.v_ref, ...), custom_call_target="tpu_custom_call" | custom-call | tf_op jit(solution)/shard_map/attend_back/pallas_call | solution.py:287
  294.4 1.6 copy-done.21
  297.2 3.4 fusion.43
  300.6 1.6 slice.155
  303.7 6.2 %convolution_convert_fusion.1.gd = bf16[2048,1024]{1,0:T(8,128)(2,1)} fusion(bf16[1024,2048]{1,0:T(8,128)(2,1)S(1)} %copy-done.32, bf16[512,1024]{1,0:T(8,128)(2,1)S(1)} %copy-done.30, bf16[512,1024]{1,0:T(8,128)(2,1)S(1)} %copy-done.9), kind=kOutput, calls=%fused_computation.10 | convolution fusion | flops 4301258752 | bytes 10485760 | tf_op jit(solution)/shard_map/dot_general | solution.py:518
  311.5 60.5 %psum.7 = f32[12,1024]{1,0:T(8,128)S(1)} all-reduce(f32[12,1024]{1,0:T(8,128)S(1)} %concatenate.35), channel_id=1, replica_groups=mesh['dp'=4,'row'=2,'col'=4] {'dp','row','col'}, use_global_device_ids=true, to_apply=%region_15.16 | all-reduce | flops 12288 | bytes 98304 | tf_op jit(solution)/shard_map/psum | solution.py:613
  374.0 3.9 convolution_convert_fusion.3.go
  377.9 5.1 convolution_convert_fusion.gq
  383.0 1.5 fusion.13.in_half
  384.5 164.3 %scatter.1 = (bf16[2048,256]{1,0:T(8,128)(2,1)}, bf16[2048,256]{1,0:T(8,128)(2,1)}, f32[128,768]{1,0:T(8,128)}, f32[256,128]{1,0:T(8,128)}, f32[128,1024]{1,0:T(8,128)}, /*index=5*/f32[1024,128]{1,0:T(8,128)}) custom-call(bf16[512,1024]{1,0:T(8,128)(2,1)} %get-tuple-element.111.out_half, bf16[512,1024]{1,0:T(8,128)(2,1)} %fusion.13.in_half, ...), custom_call_target="tpu_custom_call" | custom-call | tf_op jit(solution)/shard_map/scatter/pallas_call | solution.py:481
  548.8 2.8 convert_element_type.67
  (145 shorter events, 30.6 us)
Async XLA Ops:
  0.6 7.2 %copy-start.24 = (bf16[2,256]{1,0:T(2,128)(2,1)S(1)}, bf16[2,256]{1,0:T(2,128)(2,1)}, u32[]{:S(2)}) copy-start(bf16[2,256]{1,0:T(2,128)(2,1)} %param.18) | copy-start | bytes 3076
  9.1 147.9 %copy-start.23 = (s32[2,1024]{1,0:T(2,128)S(1)}, s32[2,1024]{1,0:T(2,128)}, u32[]{:S(2)}) copy-start(s32[2,1024]{1,0:T(2,128)} %param.16) | copy-start | bytes 24580
  155.3 38.6 %collective-permute-start.1 = (bf16[512,1024]{1,0:T(8,128)(2,1)}, bf16[512,1024]{1,0:T(8,128)(2,1)}, u32[]{:S(2)}, u32[]{:S(2)}) collective-permute-start(bf16[512,1024]{1,0:T(8,128)(2,1)} %get-tuple-element.38), channel_id=1, source_target_pairs={{0,4},{4,0},{1,5},{5,1},{2,6},{6,2},{3,7},{7,3},{8,12},{12,8},{9,1... | collective-permute-start | bytes 3145736 | tf_op jit(solution)/shard_map/ppermute | solution.py:494
  168.6 23.3 %copy-start.19 = (bf16[16,1024]{1,0:T(8,128)(2,1)S(1)}, bf16[16,1024]{1,0:T(8,128)(2,1)}, u32[]{:S(2)}) copy-start(bf16[16,1024]{1,0:T(8,128)(2,1)} %get-tuple-element.36) | copy-start | bytes 98308
  168.6 23.3 %copy-start.6 = (bf16[512,1024]{1,0:T(8,128)(2,1)S(1)}, bf16[512,1024]{1,0:T(8,128)(2,1)}, u32[]{:S(2)}) copy-start(bf16[512,1024]{1,0:T(8,128)(2,1)} %get-tuple-element.38) | copy-start | bytes 3145732
  191.5 2.4 collective-permute-start
  197.8 3.0 collective-permute-start.2
  200.8 10.7 %copy-start.26 = (bf16[2048,1024]{1,0:T(8,128)(2,1)S(1)}, bf16[2048,1024]{1,0:T(8,128)(2,1)}, u32[]{:S(2)}) copy-start(bf16[2048,1024]{1,0:T(8,128)(2,1)} %get-tuple-element.40) | copy-start | bytes 12582916
  211.5 4.5 copy-start.31
  216.2 4.2 collective-permute-start.3
  225.4 13.9 %copy-start.8 = (bf16[512,1024]{1,0:T(8,128)(2,1)}, bf16[512,1024]{1,0:T(8,128)(2,1)S(1)}, u32[]{:S(2)}) copy-start(bf16[512,1024]{1,0:T(8,128)(2,1)S(1)} %convert_element_type.58) | copy-start | bytes 3145732
  225.4 2.7 collective-permute-start.4
  228.1 11.2 %copy-start.29 = (bf16[512,1024]{1,0:T(8,128)(2,1)}, bf16[512,1024]{1,0:T(8,128)(2,1)S(1)}, u32[]{:S(2)}) copy-start(bf16[512,1024]{1,0:T(8,128)(2,1)S(1)} %collective-permute-done.4) | copy-start | bytes 3145732
  228.1 11.2 %copy-start.25 = (bf16[1024,2048]{1,0:T(8,128)(2,1)S(1)}, bf16[1024,2048]{1,0:T(8,128)(2,1)}, u32[]{:S(2)}) copy-start(bf16[1024,2048]{1,0:T(8,128)(2,1)} %get-tuple-element.39) | copy-start | bytes 12582916
  239.3 4.6 copy-start.33
  244.1 4.2 collective-permute-start.5
  252.0 9.8 %copy-start.7 = (bf16[512,1024]{1,0:T(8,128)(2,1)}, bf16[512,1024]{1,0:T(8,128)(2,1)S(1)}, u32[]{:S(2)}) copy-start(bf16[512,1024]{1,0:T(8,128)(2,1)S(1)} %convert_element_type.60) | copy-start | bytes 3145732
  252.0 9.8 %collective-permute-start.6 = (bf16[512,1024]{1,0:T(8,128)(2,1)S(1)}, bf16[512,1024]{1,0:T(8,128)(2,1)S(1)}, u32[]{:S(2)}, u32[]{:S(2)}) collective-permute-start(bf16[512,1024]{1,0:T(8,128)(2,1)S(1)} %convert_element_type.60), channel_id=1, source_target_pairs={{0,4},{4,0},{1,5},{5,1},{2,6},{6,2},{3,7},{7,3},{8,12},{12,8},{9,1... | collective-permute-start | bytes 3145736 | tf_op jit(solution)/shard_map/ppermute | solution.py:494
  294.1 3.0 copy-start.27
  297.2 6.5 %copy-start.32 = (bf16[1024,2048]{1,0:T(8,128)(2,1)S(1)}, bf16[1024,2048]{1,0:T(8,128)(2,1)}, u32[]{:S(2)}) copy-start(bf16[1024,2048]{1,0:T(8,128)(2,1)} %copy-done.31) | copy-start | bytes 12582916
  300.6 2.8 copy-start.3
  300.6 3.0 copy-start.9
  300.6 3.0 copy-start.30
  303.4 70.6 %copy-start.2 = (bf16[1024,512]{1,0:T(8,128)(2,1)S(1)}, bf16[1024,512]{1,0:T(8,128)(2,1)}, u32[]{:S(2)}) copy-start(bf16[1024,512]{1,0:T(8,128)(2,1)} %get-tuple-element.37.ctx_ref) | copy-start | bytes 3145732
  303.4 79.6 %collective-permute-start.7 = (f32[512,1024]{1,0:T(8,128)}, f32[512,1024]{1,0:T(8,128)S(1)}, u32[]{:S(2)}, u32[]{:S(2)}) collective-permute-start(f32[512,1024]{1,0:T(8,128)} %slice.155), channel_id=1, source_target_pairs={{0,4},{4,0},{1,5},{5,1},{2,6},{6,2},{3,7},{7,3},{8,12},{12,8},{9,1... | collective-permute-start | bytes 6291464 | tf_op jit(solution)/shard_map/ppermute | solution.py:494
  374.0 4.0 copy-start.17
  374.0 4.0 copy-start.22
  377.9 5.1 copy-start.1
  377.9 5.1 copy-start.4
  548.8 2.8 copy-start.18
  548.8 3.9 copy-start.12
  551.8 3.4 copy-start.14
  (10 other events, 20.9 us)

commit v2 on v1

v2 whole, which is shorter than its diff:
```python
from functools import partial
import math

import jax
import jax.numpy as jnp
from jax import lax
from jax.experimental import pallas as pl
from jax.experimental.pallas import tpu as pltpu
from jax.sharding import Mesh, PartitionSpec as P

HEAD_DIM = 64
NORM_EPSILON = 1e-05
MESH = pl.DeviceIdType.MESH
LOG2E = math.log2(math.e)
BF = jnp.bfloat16
F32 = jnp.float32
CONTRACT_LAST = (((1,), (1,)), ((), ()))
CONTRACT_FIRST = (((0,), (0,)), ((), ()))
VMEM_LIMIT = 62 * 2**20


def wait_for(ref, sem):
    pltpu.make_async_copy(ref, ref, sem).wait()


def ds(start, size, multiple=128):
    return pl.ds(pl.multiple_of(start, multiple), size)


def normalize(residual, gain, shift):
    mean = jnp.mean(residual, axis=1, keepdims=True)
    centered = residual - mean
    inverse = lax.rsqrt(jnp.mean(centered * centered, axis=1, keepdims=True) + NORM_EPSILON)
    normed = centered * inverse
    return normed * gain + shift, normed, inverse


def gather_kernel(
    tok, og, par, seg, wq, wo, wu, wd,
    parf, lse, segc, segr, inverse, vec,
    x_out, wq_out, wo_out, wu_out, wd_out, qkv_out, ctx_out, normed_out, hidden_out, act_out, slope_out, out_half, two_out, mix_out,
    xf, wqf, wof, wuf, wdf, qkv, ctx, normed, hidden, act, slope, outh, two, mix,
    ogh, wom, ctxm, hidden_one, mate_out, mate_in, segs, tq, tk, tv, tc,
    send_a, recv_a, send_f, send_b, recv_b, send_c, recv_c, recv_l, send_l, send_t, recv_t, send_g, recv_g, send_m, recv_m, send_p, recv_p,
    send_s, recv_s, send_x, recv_x, store,
    *, scale,
):
    d, r, c = lax.axis_index("dp"), lax.axis_index("core"), lax.axis_index("col")
    owner, j0 = c // 2, lax.rem(c, 2)
    half = tok.shape[0] // 4
    barrier = pltpu.get_barrier_semaphore()
    for s in range(4):
        for o in range(2):
            if s or o:
                target = {"core": lax.rem(r + o, 2), "col": lax.rem(c + s, 4)}
                pl.semaphore_signal(barrier, inc=1, device_id=target, device_id_type=MESH)
    x_peer, y_peer, far = (lax.bitwise_xor(d, p) for p in (1, 2, 3))
    peers = (x_peer, y_peer)
    for p in peers:
        pl.semaphore_signal(barrier, inc=1, device_id={"dp": p}, device_id_type=MESH)
    pl.semaphore_wait(barrier, 9)

    source, dest = (wq, wo, wu, wd), (wqf, wof, wuf, wdf)

    def whole(w, rr, j):
        rows, cols = source[w].shape
        if w in (0, 2):
            return dest[w].at[ds(rr * rows, rows), ds(j * cols, cols)]
        return dest[w].at[ds(j * rows, rows), ds(rr * cols, cols)]

    def piece(w, rr, dd, j, part=None):
        rows, cols = source[w].shape
        size = rows // 4
        base = (rr if w in (0, 2) else j) * rows + dd * size
        if part is not None:
            size = size // 2
            base = base + part * size
        return dest[w].at[ds(base, size, 32), ds((j if w in (0, 2) else rr) * cols, cols)]

    def a_copy(w, up):
        size = source[w].shape[0] // 4
        return pltpu.make_async_remote_copy(
            source[w].at[ds(d * size, size, 64)], piece(w, r, d, j0), send_a.at[w, up], recv_a.at[w, j0 * 2 + r],
            device_id={"core": owner, "col": lax.rem(c + (1 if up else 3), 4)}, device_id_type=MESH)

    def outer(up):
        return c < 3 if up else c > 0

    def mate_part(w):
        return pltpu.make_async_remote_copy(
            source[w], whole(w, r, j0), send_l.at[w], recv_l.at[w], device_id={"core": 1 - r}, device_id_type=MESH)

    def start_a(w):
        for up in (0, 1):
            @pl.when(outer(up))
            def _():
                a_copy(w, up).start()

        @pl.when(r == owner)
        def _():
            pltpu.make_async_copy(source[w], whole(w, r, j0), send_l.at[w]).start()

        @pl.when(r != owner)
        def _():
            mate_part(w).start()

    def token_copy(which, k, h, wait):
        src, dst = ((tok, xf), (og, ogh))[which]
        ssem = (send_t, send_g)[which].at[k * 2 + h]
        rsem = (recv_t, recv_g)[which].at[c]
        sref = src.at[pl.ds(k * 2 * half + h * half, half)]
        dref = dst.at[pl.ds(0, half), ds(c * 256, 256)]
        z = 2 * r + k
        me = jnp.logical_and(z == c, r == h)
        remote = pltpu.make_async_remote_copy(
            sref, dref, ssem, rsem, device_id={"core": h, "col": z}, device_id_type=MESH)
        if not wait:
            @pl.when(me)
            def _():
                pltpu.make_async_copy(sref, dref, rsem).start()

        @pl.when(jnp.logical_not(me))
        def _():
            remote.wait_send() if wait else remote.start()

    def mate_copy(q):
        src = xf.at[pl.ds(0, half), pl.ds(q * 256, 256)]
        dst = xf.at[pl.ds(half, half), pl.ds(q * 256, 256)]
        return pltpu.make_async_remote_copy(
            src, dst, send_m.at[q], recv_m.at[q], device_id={"core": 1 - r}, device_id_type=MESH)

    def par_copy(s):
        return pltpu.make_async_remote_copy(
            par, parf.at[:, ds(c * 256, 256)], send_p.at[s], recv_p.at[c],
            device_id={"col": lax.rem(c + s, 4)}, device_id_type=MESH)

    def forward(w, j, rr, up, wait):
        origin = 2 * r + j
        ref = piece(w, rr, d, j)
        copy = pltpu.make_async_remote_copy(
            ref, ref, send_f.at[w, j * 2 + rr], recv_a.at[w, j * 2 + rr],
            device_id={"col": lax.rem(c + (1 if up else 3), 4)}, device_id_type=MESH)

        @pl.when(jnp.logical_and(origin < c if up else origin > c, outer(up)))
        def _():
            copy.wait_send() if wait else copy.start()

    def b_copy(w, j, rr, p):
        ref = piece(w, rr, d, j)
        return pltpu.make_async_remote_copy(
            ref, ref, send_b.at[w, j * 2 + rr, p], recv_b.at[w, j * 2 + rr, p],
            device_id={"dp": peers[p]}, device_id_type=MESH)

    def c_copy(w, j, rr, p):
        ref = piece(w, rr, peers[p], j, p)
        return pltpu.make_async_remote_copy(
            ref, ref, send_c.at[w, j * 2 + rr, p], recv_c.at[w, j * 2 + rr, p],
            device_id={"dp": peers[1 - p]}, device_id_type=MESH)

    def b_step(w, near, rr):
        j = 1 - r if near else r

        @pl.when(2 * r + j != c)
        def _():
            wait_for(piece(w, rr, d, j), recv_a.at[w, j * 2 + rr])
            for up in (0, 1):
                forward(w, j, rr, up, False)
            for p in range(2):
                b_copy(w, j, rr, p).start()

    def c_step(w, near, rr):
        j = 1 - r if near else r

        @pl.when(2 * r + j != c)
        def _():
            for p in range(2):
                wait_for(piece(w, rr, peers[p], j), recv_b.at[w, j * 2 + rr, p])
                c_copy(w, j, rr, p).start()

    def finish_weight(w):
        @pl.when(r == owner)
        def _():
            wait_for(whole(w, r, j0), send_l.at[w])
            wait_for(whole(w, 1 - r, j0), recv_l.at[w])

        for j in range(2):
            @pl.when(2 * r + j != c)
            def _():
                for rr in range(2):
                    for p in range(2):
                        wait_for(piece(w, rr, far, j, p), recv_c.at[w, j * 2 + rr, p])

    seg_send = pltpu.make_async_remote_copy(
        seg, segs.at[r], send_s.at[0], recv_s.at[r], device_id={"core": 1 - r}, device_id_type=MESH)
    seg_own = pltpu.make_async_copy(seg, segs.at[r], recv_s.at[r])
    start_a(0)
    for s in range(1, 4):
        par_copy(s).start()
    pltpu.make_async_copy(par, parf.at[:, ds(c * 256, 256)], recv_p.at[c]).start()
    seg_send.start()
    seg_own.start()
    steps = [(w, near, rr) for w in range(4) for near in (1, 0) for rr in range(2)]
    lag = 3

    def advance(i):
        b_step(*steps[i])
        if i >= lag:
            c_step(*steps[i - lag])
        if i == 1:
            start_a(1)
        if i == 3:
            for k in range(2):
                for h in range(2):
                    token_copy(0, k, h, False)
            start_a(2)
        if i == 7:
            start_a(3)
        if i == 15:
            for k in range(2):
                for h in range(2):
                    token_copy(1, k, h, False)

    for i in range(8):
        advance(i)
    for q in range(4):
        wait_for(xf.at[pl.ds(0, half), pl.ds(q * 256, 256)], recv_t.at[q])
        mate_copy(q).start()
    for rr in range(2):
        wait_for(segs.at[rr], recv_s.at[rr])
    length, part = xf.shape[0], wqf.shape[1] // 6
    segr[:, 0:half] = jnp.broadcast_to(segs[owner, pl.ds(j0, 1), ds(r * half, half)], (8, half))
    segr[:, half:] = jnp.broadcast_to(segs[owner, pl.ds(j0, 1), ds((1 - r) * half, half)], (8, half))
    segc[...] = jnp.transpose(jnp.broadcast_to(segr[0:1, :], (128, length)))
    finish_weight(0)
    for q in range(4):
        wait_for(parf.at[:, pl.ds(q * 256, 256)], recv_p.at[q])
        wait_for(xf.at[pl.ds(half, half), pl.ds(q * 256, 256)], recv_m.at[q])

    def project(t, carry):
        place = ds(t * 256, 256)
        for j in range(2):
            lanes = slice(j * 3 * part, (j + 1) * 3 * part)
            value = jnp.dot(xf[place, :], wqf[:, lanes], preferred_element_type=F32)
            bias = parf[:, ds(r * 2 * part + j * part, part)].astype(F32)
            low = j * 3 * part
            qkv[place, low : low + part] = (value[:, :part] + bias[0:1]).astype(BF)
            qkv[place, low + part : low + 2 * part] = value[:, part : 2 * part].astype(BF)
            qkv[place, low + 2 * part : low + 3 * part] = (value[:, 2 * part :] + bias[1:2]).astype(BF)
        for k, i in ((0, 8), (2, 9)):
            @pl.when(t == k)
            def _():
                advance(i)
        return carry
    lax.fori_loop(0, length // 256, project, 0)
    pairs = (
        (xf, x_out), (wqf, wq_out), (wof, wo_out), (wuf, wu_out), (wdf, wd_out), (qkv, qkv_out), (ctx, ctx_out), (normed, normed_out),
        (hidden, hidden_out), (act, act_out), (slope, slope_out), (outh, out_half), (two, two_out), (mix, mix_out))
    stores = [pltpu.make_async_copy(near, out, store.at[i]) for i, (near, out) in enumerate(pairs)]
    for i in (0, 1, 5):
        stores[i].start()

    def to_mate(src, dst, i):
        return pltpu.make_async_remote_copy(
            src, dst, send_x.at[i], recv_x.at[i], device_id={"core": 1 - r}, device_id_type=MESH)

    top_half, low_half = pl.ds(0, half), pl.ds(half, half)
    swaps = [
        to_mate(wof, wom, 0), to_mate(ctx.at[low_half], ctxm, 1), to_mate(hidden.at[top_half], hidden.at[low_half], 2),
        to_mate(mate_out.at[pl.ds(0, 256)], mate_in.at[pl.ds(0, 256)], 3),
        to_mate(mate_out.at[pl.ds(256, 256)], mate_in.at[pl.ds(256, 256)], 4), to_mate(mix.at[top_half], mix.at[low_half], 5)]

    rows = 256

    def pair(i, carry):
        base = (i // 2) * 3 * part + lax.rem(i, 2) * 128
        tq[...] = qkv[:, ds(base, 128)]
        tk[...] = qkv[:, ds(base + part, 128)]
        tv[...] = qkv[:, ds(base + 2 * part, 128)]
        seg_k = segr[0:1, :]
        for h in range(2):
            lanes = slice(h * HEAD_DIM, (h + 1) * HEAD_DIM)
            k, v = tk[:, lanes], tv[:, lanes]
            for start in range(0, length, rows):
                q = tq[start : start + rows, lanes]
                s = lax.dot_general(q, k, CONTRACT_LAST, preferred_element_type=F32) * (scale * LOG2E)
                s = jnp.where(segc[start : start + rows, 0:1] == seg_k, s, -1e9 * LOG2E)
                top = jnp.max(s, axis=1, keepdims=True)
                e = jnp.exp2(s - top)
                total = jnp.sum(e, axis=1, keepdims=True)
                out = jnp.dot(e.astype(BF), v, preferred_element_type=F32) / total
                tc[start : start + rows, lanes] = out.astype(BF)
                log_total = top + jnp.log2(total)
                lse[i, h : h + 1, start : start + rows] = jnp.transpose(jnp.broadcast_to(log_total, (rows, 128)))[0:1, :]
            for at, n in ATTEND_STEPS:
                if at[1] == h:
                    @pl.when(i == at[0])
                    def _():
                        advance(n)
        ctx[:, ds(i * 128, 128)] = tc[...]

        @pl.when(i == 2)
        def _():
            finish_weight(1)
            swaps[0].start()
            stores[2].start()
        return carry
    lax.fori_loop(0, ctx.shape[1] // 128, pair, 0)

    swaps[1].start()
    stores[6].start()
    for i in range(10 + len(ATTEND_STEPS), 16):
        advance(i)
    c_step(*steps[13])
    rowsf = parf[...].astype(F32)
    swaps[0].wait_recv()
    swaps[1].wait_recv()

    def out_rows(t, carry):
        place = ds(t * 256, 256)
        value = jnp.dot(ctx[place, :], wof[...], preferred_element_type=F32) + jnp.dot(ctxm[place, :], wom[...], preferred_element_type=F32)
        value = xf[place, :].astype(F32) + value + rowsf[2:3]
        out, norm, inv = normalize(value, rowsf[3:4], rowsf[4:5])
        hidden_one[place, :] = out
        normed[place, :] = norm
        inverse[place, :] = inv
        hidden[place, :] = out.astype(BF)
        return carry
    lax.fori_loop(0, half // 256, out_rows, 0)
    swaps[2].start()
    stores[7].start()
    c_step(*steps[14])
    c_step(*steps[15])
    finish_weight(2)
    stores[3].start()
    n = act.shape[1] // 2
    bias = []
    for j in range(2):
        block = parf[:, ds(r * 2 * part + j * part, part)].astype(F32)
        bias.append(jnp.concatenate([block[8 + k : 9 + k] for k in range(4)], axis=1))

    def up_rows(t, carry):
        place = ds(t * 256, 256)
        for j in range(2):
            lanes = slice(j * n, (j + 1) * n)
            value = jnp.dot(hidden[place, :], wuf[:, lanes], preferred_element_type=F32) + bias[j]
            gate = 0.5 * (1.0 + lax.erf(value * math.sqrt(0.5)))
            act[place, lanes] = (value * gate).astype(BF)
            slope[place, lanes] = (gate + value * (math.sqrt(0.5 / math.pi) * jnp.exp(-0.5 * value * value))).astype(BF)
        return carry
    lax.fori_loop(0, half // 256, up_rows, 0)
    swaps[2].wait_recv()
    stores[8].start()
    lax.fori_loop(half // 256, length // 256, up_rows, 0)
    stores[9].start()
    stores[10].start()
    finish_weight(3)
    stores[4].start()
    vec[...] = jnp.zeros(vec.shape, F32)
    for t in range(2):
        mate_out[t * 256 : (t + 1) * 256, :] = jnp.dot(
            act[half + t * 256 : half + (t + 1) * 256, :], wdf[...], preferred_element_type=F32)
        swaps[3 + t].start()
    for q in range(4):
        wait_for(ogh.at[:, pl.ds(q * 256, 256)], recv_g.at[q])
    for t in range(2):
        place = slice(t * 256, (t + 1) * 256)
        value = jnp.dot(act[place, :], wdf[...], preferred_element_type=F32)
        swaps[3 + t].wait_recv()
        value = hidden_one[place, :] + (value + mate_in[place, :]) + rowsf[5:6]
        out, norm, inv = normalize(value, rowsf[6:7], rowsf[7:8])
        outh[place, :] = out.astype(BF)
        dy = ogh[place, :].astype(F32)
        scaled = dy * rowsf[6:7]
        mean = jnp.mean(scaled, axis=1, keepdims=True)
        slant = jnp.mean(scaled * norm, axis=1, keepdims=True)
        grad = inv * (scaled - mean - norm * slant)
        two[place, :] = grad
        mix[place, :] = grad.astype(BF)
        vec[3:4, :] += jnp.sum(grad, axis=0, keepdims=True)
        vec[4:5, :] += jnp.sum(dy * norm, axis=0, keepdims=True)
        vec[5:6, :] += jnp.sum(dy, axis=0, keepdims=True)
    swaps[5].start()
    stores[11].start()
    stores[12].start()
    for s in range(1, 4):
        par_copy(s).wait_send()
    seg_send.wait_send()
    swaps[5].wait_recv()
    stores[13].start()
    for copy in swaps:
        copy.wait_send()
    for q in range(4):
        mate_copy(q).wait_send()
    for which in range(2):
        for k in range(2):
            for h in range(2):
                token_copy(which, k, h, True)
    for w in range(4):
        for up in (0, 1):
            @pl.when(outer(up))
            def _():
                a_copy(w, up).wait_send()

        @pl.when(r != owner)
        def _():
            mate_part(w).wait_send()

        for j in range(2):
            @pl.when(2 * r + j != c)
            def _():
                for rr in range(2):
                    for up in (0, 1):
                        forward(w, j, rr, up, True)
                    for p in range(2):
                        b_copy(w, j, rr, p).wait_send()
                        c_copy(w, j, rr, p).wait_send()
    for copy in stores:
        copy.wait()


ATTEND_STEPS = (((0, 0), 10), ((0, 1), 11), ((1, 1), 12), ((2, 1), 13), ((3, 0), 14))


def gather(tok, og, par, seg, weights, scale):
    dma = pltpu.SemaphoreType.DMA
    vmem, anywhere = pl.BlockSpec(memory_space=pltpu.VMEM), pl.BlockSpec(memory_space=pl.ANY)
    half, width = tok.shape[0] // 4, tok.shape[1] * 4
    length, heads, units = 2 * half, weights[1].shape[0] * 2, weights[2].shape[1] * 2
    rows = (half, width)
    out = [((16, width), BF), ((heads // 128, 2, length), F32), ((length, 128), jnp.int32), ((8, length), jnp.int32), ((half, 1), F32), ((16, width), F32)]
    large = [((length, width), BF)] + [((w.shape[0] * 2, w.shape[1] * 2), BF) for w in weights]
    large += [((length, 3 * heads), BF), ((length, heads), BF), (rows, F32), ((length, width), BF), ((length, units), BF), ((length, units), BF)]
    large += [(rows, BF), (rows, F32), ((length, width), BF)]
    scratch = large + [(rows, BF), ((heads, width), BF), ((half, heads), BF)] + [(rows, F32)] * 3 + [((2,) + seg.shape, jnp.int32)]
    scratch += [((length, 128), BF)] * 4
    sems = [(4, 2), (4, 4), (4, 4)] + [(4, 4, 2)] * 4 + [(4,)] * 10 + [(1,), (2,), (6,), (6,), (14,)]
    return pl.pallas_call(
        partial(gather_kernel, scale=scale),
        out_shape=[jax.ShapeDtypeStruct(s, t) for s, t in out + large],
        in_specs=[vmem] * 8,
        out_specs=[vmem] * 6 + [anywhere] * 14,
        scratch_shapes=[pltpu.VMEM(s, t) for s, t in scratch] + [dma(s) for s in sems],
        compiler_params=pltpu.CompilerParams(collective_id=0, has_side_effects=True, vmem_limit_bytes=VMEM_LIMIT),
        name="gather",
    )(tok, og, par, seg, *weights)


def mid_kernel(
    inverse, gain, vec_in, out_half, act_far, cols_far, mix_far, slope_far, wd_far, two_far, normed_far, hidden_far, wu_far, wo_far, ctx_far,
    outp, gu_out, go, do, one_grad, vec, gsum,
    act, attn, mix, slope, wd, two_grad, normed, hidden, wu, wo, ctx, gd, gu, up_low, ub, mate_out, mate_in, first, second,
    send1, recv1, send2, recv2, send_y, recv_y, send_m, recv_m, load, store,
):
    d, r, c = lax.axis_index("dp"), lax.axis_index("core"), lax.axis_index("col")
    a, b = d // 2, lax.rem(d, 2)
    barrier = pltpu.get_barrier_semaphore()
    for s in range(4):
        for o in range(2):
            if s or o:
                target = {"core": lax.rem(r + o, 2), "col": lax.rem(c + s, 4)}
                pl.semaphore_signal(barrier, inc=1, device_id=target, device_id_type=MESH)
    x_peer, y_peer = lax.bitwise_xor(d, 1), lax.bitwise_xor(d, 2)
    for p in (x_peer, y_peer):
        pl.semaphore_signal(barrier, inc=1, device_id={"dp": p}, device_id_type=MESH)
    pl.semaphore_wait(barrier, 9)

    half, n = out_half.shape[0], gd.shape[1] // 2
    size = gd.shape[0] // 4

    def local(j, slab):
        return gd.at[ds(slab * size, size), pl.ds(j * n, n)]

    def slab_of(j, i, mine):
        if j == 0:
            return i * 2 + (b if mine else 1 - b)
        return (a if mine else 1 - a) * 2 + i

    def turn(j, kept):
        own = a if j == 0 else b
        return own if kept else 1 - own

    def copy1(j, kept):
        i = turn(j, kept)
        return pltpu.make_async_remote_copy(
            local(j, slab_of(j, i, False)), first.at[j, i], send1.at[j, i], recv1.at[j, i],
            device_id={"dp": x_peer if j == 0 else y_peer}, device_id_type=MESH)

    def copy2(j):
        return pltpu.make_async_remote_copy(
            first.at[j, turn(j, False)], second.at[j], send2.at[j], recv2.at[j],
            device_id={"dp": y_peer if j == 0 else x_peer}, device_id_type=MESH)

    def token_copy(q, wait):
        rr, k = c // 2, lax.rem(c, 2)
        sref = out_half.at[:, pl.ds(q * 256, 256)]
        dref = outp.at[ds(k * 2 * half + r * half, half)]
        sem = recv_y.at[k * 2 + r]
        me = jnp.logical_and(rr == r, q == c)
        remote = pltpu.make_async_remote_copy(
            sref, dref, send_y.at[q], sem, device_id={"core": rr, "col": q}, device_id_type=MESH)
        if not wait:
            @pl.when(me)
            def _():
                pltpu.make_async_copy(sref, dref, sem).start()

        @pl.when(jnp.logical_not(me))
        def _():
            remote.wait_send() if wait else remote.start()

    for q in range(4):
        token_copy(q, False)
    far_near = (
        (cols_far, attn), (act_far, act), (mix_far, mix), (wd_far, wd), (slope_far, slope), (wu_far, wu), (two_far, two_grad),
        (normed_far, normed), (hidden_far, hidden), (wo_far, wo), (ctx_far, ctx))
    loads = [pltpu.make_async_copy(far, near, load.at[i]) for i, (far, near) in enumerate(far_near)]
    for copy in loads:
        copy.start()
    vec[...] = vec_in[...]
    ub[...] = jnp.zeros(ub.shape, F32)
    loads[0].wait()
    loads[1].wait()

    def down_rows(t, carry):
        slab = lax.bitwise_xor(d, 3 - t)
        xt = jnp.transpose(attn[:, ds(slab * size, size)])
        for j in range(2):
            lanes = slice(j * n, (j + 1) * n)
            gd[ds(slab * size, size), lanes] = jnp.dot(xt, act[:, lanes], preferred_element_type=F32).astype(BF)
        for k, sends in ((0, ((0, False), (1, False))), (1, ((1, True),)), (2, ((0, True),))):
            @pl.when(t == k)
            def _():
                for j, kept in sends:
                    copy1(j, kept).start()
        return carry
    lax.fori_loop(0, 4, down_rows, 0)
    for copy in loads[2:5]:
        copy.wait()

    def up_rows(t, carry):
        place = ds(t * 256, 256)
        for j in range(2):
            lanes = slice(j * n, (j + 1) * n)
            value = lax.dot_general(mix[place, :], wd[lanes, :], CONTRACT_LAST, preferred_element_type=F32) * slope[place, lanes].astype(F32)
            up_low[place, lanes] = value.astype(BF)
            ub[0:1, lanes] += jnp.sum(value, axis=0, keepdims=True)
        return carry
    lax.fori_loop(0, 2 * half // 256, up_rows, 0)

    loads[5].wait()

    def mate_rows(t, carry):
        mate_out[ds(t * 256, 256), :] = lax.dot_general(
            up_low[ds(half + t * 256, 256), :], wu[...], CONTRACT_LAST, preferred_element_type=F32)
        return carry
    lax.fori_loop(0, half // 256, mate_rows, 0)
    mate = pltpu.make_async_remote_copy(
        mate_out, mate_in, send_m.at[0], recv_m.at[0], device_id={"core": 1 - r}, device_id_type=MESH)
    mate.start()
    for copy in loads[6:]:
        copy.wait()

    for j in range(2):
        give = turn(j, False)
        wait_for(first.at[j, give], recv1.at[j, give])
        src, dst = local(j, slab_of(j, give, True)), first.at[j, give]

        def add_two(t, carry):
            rows = ds(t * 64, 64, 64)
            dst[rows, :] = (src[rows, :].astype(F32) + dst[rows, :].astype(F32)).astype(BF)
            return carry
        lax.fori_loop(0, size // 64, add_two, 0)
        copy2(j).start()

    mate.wait_recv()
    width = mate_in.shape[1]
    vec[0:3, :] = jnp.zeros((3, width), F32)

    def own_rows(t, carry):
        place = ds(t * 256, 256)
        value = lax.dot_general(up_low[place, :], wu[...], CONTRACT_LAST, preferred_element_type=F32)
        value = value + mate_in[place, :] + two_grad[place, :]
        norm = normed[place, :]
        scaled = value * gain[...]
        mean = jnp.mean(scaled, axis=1, keepdims=True)
        slant = jnp.mean(scaled * norm, axis=1, keepdims=True)
        grad = inverse[place, :] * (scaled - mean - norm * slant)
        one_grad[place, :] = grad
        attn[place, :] = grad.astype(BF)
        vec[0:1, :] += jnp.sum(grad, axis=0, keepdims=True)
        vec[1:2, :] += jnp.sum(value * norm, axis=0, keepdims=True)
        vec[2:3, :] += jnp.sum(value, axis=0, keepdims=True)
        return carry
    lax.fori_loop(0, half // 256, own_rows, 0)
    pair = pltpu.make_async_remote_copy(
        attn.at[pl.ds(0, half)], attn.at[pl.ds(half, half)], send_m.at[1], recv_m.at[1],
        device_id={"core": 1 - r}, device_id_type=MESH)
    pair.start()

    def weight_rows(t, carry):
        xt = jnp.transpose(hidden[:, ds(t * 256, 256)])
        for j in range(2):
            lanes = slice(j * n, (j + 1) * n)
            gu[ds(t * 256, 256), lanes] = jnp.dot(xt, up_low[:, lanes], preferred_element_type=F32).astype(BF)
        return carry
    lax.fori_loop(0, hidden.shape[1] // 256, weight_rows, 0)
    gu_store = pltpu.make_async_copy(gu, gu_out, store.at[0])
    gu_store.start()
    part = n // 4
    for k in range(4):
        for j in range(2):
            vec[8 + k : 9 + k, ds(r * 2 * part + j * part, part)] = ub[0:1, j * n + k * part : j * n + (k + 1) * part]
    pair.wait_recv()

    def ctx_rows(t, carry):
        place = ds(t * 256, 256)
        do[place, :] = lax.dot_general(attn[place, :], wo[...], CONTRACT_LAST, preferred_element_type=F32).astype(BF)
        return carry
    lax.fori_loop(0, 2 * half // 256, ctx_rows, 0)

    def out_rows(t, carry):
        xt = jnp.transpose(ctx[:, ds(t * 256, 256)])
        go[ds(t * 256, 256), :] = jnp.dot(xt, attn[...], preferred_element_type=F32).astype(BF)
        return carry
    lax.fori_loop(0, ctx.shape[1] // 256, out_rows, 0)

    for j in range(2):
        kept = turn(j, True)
        wait_for(first.at[j, kept], recv1.at[j, kept])
        wait_for(second.at[j], recv2.at[j])
        src, more = local(j, slab_of(j, kept, True)), first.at[j, kept]

        def add_three(t, carry):
            rows = ds(t * 64, 64, 64)
            value = src[rows, :].astype(F32) + more[rows, :].astype(F32) + second[j, rows, :].astype(F32)
            gsum[j, rows, :] = value.astype(BF)
            return carry
        lax.fori_loop(0, size // 64, add_three, 0)
    for j in range(2):
        for kept in (False, True):
            copy1(j, kept).wait_send()
        copy2(j).wait_send()
    mate.wait_send()
    pair.wait_send()
    gu_store.wait()
    for q in range(4):
        token_copy(q, True)
        wait_for(outp.at[pl.ds(q * half, half)], recv_y.at[q])


def middle(out_half, act, cols, mix, slope, wd, two_grad, normed, inverse, gain, vec, hidden, wu, wo, ctx):
    dma = pltpu.SemaphoreType.DMA
    vmem, anywhere = pl.BlockSpec(memory_space=pltpu.VMEM), pl.BlockSpec(memory_space=pl.ANY)
    half, width = out_half.shape
    slab = (width // 4, act.shape[1] // 2)
    out = [((4 * half, width // 4), BF), (wu.shape, BF), (wo.shape, BF), (ctx.shape, BF), ((half, width), F32), (vec.shape, F32), ((2,) + slab, BF)]
    scratch = [(v.shape, v.dtype) for v in (act, cols, mix, slope, wd, two_grad, normed, hidden, wu, wo, ctx)]
    scratch += [(wu.shape, BF), (wu.shape, BF), (slope.shape, BF)]
    scratch += [((8, slope.shape[1]), F32), ((half, width), F32), ((half, width), F32), ((2, 2) + slab, BF), ((2,) + slab, BF)]
    sems = [(2, 2), (2, 2), (2,), (2,), (4,), (4,), (2,), (2,), (11,), (1,)]
    return pl.pallas_call(
        mid_kernel,
        out_shape=[jax.ShapeDtypeStruct(s, t) for s, t in out],
        in_specs=[vmem] * 3 + [anywhere] * 12,
        out_specs=[anywhere] * 2 + [vmem] * 5,
        scratch_shapes=[pltpu.VMEM(s, t) for s, t in scratch] + [dma(s) for s in sems],
        compiler_params=pltpu.CompilerParams(collective_id=2, has_side_effects=True, vmem_limit_bytes=VMEM_LIMIT),
        name="mid",
    )(inverse, gain, vec, out_half, act, cols, mix, slope, wd, two_grad, normed, hidden, wu, wo, ctx)


def back_kernel(
    lse, segk, segq, vec, qkv_far, do_far, ctx_far, gu_far, go_far, x_far, wq_far, one_far, gsum,
    inp, total, rq, ro, ru, rd,
    qkv, do, ctx, gu, go, x, wq, one_grad, gq, low, tq, tk, tv, tg, vbuf, mate_out, mate_in, in_half,
    r1q, r1o, r1u, r2q, r2o, r2u, r3q, r3o, r3u, r3d, tall, v1, s4, v2,
    send1, recv1, send2, recv2, send3, recv3, send_i, recv_i, send_v, recv_v, send_w, recv_w, send_m, recv_m, load,
    *, scale,
):
    d, r, c = lax.axis_index("dp"), lax.axis_index("core"), lax.axis_index("col")
    a, b = d // 2, lax.rem(d, 2)
    barrier = pltpu.get_barrier_semaphore()
    for s in range(4):
        for o in range(2):
            if s or o:
                target = {"core": lax.rem(r + o, 2), "col": lax.rem(c + s, 4)}
                pl.semaphore_signal(barrier, inc=1, device_id=target, device_id_type=MESH)
    x_peer, y_peer = lax.bitwise_xor(d, 1), lax.bitwise_xor(d, 2)
    plane = [(p, o) for p in range(4) for o in range(2) if p or o]
    for p, o in plane:
        if p:
            target = {"dp": lax.bitwise_xor(d, p), "core": lax.rem(r + o, 2)}
            pl.semaphore_signal(barrier, inc=1, device_id=target, device_id_type=MESH)
    pl.semaphore_wait(barrier, 13)

    grads, sources = (None, go, gu), (None, go_far, gu_far)
    first, second = (r1q, r1o, r1u), (r2q, r2o, r2u)
    third, result = (r3q, r3o, r3u, r3d), (rq, ro, ru, rd)
    by_rows = (True, False, True, True)
    length, part3q = low.shape[0], low.shape[1] // 2
    part = part3q // 3

    def local(w, j, slab, far=False):
        if w == 0:
            return gq.at[j, slab]
        ref = (sources if far else grads)[w]
        rows, cols = ref.shape
        if by_rows[w]:
            return ref.at[ds(slab * (rows // 4), rows // 4), pl.ds(j * (cols // 2), cols // 2)]
        return ref.at[pl.ds(j * (rows // 2), rows // 2), ds(slab * (cols // 4), cols // 4)]

    def slab_of(j, i, mine):
        if j == 0:
            return i * 2 + (b if mine else 1 - b)
        return (a if mine else 1 - a) * 2 + i

    def turn(j, kept):
        own = a if j == 0 else b
        return own if kept else 1 - own

    def copy1(w, j, kept):
        i = turn(j, kept)
        return pltpu.make_async_remote_copy(
            local(w, j, slab_of(j, i, False), True), first[w].at[j, i], send1.at[w, j, i], recv1.at[w, j, i],
            device_id={"dp": x_peer if j == 0 else y_peer}, device_id_type=MESH)

    def copy2(w, j):
        return pltpu.make_async_remote_copy(
            first[w].at[j, turn(j, False)], second[w].at[j], send2.at[w, j], recv2.at[w, j],
            device_id={"dp": y_peer if j == 0 else x_peer}, device_id_type=MESH)

    def copy3(w, j, rr, wait):
        src = gsum.at[j] if w == 3 else first[w].at[j, turn(j, True)]
        src = src.at[pl.ds(rr * 128, 128), :] if by_rows[w] else src.at[:, pl.ds(rr * 128, 128)]
        dst = third[w].at[c]
        z = 2 * r + j
        me = jnp.logical_and(z == c, r == rr)
        remote = pltpu.make_async_remote_copy(
            src, dst, send3.at[w, j, rr], recv3.at[w, c], device_id={"core": rr, "col": z}, device_id_type=MESH)
        if not wait:
            @pl.when(me)
            def _():
                pltpu.make_async_copy(src, dst, recv3.at[w, c]).start()

        @pl.when(jnp.logical_not(me))
        def _():
            remote.wait_send() if wait else remote.start()

    def send_first(w, kept):
        for j in range(2):
            copy1(w, j, kept).start()

    def step2(w):
        for j in range(2):
            give = turn(j, False)
            wait_for(first[w].at[j, give], recv1.at[w, j, give])
            src, dst = local(w, j, slab_of(j, give, True)), first[w].at[j, give]

            def body(t, carry):
                rows = ds(t * 64, 64, 64)
                dst[rows, :] = (src[rows, :].astype(F32) + dst[rows, :].astype(F32)).astype(BF)
                return carry
            lax.fori_loop(0, dst.shape[0] // 64, body, 0)
            copy2(w, j).start()

    def step3(w):
        for j in range(2):
            kept = turn(j, True)
            wait_for(first[w].at[j, kept], recv1.at[w, j, kept])
            wait_for(second[w].at[j], recv2.at[w, j])
            src, dst, more = local(w, j, slab_of(j, kept, True)), first[w].at[j, kept], second[w].at[j]

            def body(t, carry):
                rows = ds(t * 64, 64, 64)
                dst[rows, :] = (src[rows, :].astype(F32) + dst[rows, :].astype(F32) + more[rows, :].astype(F32)).astype(BF)
                return carry
            lax.fori_loop(0, dst.shape[0] // 64, body, 0)
            for rr in range(2):
                copy3(w, j, rr, False)

    def finish(w):
        for z in range(4):
            wait_for(third[w].at[z], recv3.at[w, z])

        def body(t, carry):
            rows = ds(t * 64, 64, 64)
            value = (third[w][0, rows, :].astype(F32) + third[w][1, rows, :].astype(F32)) + (
                third[w][2, rows, :].astype(F32) + third[w][3, rows, :].astype(F32))
            if w == 3:
                tall[rows, :] = value
            else:
                result[w][rows, :] = value
            return carry
        lax.fori_loop(0, third[w].shape[1] // 64, body, 0)
        if w == 3:
            rd[...] = jnp.transpose(tall[...])

    half = in_half.shape[0]

    def token_copy(q, wait):
        rr, k = c // 2, lax.rem(c, 2)
        sref = in_half.at[:, pl.ds(q * 256, 256)]
        dref = inp.at[ds(k * 2 * half + r * half, half)]
        sem = recv_i.at[k * 2 + r]
        me = jnp.logical_and(rr == r, q == c)
        remote = pltpu.make_async_remote_copy(
            sref, dref, send_i.at[q], sem, device_id={"core": rr, "col": q}, device_id_type=MESH)
        if not wait:
            @pl.when(me)
            def _():
                pltpu.make_async_copy(sref, dref, sem).start()

        @pl.when(jnp.logical_not(me))
        def _():
            remote.wait_send() if wait else remote.start()

    def vec_z(s):
        z = lax.rem(c + s, 4)
        return pltpu.make_async_remote_copy(
            vbuf.at[:, ds(z * 256, 256)], v1.at[s], send_v.at[s], recv_v.at[s], device_id={"col": z}, device_id_type=MESH)

    def vec_plane(i):
        p, o = plane[i]
        return pltpu.make_async_remote_copy(
            s4, v2.at[i], send_w.at[i], recv_w.at[i],
            device_id={"dp": lax.bitwise_xor(d, p), "core": lax.rem(r + o, 2)}, device_id_type=MESH)

    mate = pltpu.make_async_remote_copy(
        mate_out, mate_in, send_m.at[0], recv_m.at[0], device_id={"core": 1 - r}, device_id_type=MESH)

    send_first(2, False)
    send_first(2, True)
    for j in range(2):
        for rr in range(2):
            copy3(3, j, rr, False)
    far_near = (
        (qkv_far, qkv), (do_far, do), (ctx_far, ctx), (gu_far, gu), (go_far, go), (x_far, x), (wq_far, wq), (one_far, one_grad))
    loads = [pltpu.make_async_copy(far, near, load.at[i]) for i, (far, near) in enumerate(far_near)]
    for copy in loads:
        copy.start()
    vbuf[...] = vec[...]
    for copy in loads[:3]:
        copy.wait()

    rows = 256

    def pair(i, carry):
        base = (i // 2) * part3q + lax.rem(i, 2) * 128
        tq[...] = qkv[:, ds(base, 128)]
        tg[...] = do[:, ds(i * 128, 128)]
        prod = jnp.transpose(tg[...].astype(F32) * ctx[:, ds(i * 128, 128)].astype(F32))
        tk[...] = qkv[:, ds(base + part, 128)]
        tv[...] = qkv[:, ds(base + 2 * part, 128)]
        seg_q = segq[0:1, :]
        for h in range(2):
            lanes = slice(h * HEAD_DIM, (h + 1) * HEAD_DIM)
            qh, doh = tq[:, lanes], tg[:, lanes]
            delta = jnp.sum(prod[h * HEAD_DIM : (h + 1) * HEAD_DIM], axis=0, keepdims=True)
            top = lse[i, h : h + 1, :]
            dqt = jnp.zeros((HEAD_DIM, length), F32)
            vsum = jnp.zeros((1, HEAD_DIM), F32)
            for start in range(0, length, rows):
                kh = tk[start : start + rows, lanes]
                vh = tv[start : start + rows, lanes]
                s = lax.dot_general(kh, qh, CONTRACT_LAST, preferred_element_type=F32) * (scale * LOG2E)
                s = jnp.where(segk[start : start + rows, 0:1] == seg_q, s, -1e9 * LOG2E)
                p = jnp.exp2(s - top)
                dp = lax.dot_general(vh, doh, CONTRACT_LAST, preferred_element_type=F32)
                g = (p * (dp - delta)).astype(BF)
                dk = jnp.dot(g, qh, preferred_element_type=F32) * scale
                tk[start : start + rows, lanes] = dk.astype(BF)
                dv = jnp.dot(p.astype(BF), doh, preferred_element_type=F32)
                tv[start : start + rows, lanes] = dv.astype(BF)
                vsum += jnp.sum(dv, axis=0, keepdims=True)
                dqt += jnp.dot(jnp.transpose(kh), g, preferred_element_type=F32)
            dq = jnp.transpose(dqt) * scale
            tq[:, lanes] = dq.astype(BF)
            v1[0, h : h + 1, 0:HEAD_DIM] = jnp.sum(dq, axis=0, keepdims=True)
            v1[0, h : h + 1, 128 : 128 + HEAD_DIM] = vsum
        low[:, ds(base, 128)] = tq[...]
        low[:, ds(base + part, 128)] = tk[...]
        low[:, ds(base + 2 * part, 128)] = tv[...]
        place = ds(r * 2 * part + i * 128, 128)
        vbuf[6:7, place] = jnp.concatenate([v1[0, 0:1, 0:HEAD_DIM], v1[0, 1:2, 0:HEAD_DIM]], axis=1)
        vbuf[7:8, place] = jnp.concatenate([v1[0, 0:1, 128 : 128 + HEAD_DIM], v1[0, 1:2, 128 : 128 + HEAD_DIM]], axis=1)

        @pl.when(i == 1)
        def _():
            for copy in loads[3:]:
                copy.wait()
            step2(2)
            send_first(1, False)
            send_first(1, True)
        return carry
    lax.fori_loop(0, do.shape[1] // 128, pair, 0)

    for s in range(1, 4):
        vec_z(s).start()

    def weight_rows(t, carry):
        xt = jnp.transpose(x[:, ds(t * 256, 256)])
        for j in range(2):
            gq[j, t] = jnp.dot(xt, low[:, j * part3q : (j + 1) * part3q], preferred_element_type=F32).astype(BF)
        return carry
    lax.fori_loop(0, 4, weight_rows, 0)
    send_first(0, False)
    send_first(0, True)

    def mate_rows(t, carry):
        mate_out[ds(t * 256, 256), :] = lax.dot_general(
            low[ds(half + t * 256, 256), :], wq[...], CONTRACT_LAST, preferred_element_type=F32)
        return carry
    lax.fori_loop(0, half // 256, mate_rows, 0)
    mate.start()
    step3(2)
    for s in range(1, 4):
        vec_z(s).wait()
    s4[...] = (vbuf[:, ds(c * 256, 256)] + v1[1]) + (v1[2] + v1[3])
    for i in range(7):
        vec_plane(i).start()
    mate.wait_recv()

    def own_rows(t, carry):
        place = ds(t * 256, 256)
        value = lax.dot_general(low[place, :], wq[...], CONTRACT_LAST, preferred_element_type=F32)
        in_half[place, :] = (value + mate_in[place, :] + one_grad[place, :]).astype(BF)
        return carry
    lax.fori_loop(0, half // 256, own_rows, 0)
    for q in range(4):
        token_copy(q, False)
    step2(1)
    step2(0)
    step3(1)
    finish(3)
    for i in range(7):
        vec_plane(i).wait()
    total[...] = ((s4[...] + v2[0]) + (v2[1] + v2[2])) + ((v2[3] + v2[4]) + (v2[5] + v2[6]))
    step3(0)
    for w in (2, 1, 0):
        finish(w)
    for w in range(4):
        for j in range(2):
            for i in range(2):
                if w < 3:
                    copy1(w, j, i).wait_send()
                copy3(w, j, i, True)
            if w < 3:
                copy2(w, j).wait_send()
    mate.wait_send()
    for q in range(4):
        token_copy(q, True)
        wait_for(inp.at[pl.ds(q * half, half)], recv_i.at[q])


def back(x, wq, qkv, do, ctx, lse, segk, segq, one_grad, vec, grads, scale):
    dma = pltpu.SemaphoreType.DMA
    vmem, anywhere = pl.BlockSpec(memory_space=pltpu.VMEM), pl.BlockSpec(memory_space=pl.ANY)
    half, width = one_grad.shape
    far = (qkv, do, ctx, grads[1], grads[0], x, wq, one_grad)
    length, part = 2 * half, width // 4
    out, r1, r2, r3 = [((4 * half, part), BF)] + [((vec.shape[0], part), F32)], [], [], []
    for w, (rows, cols) in enumerate([wq.shape] + [g.shape for g in grads[:2]] + [(4 * grads[2].shape[1], 2 * grads[2].shape[2])]):
        if w in (0, 2, 3):
            out.append(((cols // 2, rows // 8) if w == 3 else (rows // 8, cols // 2), F32))
            slab, piece = (rows // 4, cols // 2), (rows // 8, cols // 2)
        else:
            out.append(((rows // 2, cols // 8), F32))
            slab, piece = (rows // 2, cols // 4), (rows // 2, cols // 8)
        if w < 3:
            r1.append((2, 2) + slab)
            r2.append((2,) + slab)
        r3.append((4,) + piece)
    scratch = [(v.shape, v.dtype) for v in far] + [((2, 4, width // 4, wq.shape[1] // 2), BF), (qkv.shape, BF)] + [((length, 128), BF)] * 4
    scratch += [(vec.shape, F32), ((half, width), F32), ((half, width), F32), ((half, width), BF)]
    scratch += [(s, BF) for s in r1 + r2 + r3] + [(r3[3][1:], F32)]
    scratch += [((4, vec.shape[0], part), F32), ((vec.shape[0], part), F32), ((7, vec.shape[0], part), F32)]
    sems = [(3, 2, 2), (3, 2, 2), (3, 2), (3, 2), (4, 2, 2), (4, 4), (4,), (4,), (4,), (4,), (7,), (7,), (1,), (1,), (8,)]
    return pl.pallas_call(
        partial(back_kernel, scale=scale),
        out_shape=[jax.ShapeDtypeStruct(s, t) for s, t in out],
        in_specs=[vmem] * 4 + [anywhere] * 9,
        out_specs=[anywhere] + [vmem] * 5,
        scratch_shapes=[pltpu.VMEM(s, t) for s, t in scratch] + [dma(s) for s in sems],
        compiler_params=pltpu.CompilerParams(collective_id=1, has_side_effects=True, vmem_limit_bytes=VMEM_LIMIT),
        name="back",
    )(lse, segk, segq, vec, *far, grads[2])


def part_rows(values, groups):
    if groups == 1:
        return values
    rows, cols = values.shape
    return values.reshape(4, groups, 2, rows // (8 * groups), cols).transpose(0, 2, 1, 3, 4).reshape(rows, cols)


def on_device(
    tokens, segment_ids, w_qkv, b_qv, w_out, b_out, norm1_gain, norm1_shift,
    w_up, b_up, w_down, b_down, norm2_gain, norm2_shift, out_grad,
):
    groups = lax.axis_size("rh")
    core, col = lax.axis_index("core"), lax.axis_index("col")
    part = tokens.shape[1]
    scale = 1.0 / math.sqrt(HEAD_DIM)
    wq, wo, wu, wd = w_qkv.reshape(w_qkv.shape[0], 3 * part), w_out, w_up, w_down
    if groups > 1:
        both_rows = ("rh", "core")
        wq, wu = (lax.all_gather(w, both_rows, axis=0, tiled=True) for w in (wq, wu))
        wo, wd = (lax.all_gather(w, both_rows, axis=1, tiled=True) for w in (wo, wd))
        wq, wu = (lax.dynamic_slice_in_dim(w, core * (w.shape[0] // 2), w.shape[0] // 2, 0) for w in (wq, wu))
        wo, wd = (lax.dynamic_slice_in_dim(w, core * (w.shape[1] // 2), w.shape[1] // 2, 1) for w in (wo, wd))
    vectors = [b_qv[0], b_qv[1], b_out, norm1_gain, norm1_shift, b_down, norm2_gain, norm2_shift] + [b_up[k * part : (k + 1) * part] for k in range(4)]
    index = lax.broadcasted_iota(jnp.int32, (16, part), 0)
    par = jnp.zeros((16, part), BF)
    for k, vector in enumerate(vectors):
        par = jnp.where(index == k, vector[None], par)
    (params, lse, seg_col, seg_row, inverse_one, vec, x, wq, wo, wu, wd, qkv, ctx, normed_one, hidden, activated, slope, output, two_grad,
     mix) = gather(tokens, out_grad, par, segment_ids, (wq, wo, wu, wd), scale)
    gain1 = params[3:4].astype(F32)
    x_cols, hidden_cols, mix_cols = x, hidden, mix
    if groups > 1:
        x_cols, hidden_cols, mix_cols = (part_rows(v.T, groups).T for v in (x, hidden, mix))
    output, up_wgrad, out_wgrad, ctx_grad, one_grad, vec, down_sum = middle(
        output, activated, mix_cols, mix, slope, wd, two_grad, normed_one, inverse_one, gain1, vec, hidden_cols, wu, wo, ctx)
    if groups > 1:
        out_wgrad = part_rows(out_wgrad.T, groups).T
    in_grad, sums, qkv_share, out_share, up_share, down_share = back(
        x_cols, wq, qkv, ctx_grad, ctx, lse, seg_col, seg_row, one_grad, vec, (out_wgrad, up_wgrad, down_sum), scale)
    if groups > 1:
        sums = lax.psum(sums, "rh")
        qkv_share, up_share = (lax.psum_scatter(g, "rh", scatter_dimension=0, tiled=True) for g in (qkv_share, up_share))
        out_share, down_share = (lax.psum_scatter(g, "rh", scatter_dimension=1, tiled=True) for g in (out_share, down_share))
    return (
        output,
        in_grad.astype(F32),
        qkv_share.reshape(qkv_share.shape[0], 3, part),
        sums[6:8],
        out_share,
        sums[0],
        sums[1],
        sums[2],
        up_share,
        sums[8:12].reshape(-1),
        down_share,
        sums[3],
        sums[4],
        sums[5],
    )


def solution(mesh):
    dp, row, col = (mesh.shape[name] for name in ("dp", "row", "col"))
    fine = Mesh(mesh.devices.reshape(dp, row // 2, 2, col), ("dp", "rh", "core", "col"))
    row, every = ("rh", "core"), ("dp", "rh", "core")
    return jax.shard_map(
        on_device,
        mesh=fine,
        in_specs=(
            P(every, "col"), P(every, None), P(row, None, "col"), P(None, "col"), P("col", row), P("col"), P("col"), P("col"),
            P(row, "col"), P("col"), P("col", row), P("col"), P("col"), P("col"), P(every, "col"),
        ),
        out_specs=(
            P(every, "col"), P(every, "col"), P(every, None, "col"), P(None, "col"), P("col", every), P("col"), P("col"),
            P("col"), P(every, "col"), P("col"), P("col", every), P("col"), P("col"), P("col"),
        ),
        check_vma=False,
    )
```

time: 559 us -> 306 us (0.55)
  Pallas kernels: 360 us -> 285 us
  matrix products: 72.9 us -> 0 us
  blocking collectives: 62.7 us -> 0 us
  local copies, waits for them, and re-layouts: 30.6 us -> 13.6 us
  waiting for transfers between devices: 13.5 us -> 0 us
  other arithmetic: 13.3 us -> 5.54 us
    pallas_call x4 -> x3, Pallas kernels: 360 us -> 285 us  [the longest x1 126 us: gather(): pl.pallas_call(partial(gather_kernel, scale=scale), out_shape=[jax.ShapeD...]
    dot_general x13 -> x0, matrix products: 72.9 us -> none  [mm(): return lax.dot_general(left, right, dims, preferred_element_type=F32)]
    psum x1 -> x0, blocking collectives: 60.5 us -> none  [on_device(): lax.psum(jnp.concatenate([full, owned], axis=0), ('dp', 'rh', 'core', 'co...]
    ppermute x8 -> x0, waiting for transfers between devices: 13.5 us -> none  [swap(): return lax.ppermute(values, 'core', [(0, 1), (1, 0)])]
    unnamed x88 -> x16, local copies, waits for them, and re-layouts: 15 us -> 6.85 us
    reduce_sum x7 -> x0, other arithmetic: 6.45 us -> none  [the longest x2 2.43 us: normalize_back(): return (grad, jnp.sum(incoming * normed, axis=0), jnp.sum(incoming, axis=0))]
  transfers between devices with their start and end apart: 8 -> 0, of which waited for: 4 -> 0; matrix products, arithmetic and copies ran while one was open for 8% -> 0% of each run, Pallas kernels for 4% -> 0%
where the time goes in v2:
time: 306 us; the launch traced here: 305 us
  Pallas kernels  285 us (93%)
  local copies, waits for them, and re-layouts  13.6 us (4%)
  other arithmetic  5.54 us (2%)
    pallas_call x1, Pallas kernels, gather(): pl.pallas_call(partial(gather_kernel, scale=scale), out_shape=[jax.ShapeD...  126 us
    pallas_call x1, Pallas kernels, back(): pl.pallas_call(partial(back_kernel, scale=scale), out_shape=[jax.ShapeDty...  113 us
    pallas_call x1, Pallas kernels, middle(): pl.pallas_call(mid_kernel, out_shape=[jax.ShapeDtypeStruct(s, t) for s, t...  47.1 us
    unnamed x16, local copies, waits for them, and re-layouts  6.85 us

profile of v2, /device:TPU:9, one launch (start us, length us, event | category | flops | bytes accessed | tf_op | source)
XLA Modules:
  0.0 305.4 jit_solution(59822240780632313)
XLA Ops:
  0.6 0.8 slice_reduce_fusion.1
  1.5 0.8 fusion.1
  2.3 1.4 select_select_fusion.par
  3.8 1.4 copy.31
  5.2 1.2 copy.32.wq
  6.3 125.6 %gather.1 = (bf16[16,1024]{1,0:T(8,128)(2,1)}, f32[4,2,1024]{2,1,0:T(2,128)}, s32[1024,128]{1,0:T(8,128)}, s32[8,1024]{1,0:T(8,128)}, f32[512,1]{1,0:T(8,128)}, ...) custom-call(bf16[2048,256]{1,0:T(8,128)(2,1)} %tok.1, ...), custom_call_target="tpu_custom_call" | custom-call | tf_op jit(solution)/shard_map/gather/pallas_call | solution.py:437
  131.9 1.3 slice_convert_fusion.gain
  133.2 47.1 %mid.1 = (bf16[2048,256]{1,0:T(8,128)(2,1)}, bf16[1024,2048]{1,0:T(8,128)(2,1)}, bf16[512,1024]{1,0:T(8,128)(2,1)}, bf16[1024,512]{1,0:T(8,128)(2,1)}, f32[512,1...) custom-call(f32[512,1]{1,0:T(8,128)} %get-tuple-element.47.inverse, ...), custom_call_target="tpu_custom_call" | custom-call | tf_op jit(solution)/shard_map/mid/pallas_call | solution.py:660
  180.4 112.8 %back.1 = (bf16[2048,256]{1,0:T(8,128)(2,1)}, f32[16,256]{1,0:T(8,128)}, f32[128,768]{1,0:T(8,128)}, f32[256,128]{1,0:T(8,128)}, f32[128,1024]{1,0:T(8,128)}, /*index=5*/f32[1024,128]{1,0:T(8,128)}) custom-call(f32[4,2,1024]{2,1,0:T(2,128)} %get-tuple-element.62.lse, s32[1024,128]{1,0:T(8,128)} %get-tuple-element.63.segk, s32[8,1024]{1,0:T(8,128)} %get-tuple-element.64.segq, ...), custom_call_target="tpu_custom_call" | custom-call | tf_op jit(solution)/shard_map/back/pallas_call | solution.py:977
  293.1 0.0 copy-start
  293.1 1.4 slice.52
  294.5 0.7 slice_bitcast_fusion
  295.2 1.5 fusion
  296.7 0.6 copy.35
  297.3 1.1 copy.33
  298.4 0.0 copy-start.3
  298.5 0.0 copy-start.2
  298.5 0.9 copy.34
  299.4 0.0 copy-start.1
  299.4 2.8 convert_element_type.7
  302.1 0.0 copy-done
  302.1 1.0 copy.40
  303.1 0.0 copy-done.3
  303.1 0.7 copy.41
  303.8 0.0 copy-done.2
  303.8 0.8 copy.42
  304.6 0.0 copy-done.1
  304.6 0.8 copy.43
  (6 shorter events, 0.0 us)
Async XLA Ops:
  293.1 9.0 %copy-start = (bf16[2048,256]{1,0:T(8,128)(2,1)S(1)}, bf16[2048,256]{1,0:T(8,128)(2,1)}, u32[]{:S(2)}) copy-start(bf16[2048,256]{1,0:T(8,128)(2,1)} %get-tuple-element.146) | copy-start | bytes 3145732
  298.4 4.7 %copy-start.3 = (f32[256,128]{1,0:T(8,128)S(1)}, f32[256,128]{1,0:T(8,128)}, u32[]{:S(2)}) copy-start(f32[256,128]{1,0:T(8,128)} %get-tuple-element.150) | copy-start | bytes 393220
  298.5 5.3 %copy-start.2 = (f32[128,1024]{1,0:T(8,128)S(1)}, f32[128,1024]{1,0:T(8,128)}, u32[]{:S(2)}) copy-start(f32[128,1024]{1,0:T(8,128)} %get-tuple-element.154) | copy-start | bytes 1572868
  299.4 5.2 %copy-start.1 = (f32[1024,128]{1,0:T(8,128)S(1)}, f32[1024,128]{1,0:T(8,128)}, u32[]{:S(2)}) copy-start(f32[1024,128]{1,0:T(8,128)} %get-tuple-element.156) | copy-start | bytes 1572868

commit v3 on v2

--- a/solution.py
+++ b/solution.py
@@ -200,28 +200,23 @@
     seg_send.start()
     seg_own.start()
     steps = [(w, near, rr) for w in range(4) for near in (1, 0) for rr in range(2)]
-    lag = 3
-
-    def advance(i):
+
+    def advance(i, lag):
         b_step(*steps[i])
-        if i >= lag:
-            c_step(*steps[i - lag])
-        if i == 1:
-            start_a(1)
-        if i == 3:
-            for k in range(2):
-                for h in range(2):
-                    token_copy(0, k, h, False)
-            start_a(2)
-        if i == 7:
-            start_a(3)
-        if i == 15:
-            for k in range(2):
-                for h in range(2):
-                    token_copy(1, k, h, False)
-
-    for i in range(8):
-        advance(i)
+        c_step(*steps[i - lag])
+
+    for i in range(2):
+        b_step(*steps[i])
+    start_a(1)
+    for i in range(2, 4):
+        b_step(*steps[i])
+    for k in range(2):
+        for h in range(2):
+            token_copy(0, k, h, False)
+    start_a(2)
+    start_a(3)
+    for i in range(4):
+        c_step(*steps[i])
     for q in range(4):
         wait_for(xf.at[pl.ds(0, half), pl.ds(q * 256, 256)], recv_t.at[q])
         mate_copy(q).start()
@@ -234,10 +229,14 @@
     finish_weight(0)
     for q in range(4):
         wait_for(parf.at[:, pl.ds(q * 256, 256)], recv_p.at[q])
-        wait_for(xf.at[pl.ds(half, half), pl.ds(q * 256, 256)], recv_m.at[q])
 
     def project(t, carry):
         place = ds(t * 256, 256)
+
+        @pl.when(t == half // 256)
+        def _():
+            for q in range(4):
+                wait_for(xf.at[pl.ds(half, half), pl.ds(q * 256, 256)], recv_m.at[q])
         for j in range(2):
             lanes = slice(j * 3 * part, (j + 1) * 3 * part)
             value = jnp.dot(xf[place, :], wqf[:, lanes], preferred_element_type=F32)
@@ -246,10 +245,10 @@
             qkv[place, low : low + part] = (value[:, :part] + bias[0:1]).astype(BF)
             qkv[place, low + part : low + 2 * part] = value[:, part : 2 * part].astype(BF)
             qkv[place, low + 2 * part : low + 3 * part] = (value[:, 2 * part :] + bias[1:2]).astype(BF)
-        for k, i in ((0, 8), (2, 9)):
+        for k in range(4):
             @pl.when(t == k)
             def _():
-                advance(i)
+                b_step(*steps[4 + k])
         return carry
     lax.fori_loop(0, length // 256, project, 0)
     pairs = (
@@ -291,11 +290,10 @@
                 tc[start : start + rows, lanes] = out.astype(BF)
                 log_total = top + jnp.log2(total)
                 lse[i, h : h + 1, start : start + rows] = jnp.transpose(jnp.broadcast_to(log_total, (rows, 128)))[0:1, :]
-            for at, n in ATTEND_STEPS:
-                if at[1] == h:
-                    @pl.when(i == at[0])
-                    def _():
-                        advance(n)
+            for k in range(4):
+                @pl.when(i == k)
+                def _():
+                    advance(8 + 2 * k + h, 4)
         ctx[:, ds(i * 128, 128)] = tc[...]
 
         @pl.when(i == 2)
@@ -308,8 +306,10 @@
 
     swaps[1].start()
     stores[6].start()
-    for i in range(10 + len(ATTEND_STEPS), 16):
-        advance(i)
+    for k in range(2):
+        for h in range(2):
+            token_copy(1, k, h, False)
+    c_step(*steps[12])
     c_step(*steps[13])
     rowsf = parf[...].astype(F32)
     swaps[0].wait_recv()
@@ -340,6 +340,11 @@
 
     def up_rows(t, carry):
         place = ds(t * 256, 256)
+
+        @pl.when(t == half // 256)
+        def _():
+            swaps[2].wait_recv()
+            stores[8].start()
         for j in range(2):
             lanes = slice(j * n, (j + 1) * n)
             value = jnp.dot(hidden[place, :], wuf[:, lanes], preferred_element_type=F32) + bias[j]
@@ -347,25 +352,31 @@
             act[place, lanes] = (value * gate).astype(BF)
             slope[place, lanes] = (gate + value * (math.sqrt(0.5 / math.pi) * jnp.exp(-0.5 * value * value))).astype(BF)
         return carry
-    lax.fori_loop(0, half // 256, up_rows, 0)
-    swaps[2].wait_recv()
-    stores[8].start()
-    lax.fori_loop(half // 256, length // 256, up_rows, 0)
+    lax.fori_loop(0, length // 256, up_rows, 0)
     stores[9].start()
     stores[10].start()
     finish_weight(3)
     stores[4].start()
     vec[...] = jnp.zeros(vec.shape, F32)
-    for t in range(2):
-        mate_out[t * 256 : (t + 1) * 256, :] = jnp.dot(
-            act[half + t * 256 : half + (t + 1) * 256, :], wdf[...], preferred_element_type=F32)
-        swaps[3 + t].start()
+
+    def mate_rows(t, carry):
+        mate_out[ds(t * 256, 256), :] = jnp.dot(act[ds(half + t * 256, 256), :], wdf[...], preferred_element_type=F32)
+        for k in range(2):
+            @pl.when(t == k)
+            def _():
+                swaps[3 + k].start()
+        return carry
+    lax.fori_loop(0, half // 256, mate_rows, 0)
     for q in range(4):
         wait_for(ogh.at[:, pl.ds(q * 256, 256)], recv_g.at[q])
-    for t in range(2):
-        place = slice(t * 256, (t + 1) * 256)
+
+    def last_rows(t, carry):
+        place = ds(t * 256, 256)
         value = jnp.dot(act[place, :], wdf[...], preferred_element_type=F32)
-        swaps[3 + t].wait_recv()
+        for k in range(2):
+            @pl.when(t == k)
+            def _():
+                swaps[3 + k].wait_recv()
         value = hidden_one[place, :] + (value + mate_in[place, :]) + rowsf[5:6]
         out, norm, inv = normalize(value, rowsf[6:7], rowsf[7:8])
         outh[place, :] = out.astype(BF)
@@ -379,6 +390,8 @@
         vec[3:4, :] += jnp.sum(grad, axis=0, keepdims=True)
         vec[4:5, :] += jnp.sum(dy * norm, axis=0, keepdims=True)
         vec[5:6, :] += jnp.sum(dy, axis=0, keepdims=True)
+        return carry
+    lax.fori_loop(0, half // 256, last_rows, 0)
     swaps[5].start()
     stores[11].start()
     stores[12].start()
@@ -416,9 +429,6 @@
                         c_copy(w, j, rr, p).wait_send()
     for copy in stores:
         copy.wait()
-
-
-ATTEND_STEPS = (((0, 0), 10), ((0, 1), 11), ((1, 1), 12), ((2, 1), 13), ((3, 0), 14))
 
 
 def gather(tok, og, par, seg, weights, scale):
@@ -446,9 +456,9 @@
 
 
 def mid_kernel(
-    inverse, gain, vec_in, out_half, act_far, cols_far, mix_far, slope_far, wd_far, two_far, normed_far, hidden_far, wu_far, wo_far, ctx_far,
-    outp, gu_out, go, do, one_grad, vec, gsum,
-    act, attn, mix, slope, wd, two_grad, normed, hidden, wu, wo, ctx, gd, gu, up_low, ub, mate_out, mate_in, first, second,
+    inverse, gain, vec_in, out_half, act_far, cols_far, mix_far, slope_far, wd_far, two_far, normed_far, hidden_far, wu_far, wo_far,
+    outp, gu_out, attn_out, do, one_grad, vec, gsum,
+    act, attn, mix, slope, wd, two_grad, normed, hidden, wu, wo, gd, gu, up_low, ub, mate_out, mate_in, first, second,
     send1, recv1, send2, recv2, send_y, recv_y, send_m, recv_m, load, store,
 ):
     d, r, c = lax.axis_index("dp"), lax.axis_index("core"), lax.axis_index("col")
@@ -511,7 +521,7 @@
         token_copy(q, False)
     far_near = (
         (cols_far, attn), (act_far, act), (mix_far, mix), (wd_far, wd), (slope_far, slope), (wu_far, wu), (two_far, two_grad),
-        (normed_far, normed), (hidden_far, hidden), (wo_far, wo), (ctx_far, ctx))
+        (normed_far, normed), (hidden_far, hidden), (wo_far, wo))
     loads = [pltpu.make_async_copy(far, near, load.at[i]) for i, (far, near) in enumerate(far_near)]
     for copy in loads:
         copy.start()
@@ -610,18 +620,14 @@
         for j in range(2):
             vec[8 + k : 9 + k, ds(r * 2 * part + j * part, part)] = ub[0:1, j * n + k * part : j * n + (k + 1) * part]
     pair.wait_recv()
+    attn_store = pltpu.make_async_copy(attn, attn_out, store.at[1])
+    attn_store.start()
 
     def ctx_rows(t, carry):
         place = ds(t * 256, 256)
         do[place, :] = lax.dot_general(attn[place, :], wo[...], CONTRACT_LAST, preferred_element_type=F32).astype(BF)
         return carry
     lax.fori_loop(0, 2 * half // 256, ctx_rows, 0)
-
-    def out_rows(t, carry):
-        xt = jnp.transpose(ctx[:, ds(t * 256, 256)])
-        go[ds(t * 256, 256), :] = jnp.dot(xt, attn[...], preferred_element_type=F32).astype(BF)
-        return carry
-    lax.fori_loop(0, ctx.shape[1] // 256, out_rows, 0)
 
     for j in range(2):
         kept = turn(j, True)
@@ -642,37 +648,38 @@
     mate.wait_send()
     pair.wait_send()
     gu_store.wait()
+    attn_store.wait()
     for q in range(4):
         token_copy(q, True)
         wait_for(outp.at[pl.ds(q * half, half)], recv_y.at[q])
 
 
-def middle(out_half, act, cols, mix, slope, wd, two_grad, normed, inverse, gain, vec, hidden, wu, wo, ctx):
+def middle(out_half, act, cols, mix, slope, wd, two_grad, normed, inverse, gain, vec, hidden, wu, wo):
     dma = pltpu.SemaphoreType.DMA
     vmem, anywhere = pl.BlockSpec(memory_space=pltpu.VMEM), pl.BlockSpec(memory_space=pl.ANY)
     half, width = out_half.shape
     slab = (width // 4, act.shape[1] // 2)
-    out = [((4 * half, width // 4), BF), (wu.shape, BF), (wo.shape, BF), (ctx.shape, BF), ((half, width), F32), (vec.shape, F32), ((2,) + slab, BF)]
-    scratch = [(v.shape, v.dtype) for v in (act, cols, mix, slope, wd, two_grad, normed, hidden, wu, wo, ctx)]
+    out = [((4 * half, width // 4), BF), (wu.shape, BF), (cols.shape, BF), ((2 * half, wo.shape[0]), BF), ((half, width), F32), (vec.shape, F32), ((2,) + slab, BF)]
+    scratch = [(v.shape, v.dtype) for v in (act, cols, mix, slope, wd, two_grad, normed, hidden, wu, wo)]
     scratch += [(wu.shape, BF), (wu.shape, BF), (slope.shape, BF)]
     scratch += [((8, slope.shape[1]), F32), ((half, width), F32), ((half, width), F32), ((2, 2) + slab, BF), ((2,) + slab, BF)]
-    sems = [(2, 2), (2, 2), (2,), (2,), (4,), (4,), (2,), (2,), (11,), (1,)]
+    sems = [(2, 2), (2, 2), (2,), (2,), (4,), (4,), (2,), (2,), (10,), (2,)]
     return pl.pallas_call(
         mid_kernel,
         out_shape=[jax.ShapeDtypeStruct(s, t) for s, t in out],
-        in_specs=[vmem] * 3 + [anywhere] * 12,
-        out_specs=[anywhere] * 2 + [vmem] * 5,
+        in_specs=[vmem] * 3 + [anywhere] * 11,
+        out_specs=[anywhere] * 3 + [vmem] * 4,
         scratch_shapes=[pltpu.VMEM(s, t) for s, t in scratch] + [dma(s) for s in sems],
         compiler_params=pltpu.CompilerParams(collective_id=2, has_side_effects=True, vmem_limit_bytes=VMEM_LIMIT),
         name="mid",
-    )(inverse, gain, vec, out_half, act, cols, mix, slope, wd, two_grad, normed, hidden, wu, wo, ctx)
+    )(inverse, gain, vec, out_half, act, cols, mix, slope, wd, two_grad, normed, hidden, wu, wo)
 
 
 def back_kernel(
-    lse, segk, segq, vec, qkv_far, do_far, ctx_far, gu_far, go_far, x_far, wq_far, one_far, gsum,
+    lse, segk, segq, vec, qkv_far, do_far, ctx_far, gu_far, attn_far, x_far, wq_far, one_far, gsum,
     inp, total, rq, ro, ru, rd,
-    qkv, do, ctx, gu, go, x, wq, one_grad, gq, low, tq, tk, tv, tg, vbuf, mate_out, mate_in, in_half,
-    r1q, r1o, r1u, r2q, r2o, r2u, r3q, r3o, r3u, r3d, tall, v1, s4, v2,
+    qkv, do, ctx, gu, attn, x, wq, one_grad, go, inp_low, gq, low, tq, tk, tv, tg, vbuf, mate_out, mate_in, in_half,
+    r1q, r1o, r1u, r1v, r2q, r2o, r2u, r2v, r3q, r3o, r3u, r3d, r3v, tall, v1, s4, v2,
     send1, recv1, send2, recv2, send3, recv3, send_i, recv_i, send_v, recv_v, send_w, recv_w, send_m, recv_m, load,
     *, scale,
 ):
@@ -692,21 +699,22 @@
             pl.semaphore_signal(barrier, inc=1, device_id=target, device_id_type=MESH)
     pl.semaphore_wait(barrier, 13)
 
-    grads, sources = (None, go, gu), (None, go_far, gu_far)
-    first, second = (r1q, r1o, r1u), (r2q, r2o, r2u)
-    third, result = (r3q, r3o, r3u, r3d), (rq, ro, ru, rd)
-    by_rows = (True, False, True, True)
+    first, second = (r1q, r1o, r1u, None, r1v), (r2q, r2o, r2u, None, r2v)
+    third = (r3q, r3o, r3u, r3d, r3v)
+    by_rows = (True, False, True, True, True)
+    half_up = gu.shape[1] // 4
+    result = (rq, ro, ru.at[:, pl.ds(0, half_up)], rd, ru.at[:, pl.ds(half_up, half_up)])
     length, part3q = low.shape[0], low.shape[1] // 2
     part = part3q // 3
 
     def local(w, j, slab, far=False):
         if w == 0:
             return gq.at[j, slab]
-        ref = (sources if far else grads)[w]
-        rows, cols = ref.shape
-        if by_rows[w]:
-            return ref.at[ds(slab * (rows // 4), rows // 4), pl.ds(j * (cols // 2), cols // 2)]
-        return ref.at[pl.ds(j * (rows // 2), rows // 2), ds(slab * (cols // 4), cols // 4)]
+        if w == 1:
+            rows, cols = go.shape
+            return go.at[pl.ds(j * (rows // 2), rows // 2), ds(slab * (cols // 4), cols // 4)]
+        ref, start = gu_far if far else gu, 2 * j * half_up + (half_up if w == 4 else 0)
+        return ref.at[ds(slab * (gu.shape[0] // 4), gu.shape[0] // 4), pl.ds(start, half_up)]
 
     def slab_of(j, i, mine):
         if j == 0:
@@ -799,7 +807,7 @@
     def token_copy(q, wait):
         rr, k = c // 2, lax.rem(c, 2)
         sref = in_half.at[:, pl.ds(q * 256, 256)]
-        dref = inp.at[ds(k * 2 * half + r * half, half)]
+        dref = inp_low.at[ds(k * 2 * half + r * half, half)]
         sem = recv_i.at[k * 2 + r]
         me = jnp.logical_and(rr == r, q == c)
         remote = pltpu.make_async_remote_copy(
@@ -833,7 +841,7 @@
         for rr in range(2):
             copy3(3, j, rr, False)
     far_near = (
-        (qkv_far, qkv), (do_far, do), (ctx_far, ctx), (gu_far, gu), (go_far, go), (x_far, x), (wq_far, wq), (one_far, one_grad))
+        (qkv_far, qkv), (do_far, do), (ctx_far, ctx), (gu_far, gu), (attn_far, attn), (x_far, x), (wq_far, wq), (one_far, one_grad))
     loads = [pltpu.make_async_copy(far, near, load.at[i]) for i, (far, near) in enumerate(far_near)]
     for copy in loads:
         copy.start()
@@ -883,18 +891,31 @@
         vbuf[6:7, place] = jnp.concatenate([v1[0, 0:1, 0:HEAD_DIM], v1[0, 1:2, 0:HEAD_DIM]], axis=1)
         vbuf[7:8, place] = jnp.concatenate([v1[0, 0:1, 128 : 128 + HEAD_DIM], v1[0, 1:2, 128 : 128 + HEAD_DIM]], axis=1)
 
-        @pl.when(i == 1)
+        @pl.when(i == 0)
         def _():
             for copy in loads[3:]:
                 copy.wait()
             step2(2)
-            send_first(1, False)
-            send_first(1, True)
+            send_first(4, False)
+            send_first(4, True)
+
+        @pl.when(i == 2)
+        def _():
+            step3(2)
+            step2(4)
         return carry
     lax.fori_loop(0, do.shape[1] // 128, pair, 0)
 
     for s in range(1, 4):
         vec_z(s).start()
+
+    def out_rows(t, carry):
+        xt = jnp.transpose(ctx[:, ds(t * 256, 256)])
+        go[ds(t * 256, 256), :] = jnp.dot(xt, attn[...], preferred_element_type=F32).astype(BF)
+        return carry
+    lax.fori_loop(0, ctx.shape[1] // 256, out_rows, 0)
+    send_first(1, False)
+    send_first(1, True)
 
     def weight_rows(t, carry):
         xt = jnp.transpose(x[:, ds(t * 256, 256)])
@@ -911,7 +932,7 @@
         return carry
     lax.fori_loop(0, half // 256, mate_rows, 0)
     mate.start()
-    step3(2)
+    step3(4)
     for s in range(1, 4):
         vec_z(s).wait()
     s4[...] = (vbuf[:, ds(c * 256, 256)] + v1[1]) + (v1[2] + v1[3])
@@ -934,21 +955,26 @@
     for i in range(7):
         vec_plane(i).wait()
     total[...] = ((s4[...] + v2[0]) + (v2[1] + v2[2])) + ((v2[3] + v2[4]) + (v2[5] + v2[6]))
+    finish(2)
+    finish(4)
+    for q in range(4):
+        place = pl.ds(q * half, half)
+        wait_for(inp_low.at[place], recv_i.at[q])
+        inp[place, :] = inp_low[place, :].astype(F32)
     step3(0)
-    for w in (2, 1, 0):
-        finish(w)
-    for w in range(4):
+    finish(1)
+    finish(0)
+    for w in range(5):
         for j in range(2):
             for i in range(2):
-                if w < 3:
+                if w != 3:
                     copy1(w, j, i).wait_send()
                 copy3(w, j, i, True)
-            if w < 3:
+            if w != 3:
                 copy2(w, j).wait_send()
     mate.wait_send()
     for q in range(4):
         token_copy(q, True)
-        wait_for(inp.at[pl.ds(q * half, half)], recv_i.at[q])
 
 
 def back(x, wq, qkv, do, ctx, lse, segk, segq, one_grad, vec, grads, scale):
@@ -957,28 +983,22 @@
     half, width = one_grad.shape
     far = (qkv, do, ctx, grads[1], grads[0], x, wq, one_grad)
     length, part = 2 * half, width // 4
-    out, r1, r2, r3 = [((4 * half, part), BF)] + [((vec.shape[0], part), F32)], [], [], []
-    for w, (rows, cols) in enumerate([wq.shape] + [g.shape for g in grads[:2]] + [(4 * grads[2].shape[1], 2 * grads[2].shape[2])]):
-        if w in (0, 2, 3):
-            out.append(((cols // 2, rows // 8) if w == 3 else (rows // 8, cols // 2), F32))
-            slab, piece = (rows // 4, cols // 2), (rows // 8, cols // 2)
-        else:
-            out.append(((rows // 2, cols // 8), F32))
-            slab, piece = (rows // 2, cols // 4), (rows // 2, cols // 8)
-        if w < 3:
-            r1.append((2, 2) + slab)
-            r2.append((2,) + slab)
-        r3.append((4,) + piece)
-    scratch = [(v.shape, v.dtype) for v in far] + [((2, 4, width // 4, wq.shape[1] // 2), BF), (qkv.shape, BF)] + [((length, 128), BF)] * 4
+    rows_q, heads, units = wq.shape[1] // 2, do.shape[1], grads[1].shape[1] // 2
+    slab, own, cut = width // 4, width // 8, units // 2
+    out = [((4 * half, part), F32), ((vec.shape[0], part), F32), ((own, rows_q), F32), ((heads // 2, own), F32), ((own, units), F32), ((units, own), F32)]
+    slabs = [(slab, rows_q), (heads // 2, slab), (slab, cut), (slab, cut)]
+    r1, r2 = [(2, 2) + v for v in slabs], [(2,) + v for v in slabs]
+    r3 = [(4, own, rows_q), (4, heads // 2, own), (4, own, cut), (4, own, units), (4, own, cut)]
+    scratch = [(v.shape, v.dtype) for v in far] + [((heads, width), BF), ((4 * half, part), BF), ((2, 4, width // 4, wq.shape[1] // 2), BF), (qkv.shape, BF)] + [((length, 128), BF)] * 4
     scratch += [(vec.shape, F32), ((half, width), F32), ((half, width), F32), ((half, width), BF)]
     scratch += [(s, BF) for s in r1 + r2 + r3] + [(r3[3][1:], F32)]
     scratch += [((4, vec.shape[0], part), F32), ((vec.shape[0], part), F32), ((7, vec.shape[0], part), F32)]
-    sems = [(3, 2, 2), (3, 2, 2), (3, 2), (3, 2), (4, 2, 2), (4, 4), (4,), (4,), (4,), (4,), (7,), (7,), (1,), (1,), (8,)]
+    sems = [(5, 2, 2), (5, 2, 2), (5, 2), (5, 2), (5, 2, 2), (5, 4), (4,), (4,), (4,), (4,), (7,), (7,), (1,), (1,), (8,)]
     return pl.pallas_call(
         partial(back_kernel, scale=scale),
         out_shape=[jax.ShapeDtypeStruct(s, t) for s, t in out],
         in_specs=[vmem] * 4 + [anywhere] * 9,
-        out_specs=[anywhere] + [vmem] * 5,
+        out_specs=[vmem] * 6,
         scratch_shapes=[pltpu.VMEM(s, t) for s, t in scratch] + [dma(s) for s in sems],
         compiler_params=pltpu.CompilerParams(collective_id=1, has_side_effects=True, vmem_limit_bytes=VMEM_LIMIT),
         name="back",
@@ -1018,19 +1038,19 @@
     x_cols, hidden_cols, mix_cols = x, hidden, mix
     if groups > 1:
         x_cols, hidden_cols, mix_cols = (part_rows(v.T, groups).T for v in (x, hidden, mix))
-    output, up_wgrad, out_wgrad, ctx_grad, one_grad, vec, down_sum = middle(
-        output, activated, mix_cols, mix, slope, wd, two_grad, normed_one, inverse_one, gain1, vec, hidden_cols, wu, wo, ctx)
+    output, up_wgrad, attn, ctx_grad, one_grad, vec, down_sum = middle(
+        output, activated, mix_cols, mix, slope, wd, two_grad, normed_one, inverse_one, gain1, vec, hidden_cols, wu, wo)
     if groups > 1:
-        out_wgrad = part_rows(out_wgrad.T, groups).T
+        attn = part_rows(attn.T, groups).T
     in_grad, sums, qkv_share, out_share, up_share, down_share = back(
-        x_cols, wq, qkv, ctx_grad, ctx, lse, seg_col, seg_row, one_grad, vec, (out_wgrad, up_wgrad, down_sum), scale)
+        x_cols, wq, qkv, ctx_grad, ctx, lse, seg_col, seg_row, one_grad, vec, (attn, up_wgrad, down_sum), scale)
     if groups > 1:
         sums = lax.psum(sums, "rh")
         qkv_share, up_share = (lax.psum_scatter(g, "rh", scatter_dimension=0, tiled=True) for g in (qkv_share, up_share))
         out_share, down_share = (lax.psum_scatter(g, "rh", scatter_dimension=1, tiled=True) for g in (out_share, down_share))
     return (
         output,
-        in_grad.astype(F32),
+        in_grad,
         qkv_share.reshape(qkv_share.shape[0], 3, part),
         sums[6:8],
         out_share,

time: 306 us -> 303 us (level)
    pallas_call x1, Pallas kernels: 113 us -> 105 us  [back(): pl.pallas_call(partial(back_kernel, scale=scale), out_shape=[jax.ShapeDty...]
    pallas_call x1, Pallas kernels: 126 us -> 132 us  [gather(): pl.pallas_call(partial(gather_kernel, scale=scale), out_shape=[jax.ShapeD...]
    unnamed x16 -> x19, local copies, waits for them, and re-layouts: 6.85 us -> 8.17 us
where the time goes in v3:
time: 303 us; the launch traced here: 302 us
  Pallas kernels  283 us (93%)
  local copies, waits for them, and re-layouts  15 us (5%)
    pallas_call x1, Pallas kernels, gather(): pl.pallas_call(partial(gather_kernel, scale=scale), out_shape=[jax.ShapeD...  132 us
    pallas_call x1, Pallas kernels, back(): pl.pallas_call(partial(back_kernel, scale=scale), out_shape=[jax.ShapeDty...  105 us
    pallas_call x1, Pallas kernels, middle(): pl.pallas_call(mid_kernel, out_shape=[jax.ShapeDtypeStruct(s, t) for s, t...  46.5 us
    unnamed x19, local copies, waits for them, and re-layouts  8.17 us

profile of v3, /device:TPU:9, one launch (start us, length us, event | category | flops | bytes accessed | tf_op | source)
XLA Modules:
  0.0 301.9 jit_solution(915152288460825054)
XLA Ops:
  0.6 0.8 slice_reduce_fusion.1
  1.5 0.8 fusion.1
  2.3 1.4 select_select_fusion.par
  3.8 1.4 copy.31
  5.2 1.2 copy.32.wq
  6.3 132.0 %gather.1 = (bf16[16,1024]{1,0:T(8,128)(2,1)}, f32[4,2,1024]{2,1,0:T(2,128)}, s32[1024,128]{1,0:T(8,128)}, s32[8,1024]{1,0:T(8,128)}, f32[512,1]{1,0:T(8,128)}, ...) custom-call(bf16[2048,256]{1,0:T(8,128)(2,1)} %tok.1, ...), custom_call_target="tpu_custom_call" | custom-call | tf_op jit(solution)/shard_map/gather/pallas_call | solution.py:447
  138.3 1.3 slice_convert_fusion.gain
  139.6 46.5 %mid.1 = (bf16[2048,256]{1,0:T(8,128)(2,1)}, bf16[1024,2048]{1,0:T(8,128)(2,1)}, bf16[1024,1024]{1,0:T(8,128)(2,1)}, bf16[1024,512]{1,0:T(8,128)(2,1)}, f32[512,...) custom-call(f32[512,1]{1,0:T(8,128)} %get-tuple-element.47.inverse, ...), custom_call_target="tpu_custom_call" | custom-call | tf_op jit(solution)/shard_map/mid/pallas_call | solution.py:667
  186.2 0.0 copy-start.1
  186.2 104.9 %back.1 = (f32[2048,256]{1,0:T(8,128)}, f32[16,256]{1,0:T(8,128)}, f32[128,768]{1,0:T(8,128)}, f32[256,128]{1,0:T(8,128)}, f32[128,1024]{1,0:T(8,128)}, /*index=5*/f32[1024,128]{1,0:T(8,128)}) custom-call(f32[4,2,1024]{2,1,0:T(2,128)} %get-tuple-element.61.lse, s32[1024,128]{1,0:T(8,128)} %get-tuple-element.62.segk, s32[8,1024]{1,0:T(8,128)} %get-tuple-element.63.segq, ...), custom_call_target="tpu_custom_call" | custom-call | tf_op jit(solution)/shard_map/back/pallas_call | solution.py:997
  291.1 0.0 copy-start
  291.1 1.4 slice.52
  292.5 0.7 slice_bitcast_fusion
  293.2 1.5 fusion
  294.7 0.6 copy.35
  295.3 1.1 copy.33
  296.5 0.9 copy.34
  297.4 0.0 copy-done.1
  297.4 1.0 copy.41
  298.4 0.0 copy-done
  298.4 0.0 copy-start.4
  298.4 0.0 copy-start.3
  298.4 0.0 copy-start.2
  298.4 1.3 copy.42
  299.7 0.0 copy-done.4
  299.7 0.7 copy.43
  300.4 0.0 copy-done.3
  300.4 0.8 copy.44
  301.1 0.0 copy-done.2
  301.1 0.8 copy.45
  (6 shorter events, 0.0 us)
Async XLA Ops:
  186.2 111.2 %copy-start.1 = (bf16[2048,256]{1,0:T(8,128)(2,1)S(1)}, bf16[2048,256]{1,0:T(8,128)(2,1)}, u32[]{:S(2)}) copy-start(bf16[2048,256]{1,0:T(8,128)(2,1)} %get-tuple-element.146) | copy-start | bytes 3145732
  291.1 7.3 %copy-start = (f32[2048,256]{1,0:T(8,128)S(1)}, f32[2048,256]{1,0:T(8,128)}, u32[]{:S(2)}) copy-start(f32[2048,256]{1,0:T(8,128)} %get-tuple-element.147) | copy-start | bytes 6291460
  298.4 1.3 copy-start.4
  298.4 2.0 copy-start.3
  298.4 2.8 copy-start.2

commit v4 on v3

--- a/solution.py
+++ b/solution.py
@@ -37,10 +37,10 @@
 
 def gather_kernel(
     tok, og, par, seg, wq, wo, wu, wd,
-    parf, lse, segc, segr, inverse, vec,
+    rows_out, lse, segc, segr, inverse, vec,
     x_out, wq_out, wo_out, wu_out, wd_out, qkv_out, ctx_out, normed_out, hidden_out, act_out, slope_out, out_half, two_out, mix_out,
     xf, wqf, wof, wuf, wdf, qkv, ctx, normed, hidden, act, slope, outh, two, mix,
-    ogh, wom, ctxm, hidden_one, mate_out, mate_in, segs, tq, tk, tv, tc,
+    parf, ogh, wom, ctxm, hidden_one, mate_out, mate_in, segs, tq, tk, tv, tc,
     send_a, recv_a, send_f, send_b, recv_b, send_c, recv_c, recv_l, send_l, send_t, recv_t, send_g, recv_g, send_m, recv_m, send_p, recv_p,
     send_s, recv_s, send_x, recv_x, store,
     *, scale,
@@ -201,22 +201,27 @@
     seg_own.start()
     steps = [(w, near, rr) for w in range(4) for near in (1, 0) for rr in range(2)]
 
-    def advance(i, lag):
+    def tokens_out(which):
+        for k in range(2):
+            for h in range(2):
+                token_copy(which, k, h, False)
+
+    def advance(i):
         b_step(*steps[i])
-        c_step(*steps[i - lag])
-
-    for i in range(2):
-        b_step(*steps[i])
-    start_a(1)
-    for i in range(2, 4):
-        b_step(*steps[i])
-    for k in range(2):
-        for h in range(2):
-            token_copy(0, k, h, False)
-    start_a(2)
-    start_a(3)
-    for i in range(4):
-        c_step(*steps[i])
+        if i >= 3:
+            c_step(*steps[i - 3])
+        if i == 1:
+            start_a(1)
+        if i == 3:
+            tokens_out(0)
+            start_a(2)
+        if i == 7:
+            start_a(3)
+        if i == 15:
+            tokens_out(1)
+
+    for i in range(8):
+        advance(i)
     for q in range(4):
         wait_for(xf.at[pl.ds(0, half), pl.ds(q * 256, 256)], recv_t.at[q])
         mate_copy(q).start()
@@ -245,10 +250,10 @@
             qkv[place, low : low + part] = (value[:, :part] + bias[0:1]).astype(BF)
             qkv[place, low + part : low + 2 * part] = value[:, part : 2 * part].astype(BF)
             qkv[place, low + 2 * part : low + 3 * part] = (value[:, 2 * part :] + bias[1:2]).astype(BF)
-        for k in range(4):
+        for k, i in ((0, 8), (2, 9)):
             @pl.when(t == k)
             def _():
-                b_step(*steps[4 + k])
+                advance(i)
         return carry
     lax.fori_loop(0, length // 256, project, 0)
     pairs = (
@@ -290,10 +295,11 @@
                 tc[start : start + rows, lanes] = out.astype(BF)
                 log_total = top + jnp.log2(total)
                 lse[i, h : h + 1, start : start + rows] = jnp.transpose(jnp.broadcast_to(log_total, (rows, 128)))[0:1, :]
-            for k in range(4):
-                @pl.when(i == k)
-                def _():
-                    advance(8 + 2 * k + h, 4)
+            for place, step in ATTEND_STEPS:
+                if place[1] == h:
+                    @pl.when(i == place[0])
+                    def _():
+                        advance(step)
         ctx[:, ds(i * 128, 128)] = tc[...]
 
         @pl.when(i == 2)
@@ -306,12 +312,10 @@
 
     swaps[1].start()
     stores[6].start()
-    for k in range(2):
-        for h in range(2):
-            token_copy(1, k, h, False)
-    c_step(*steps[12])
+    advance(15)
     c_step(*steps[13])
     rowsf = parf[...].astype(F32)
+    rows_out[...] = rowsf
     swaps[0].wait_recv()
     swaps[1].wait_recv()
 
@@ -431,17 +435,20 @@
         copy.wait()
 
 
+ATTEND_STEPS = (((0, 0), 10), ((0, 1), 11), ((1, 1), 12), ((2, 1), 13), ((3, 0), 14))
+
+
 def gather(tok, og, par, seg, weights, scale):
     dma = pltpu.SemaphoreType.DMA
     vmem, anywhere = pl.BlockSpec(memory_space=pltpu.VMEM), pl.BlockSpec(memory_space=pl.ANY)
     half, width = tok.shape[0] // 4, tok.shape[1] * 4
     length, heads, units = 2 * half, weights[1].shape[0] * 2, weights[2].shape[1] * 2
     rows = (half, width)
-    out = [((16, width), BF), ((heads // 128, 2, length), F32), ((length, 128), jnp.int32), ((8, length), jnp.int32), ((half, 1), F32), ((16, width), F32)]
+    out = [((16, width), F32), ((heads // 128, 2, length), F32), ((length, 128), jnp.int32), ((8, length), jnp.int32), ((half, 1), F32), ((16, width), F32)]
     large = [((length, width), BF)] + [((w.shape[0] * 2, w.shape[1] * 2), BF) for w in weights]
     large += [((length, 3 * heads), BF), ((length, heads), BF), (rows, F32), ((length, width), BF), ((length, units), BF), ((length, units), BF)]
     large += [(rows, BF), (rows, F32), ((length, width), BF)]
-    scratch = large + [(rows, BF), ((heads, width), BF), ((half, heads), BF)] + [(rows, F32)] * 3 + [((2,) + seg.shape, jnp.int32)]
+    scratch = large + [((16, width), BF), (rows, BF), ((heads, width), BF), ((half, heads), BF)] + [(rows, F32)] * 3 + [((2,) + seg.shape, jnp.int32)]
     scratch += [((length, 128), BF)] * 4
     sems = [(4, 2), (4, 4), (4, 4)] + [(4, 4, 2)] * 4 + [(4,)] * 10 + [(1,), (2,), (6,), (6,), (14,)]
     return pl.pallas_call(
@@ -457,9 +464,9 @@
 
 def mid_kernel(
     inverse, gain, vec_in, out_half, act_far, cols_far, mix_far, slope_far, wd_far, two_far, normed_far, hidden_far, wu_far, wo_far,
-    outp, gu_out, attn_out, do, one_grad, vec, gsum,
-    act, attn, mix, slope, wd, two_grad, normed, hidden, wu, wo, gd, gu, up_low, ub, mate_out, mate_in, first, second,
-    send1, recv1, send2, recv2, send_y, recv_y, send_m, recv_m, load, store,
+    outp, gu_out, attn_out, do, one_grad, vec, gsum, early,
+    act, attn, mix, slope, wd, two_grad, normed, hidden, wu, wo, gd, gu, up_low, ub, mate_out, mate_in, first, second, third,
+    send1, recv1, send2, recv2, send3, recv3, send_y, recv_y, send_m, recv_m, load, store,
 ):
     d, r, c = lax.axis_index("dp"), lax.axis_index("core"), lax.axis_index("col")
     a, b = d // 2, lax.rem(d, 2)
@@ -475,10 +482,10 @@
     pl.semaphore_wait(barrier, 9)
 
     half, n = out_half.shape[0], gd.shape[1] // 2
-    size = gd.shape[0] // 4
-
-    def local(j, slab):
-        return gd.at[ds(slab * size, size), pl.ds(j * n, n)]
+    size, cut = gd.shape[0] // 4, n // 2
+
+    def local(p, j, slab):
+        return gd.at[ds(slab * size, size), pl.ds(j * n + p * cut, cut)]
 
     def slab_of(j, i, mine):
         if j == 0:
@@ -489,16 +496,62 @@
         own = a if j == 0 else b
         return own if kept else 1 - own
 
-    def copy1(j, kept):
+    def copy1(p, j, kept):
         i = turn(j, kept)
         return pltpu.make_async_remote_copy(
-            local(j, slab_of(j, i, False)), first.at[j, i], send1.at[j, i], recv1.at[j, i],
+            local(p, j, slab_of(j, i, False)), first.at[p, j, i], send1.at[p, j, i], recv1.at[p, j, i],
             device_id={"dp": x_peer if j == 0 else y_peer}, device_id_type=MESH)
 
-    def copy2(j):
-        return pltpu.make_async_remote_copy(
-            first.at[j, turn(j, False)], second.at[j], send2.at[j], recv2.at[j],
+    def copy2(p, j):
+        return pltpu.make_async_remote_copy(
+            first.at[p, j, turn(j, False)], second.at[p, j], send2.at[p, j], recv2.at[p, j],
             device_id={"dp": y_peer if j == 0 else x_peer}, device_id_type=MESH)
+
+    def copy3(j, rr, wait):
+        src, dst = first.at[0, j, turn(j, True)].at[pl.ds(rr * 128, 128), :], third.at[c]
+        z = 2 * r + j
+        me = jnp.logical_and(z == c, r == rr)
+        remote = pltpu.make_async_remote_copy(
+            src, dst, send3.at[j, rr], recv3.at[c], device_id={"core": rr, "col": z}, device_id_type=MESH)
+        if not wait:
+            @pl.when(me)
+            def _():
+                pltpu.make_async_copy(src, dst, recv3.at[c]).start()
+
+        @pl.when(jnp.logical_not(me))
+        def _():
+            remote.wait_send() if wait else remote.start()
+
+    def step2(p):
+        for j in range(2):
+            give = turn(j, False)
+            wait_for(first.at[p, j, give], recv1.at[p, j, give])
+            src, dst = local(p, j, slab_of(j, give, True)), first.at[p, j, give]
+
+            def add_two(t, carry):
+                rows = ds(t * 64, 64, 64)
+                dst[rows, :] = (src[rows, :].astype(F32) + dst[rows, :].astype(F32)).astype(BF)
+                return carry
+            lax.fori_loop(0, size // 64, add_two, 0)
+            copy2(p, j).start()
+
+    def step3(p):
+        for j in range(2):
+            kept = turn(j, True)
+            wait_for(first.at[p, j, kept], recv1.at[p, j, kept])
+            wait_for(second.at[p, j], recv2.at[p, j])
+            src, more = local(p, j, slab_of(j, kept, True)), first.at[p, j, kept]
+            dst = gsum.at[j] if p else more
+
+            def add_three(t, carry):
+                rows = ds(t * 64, 64, 64)
+                value = src[rows, :].astype(F32) + more[rows, :].astype(F32) + second[p, j, rows, :].astype(F32)
+                dst[rows, :] = value.astype(BF)
+                return carry
+            lax.fori_loop(0, size // 64, add_three, 0)
+            if p == 0:
+                for rr in range(2):
+                    copy3(j, rr, False)
 
     def token_copy(q, wait):
         rr, k = c // 2, lax.rem(c, 2)
@@ -540,7 +593,7 @@
             @pl.when(t == k)
             def _():
                 for j, kept in sends:
-                    copy1(j, kept).start()
+                    copy1(0, j, kept).start()
         return carry
     lax.fori_loop(0, 4, down_rows, 0)
     for copy in loads[2:5]:
@@ -553,6 +606,13 @@
             value = lax.dot_general(mix[place, :], wd[lanes, :], CONTRACT_LAST, preferred_element_type=F32) * slope[place, lanes].astype(F32)
             up_low[place, lanes] = value.astype(BF)
             ub[0:1, lanes] += jnp.sum(value, axis=0, keepdims=True)
+
+        @pl.when(t == 0)
+        def _():
+            step2(0)
+            for kept in (False, True):
+                for j in range(2):
+                    copy1(1, j, kept).start()
         return carry
     lax.fori_loop(0, 2 * half // 256, up_rows, 0)
 
@@ -569,18 +629,7 @@
     for copy in loads[6:]:
         copy.wait()
 
-    for j in range(2):
-        give = turn(j, False)
-        wait_for(first.at[j, give], recv1.at[j, give])
-        src, dst = local(j, slab_of(j, give, True)), first.at[j, give]
-
-        def add_two(t, carry):
-            rows = ds(t * 64, 64, 64)
-            dst[rows, :] = (src[rows, :].astype(F32) + dst[rows, :].astype(F32)).astype(BF)
-            return carry
-        lax.fori_loop(0, size // 64, add_two, 0)
-        copy2(j).start()
-
+    step3(0)
     mate.wait_recv()
     width = mate_in.shape[1]
     vec[0:3, :] = jnp.zeros((3, width), F32)
@@ -590,7 +639,7 @@
         value = lax.dot_general(up_low[place, :], wu[...], CONTRACT_LAST, preferred_element_type=F32)
         value = value + mate_in[place, :] + two_grad[place, :]
         norm = normed[place, :]
-        scaled = value * gain[...]
+        scaled = value * gain[3:4, :]
         mean = jnp.mean(scaled, axis=1, keepdims=True)
         slant = jnp.mean(scaled * norm, axis=1, keepdims=True)
         grad = inverse[place, :] * (scaled - mean - norm * slant)
@@ -601,6 +650,7 @@
         vec[2:3, :] += jnp.sum(value, axis=0, keepdims=True)
         return carry
     lax.fori_loop(0, half // 256, own_rows, 0)
+    step2(1)
     pair = pltpu.make_async_remote_copy(
         attn.at[pl.ds(0, half)], attn.at[pl.ds(half, half)], send_m.at[1], recv_m.at[1],
         device_id={"core": 1 - r}, device_id_type=MESH)
@@ -629,22 +679,18 @@
         return carry
     lax.fori_loop(0, 2 * half // 256, ctx_rows, 0)
 
+    for z in range(4):
+        wait_for(third.at[z], recv3.at[z])
+    value = (third[0].astype(F32) + third[1].astype(F32)) + (third[2].astype(F32) + third[3].astype(F32))
+    early[...] = jnp.transpose(value)
+    step3(1)
     for j in range(2):
-        kept = turn(j, True)
-        wait_for(first.at[j, kept], recv1.at[j, kept])
-        wait_for(second.at[j], recv2.at[j])
-        src, more = local(j, slab_of(j, kept, True)), first.at[j, kept]
-
-        def add_three(t, carry):
-            rows = ds(t * 64, 64, 64)
-            value = src[rows, :].astype(F32) + more[rows, :].astype(F32) + second[j, rows, :].astype(F32)
-            gsum[j, rows, :] = value.astype(BF)
-            return carry
-        lax.fori_loop(0, size // 64, add_three, 0)
-    for j in range(2):
-        for kept in (False, True):
-            copy1(j, kept).wait_send()
-        copy2(j).wait_send()
+        for i in range(2):
+            for p in range(2):
+                copy1(p, j, i).wait_send()
+            copy3(j, i, True)
+        for p in range(2):
+            copy2(p, j).wait_send()
     mate.wait_send()
     pair.wait_send()
     gu_store.wait()
@@ -658,17 +704,17 @@
     dma = pltpu.SemaphoreType.DMA
     vmem, anywhere = pl.BlockSpec(memory_space=pltpu.VMEM), pl.BlockSpec(memory_space=pl.ANY)
     half, width = out_half.shape
-    slab = (width // 4, act.shape[1] // 2)
-    out = [((4 * half, width // 4), BF), (wu.shape, BF), (cols.shape, BF), ((2 * half, wo.shape[0]), BF), ((half, width), F32), (vec.shape, F32), ((2,) + slab, BF)]
+    slab = (width // 4, act.shape[1] // 4)
+    out = [((4 * half, width // 4), BF), (wu.shape, BF), (cols.shape, BF), ((2 * half, wo.shape[0]), BF), ((half, width), F32), (vec.shape, F32), ((2,) + slab, BF), ((slab[1], width // 8), F32)]
     scratch = [(v.shape, v.dtype) for v in (act, cols, mix, slope, wd, two_grad, normed, hidden, wu, wo)]
     scratch += [(wu.shape, BF), (wu.shape, BF), (slope.shape, BF)]
-    scratch += [((8, slope.shape[1]), F32), ((half, width), F32), ((half, width), F32), ((2, 2) + slab, BF), ((2,) + slab, BF)]
-    sems = [(2, 2), (2, 2), (2,), (2,), (4,), (4,), (2,), (2,), (10,), (2,)]
+    scratch += [((8, slope.shape[1]), F32), ((half, width), F32), ((half, width), F32), ((2, 2, 2) + slab, BF), ((2, 2) + slab, BF), ((4, width // 8, slab[1]), BF)]
+    sems = [(2, 2, 2), (2, 2, 2), (2, 2), (2, 2), (2, 2), (4,), (4,), (4,), (2,), (2,), (10,), (2,)]
     return pl.pallas_call(
         mid_kernel,
         out_shape=[jax.ShapeDtypeStruct(s, t) for s, t in out],
         in_specs=[vmem] * 3 + [anywhere] * 11,
-        out_specs=[anywhere] * 3 + [vmem] * 4,
+        out_specs=[anywhere] * 3 + [vmem] * 5,
         scratch_shapes=[pltpu.VMEM(s, t) for s, t in scratch] + [dma(s) for s in sems],
         compiler_params=pltpu.CompilerParams(collective_id=2, has_side_effects=True, vmem_limit_bytes=VMEM_LIMIT),
         name="mid",
@@ -676,7 +722,7 @@
 
 
 def back_kernel(
-    lse, segk, segq, vec, qkv_far, do_far, ctx_far, gu_far, attn_far, x_far, wq_far, one_far, gsum,
+    lse, segk, segq, vec, early, qkv_far, do_far, ctx_far, gu_far, attn_far, x_far, wq_far, one_far, gsum,
     inp, total, rq, ro, ru, rd,
     qkv, do, ctx, gu, attn, x, wq, one_grad, go, inp_low, gq, low, tq, tk, tv, tg, vbuf, mate_out, mate_in, in_half,
     r1q, r1o, r1u, r1v, r2q, r2o, r2u, r2v, r3q, r3o, r3u, r3d, r3v, tall, v1, s4, v2,
@@ -800,7 +846,9 @@
             return carry
         lax.fori_loop(0, third[w].shape[1] // 64, body, 0)
         if w == 3:
-            rd[...] = jnp.transpose(tall[...])
+            cut = tall.shape[1]
+            rd[0:cut, :] = early[...]
+            rd[cut:, :] = jnp.transpose(tall[...])
 
     half = in_half.shape[0]
 
@@ -909,6 +957,15 @@
     for s in range(1, 4):
         vec_z(s).start()
 
+    def weight_rows(t, carry):
+        xt = jnp.transpose(x[:, ds(t * 256, 256)])
+        for j in range(2):
+            gq[j, t] = jnp.dot(xt, low[:, j * part3q : (j + 1) * part3q], preferred_element_type=F32).astype(BF)
+        return carry
+    lax.fori_loop(0, 4, weight_rows, 0)
+    send_first(0, False)
+    send_first(0, True)
+
     def out_rows(t, carry):
         xt = jnp.transpose(ctx[:, ds(t * 256, 256)])
         go[ds(t * 256, 256), :] = jnp.dot(xt, attn[...], preferred_element_type=F32).astype(BF)
@@ -916,15 +973,6 @@
     lax.fori_loop(0, ctx.shape[1] // 256, out_rows, 0)
     send_first(1, False)
     send_first(1, True)
-
-    def weight_rows(t, carry):
-        xt = jnp.transpose(x[:, ds(t * 256, 256)])
-        for j in range(2):
-            gq[j, t] = jnp.dot(xt, low[:, j * part3q : (j + 1) * part3q], preferred_element_type=F32).astype(BF)
-        return carry
-    lax.fori_loop(0, 4, weight_rows, 0)
-    send_first(0, False)
-    send_first(0, True)
 
     def mate_rows(t, carry):
         mate_out[ds(t * 256, 256), :] = lax.dot_general(
@@ -948,8 +996,8 @@
     lax.fori_loop(0, half // 256, own_rows, 0)
     for q in range(4):
         token_copy(q, False)
+    step2(0)
     step2(1)
-    step2(0)
     step3(1)
     finish(3)
     for i in range(7):
@@ -988,7 +1036,7 @@
     out = [((4 * half, part), F32), ((vec.shape[0], part), F32), ((own, rows_q), F32), ((heads // 2, own), F32), ((own, units), F32), ((units, own), F32)]
     slabs = [(slab, rows_q), (heads // 2, slab), (slab, cut), (slab, cut)]
     r1, r2 = [(2, 2) + v for v in slabs], [(2,) + v for v in slabs]
-    r3 = [(4, own, rows_q), (4, heads // 2, own), (4, own, cut), (4, own, units), (4, own, cut)]
+    r3 = [(4, own, rows_q), (4, heads // 2, own), (4, own, cut), (4, own, cut), (4, own, cut)]
     scratch = [(v.shape, v.dtype) for v in far] + [((heads, width), BF), ((4 * half, part), BF), ((2, 4, width // 4, wq.shape[1] // 2), BF), (qkv.shape, BF)] + [((length, 128), BF)] * 4
     scratch += [(vec.shape, F32), ((half, width), F32), ((half, width), F32), ((half, width), BF)]
     scratch += [(s, BF) for s in r1 + r2 + r3] + [(r3[3][1:], F32)]
@@ -997,12 +1045,12 @@
     return pl.pallas_call(
         partial(back_kernel, scale=scale),
         out_shape=[jax.ShapeDtypeStruct(s, t) for s, t in out],
-        in_specs=[vmem] * 4 + [anywhere] * 9,
+        in_specs=[vmem] * 5 + [anywhere] * 9,
         out_specs=[vmem] * 6,
         scratch_shapes=[pltpu.VMEM(s, t) for s, t in scratch] + [dma(s) for s in sems],
         compiler_params=pltpu.CompilerParams(collective_id=1, has_side_effects=True, vmem_limit_bytes=VMEM_LIMIT),
         name="back",
-    )(lse, segk, segq, vec, *far, grads[2])
+    )(lse, segk, segq, vec, grads[3], *far, grads[2])
 
 
 def part_rows(values, groups):
@@ -1034,16 +1082,15 @@
         par = jnp.where(index == k, vector[None], par)
     (params, lse, seg_col, seg_row, inverse_one, vec, x, wq, wo, wu, wd, qkv, ctx, normed_one, hidden, activated, slope, output, two_grad,
      mix) = gather(tokens, out_grad, par, segment_ids, (wq, wo, wu, wd), scale)
-    gain1 = params[3:4].astype(F32)
     x_cols, hidden_cols, mix_cols = x, hidden, mix
     if groups > 1:
         x_cols, hidden_cols, mix_cols = (part_rows(v.T, groups).T for v in (x, hidden, mix))
-    output, up_wgrad, attn, ctx_grad, one_grad, vec, down_sum = middle(
-        output, activated, mix_cols, mix, slope, wd, two_grad, normed_one, inverse_one, gain1, vec, hidden_cols, wu, wo)
+    output, up_wgrad, attn, ctx_grad, one_grad, vec, down_sum, down_early = middle(
+        output, activated, mix_cols, mix, slope, wd, two_grad, normed_one, inverse_one, params, vec, hidden_cols, wu, wo)
     if groups > 1:
         attn = part_rows(attn.T, groups).T
     in_grad, sums, qkv_share, out_share, up_share, down_share = back(
-        x_cols, wq, qkv, ctx_grad, ctx, lse, seg_col, seg_row, one_grad, vec, (attn, up_wgrad, down_sum), scale)
+        x_cols, wq, qkv, ctx_grad, ctx, lse, seg_col, seg_row, one_grad, vec, (attn, up_wgrad, down_sum, down_early), scale)
     if groups > 1:
         sums = lax.psum(sums, "rh")
         qkv_share, up_share = (lax.psum_scatter(g, "rh", scatter_dimension=0, tiled=True) for g in (qkv_share, up_share))

time: 303 us -> 294 us (0.970)
  Pallas kernels: 283 us -> 276 us
    pallas_call x1, Pallas kernels: 132 us -> 126 us  [gather(): pl.pallas_call(partial(gather_kernel, scale=scale), out_shape=[jax.ShapeD...]
where the time goes in v4:
time: 294 us; the launch traced here: 293 us
  Pallas kernels  276 us (94%)
  local copies, waits for them, and re-layouts  15 us (5%)
    pallas_call x1, Pallas kernels, gather(): pl.pallas_call(partial(gather_kernel, scale=scale), out_shape=[jax.ShapeD...  126 us
    pallas_call x1, Pallas kernels, back(): pl.pallas_call(partial(back_kernel, scale=scale), out_shape=[jax.ShapeDty...  106 us
    pallas_call x1, Pallas kernels, middle(): pl.pallas_call(mid_kernel, out_shape=[jax.ShapeDtypeStruct(s, t) for s, t...  44 us
    unnamed x19, local copies, waits for them, and re-layouts  8.17 us

profile of v4, /device:TPU:9, one launch (start us, length us, event | category | flops | bytes accessed | tf_op | source)
XLA Modules:
  0.0 293.1 jit_solution(12690849359024128775)
XLA Ops:
  0.6 0.8 slice_reduce_fusion.1
  1.5 0.8 fusion.1
  2.3 1.4 select_select_fusion.par
  3.8 1.4 copy.31
  5.2 1.2 copy.32.wq
  6.3 126.0 %gather.1 = (f32[16,1024]{1,0:T(8,128)}, f32[4,2,1024]{2,1,0:T(2,128)}, s32[1024,128]{1,0:T(8,128)}, s32[8,1024]{1,0:T(8,128)}, f32[512,1]{1,0:T(8,128)}, /*inde...) custom-call(bf16[2048,256]{1,0:T(8,128)(2,1)} %tok.1, ...), custom_call_target="tpu_custom_call" | custom-call | tf_op jit(solution)/shard_map/gather/pallas_call | solution.py:454
  132.3 44.0 %mid.1 = (bf16[2048,256]{1,0:T(8,128)(2,1)}, bf16[1024,2048]{1,0:T(8,128)(2,1)}, bf16[1024,1024]{1,0:T(8,128)(2,1)}, bf16[1024,512]{1,0:T(8,128)(2,1)}, f32[512,...) custom-call(f32[512,1]{1,0:T(8,128)} %get-tuple-element.48.inverse, ...), custom_call_target="tpu_custom_call" | custom-call | tf_op jit(solution)/shard_map/mid/pallas_call | solution.py:713
  176.3 0.0 copy-start.1
  176.3 105.9 %back.1 = (f32[2048,256]{1,0:T(8,128)}, f32[16,256]{1,0:T(8,128)}, f32[128,768]{1,0:T(8,128)}, f32[256,128]{1,0:T(8,128)}, f32[128,1024]{1,0:T(8,128)}, /*index=5*/f32[1024,128]{1,0:T(8,128)}) custom-call(f32[4,2,1024]{2,1,0:T(2,128)} %get-tuple-element.62.lse, s32[1024,128]{1,0:T(8,128)} %get-tuple-element.63.segk, s32[8,1024]{1,0:T(8,128)} %get-tuple-element.64.segq, ...), custom_call_target="tpu_custom_call" | custom-call | tf_op jit(solution)/shard_map/back/pallas_call | solution.py:1045
  282.2 0.0 copy-start
  282.2 1.4 slice.48
  283.7 0.7 slice_bitcast_fusion
  284.4 1.5 fusion
  285.9 0.6 copy.35
  286.5 1.1 copy.33
  287.6 0.9 copy.34
  288.5 0.0 copy-done.1
  288.6 1.0 copy.41
  289.5 0.0 copy-done
  289.5 0.0 copy-start.4
  289.5 0.0 copy-start.3
  289.5 0.0 copy-start.2
  289.5 1.3 copy.42
  290.9 0.0 copy-done.4
  290.9 0.7 copy.43
  291.5 0.0 copy-done.3
  291.5 0.8 copy.44
  292.3 0.0 copy-done.2
  292.3 0.8 copy.45
  (6 shorter events, 0.0 us)
Async XLA Ops:
  176.3 112.2 %copy-start.1 = (bf16[2048,256]{1,0:T(8,128)(2,1)S(1)}, bf16[2048,256]{1,0:T(8,128)(2,1)}, u32[]{:S(2)}) copy-start(bf16[2048,256]{1,0:T(8,128)(2,1)} %get-tuple-element.148) | copy-start | bytes 3145732
  282.2 7.3 %copy-start = (f32[2048,256]{1,0:T(8,128)S(1)}, f32[2048,256]{1,0:T(8,128)}, u32[]{:S(2)}) copy-start(f32[2048,256]{1,0:T(8,128)} %get-tuple-element.149) | copy-start | bytes 6291460
  289.5 1.3 copy-start.4
  289.5 2.0 copy-start.3
  289.5 2.8 copy-start.2

commit v5 on v4

--- a/solution.py
+++ b/solution.py
@@ -1075,11 +1075,10 @@
         wo, wd = (lax.all_gather(w, both_rows, axis=1, tiled=True) for w in (wo, wd))
         wq, wu = (lax.dynamic_slice_in_dim(w, core * (w.shape[0] // 2), w.shape[0] // 2, 0) for w in (wq, wu))
         wo, wd = (lax.dynamic_slice_in_dim(w, core * (w.shape[1] // 2), w.shape[1] // 2, 1) for w in (wo, wd))
-    vectors = [b_qv[0], b_qv[1], b_out, norm1_gain, norm1_shift, b_down, norm2_gain, norm2_shift] + [b_up[k * part : (k + 1) * part] for k in range(4)]
     index = lax.broadcasted_iota(jnp.int32, (16, part), 0)
-    par = jnp.zeros((16, part), BF)
-    for k, vector in enumerate(vectors):
-        par = jnp.where(index == k, vector[None], par)
+    par = jnp.where(index < 8, jnp.pad(b_qv, ((0, 14), (0, 0))), jnp.pad(b_up.reshape(4, part), ((8, 4), (0, 0))))
+    for k, vector in enumerate((b_out, norm1_gain, norm1_shift, b_down, norm2_gain, norm2_shift)):
+        par = jnp.where(index == k + 2, vector[None], par)
     (params, lse, seg_col, seg_row, inverse_one, vec, x, wq, wo, wu, wd, qkv, ctx, normed_one, hidden, activated, slope, output, two_grad,
      mix) = gather(tokens, out_grad, par, segment_ids, (wq, wo, wu, wd), scale)
     x_cols, hidden_cols, mix_cols = x, hidden, mix

time: 294 us -> 293 us (level)
  no operation moved by 1% of the time
where the time goes in v5:
time: 293 us; the launch traced here: 292 us
  Pallas kernels  276 us (94%)
  local copies, waits for them, and re-layouts  14.1 us (5%)
    pallas_call x1, Pallas kernels, gather(): pl.pallas_call(partial(gather_kernel, scale=scale), out_shape=[jax.ShapeD...  126 us
    pallas_call x1, Pallas kernels, back(): pl.pallas_call(partial(back_kernel, scale=scale), out_shape=[jax.ShapeDty...  106 us
    pallas_call x1, Pallas kernels, middle(): pl.pallas_call(mid_kernel, out_shape=[jax.ShapeDtypeStruct(s, t) for s, t...  43.9 us
    unnamed x19, local copies, waits for them, and re-layouts  8.17 us

profile of v5, /device:TPU:9, one launch (start us, length us, event | category | flops | bytes accessed | tf_op | source)
XLA Modules:
  0.0 292.2 jit_solution(4481873417094785177)
XLA Ops:
  0.7 0.7 reshape.46
  1.4 1.4 select_select_fusion.par
  2.8 1.4 copy.31
  4.2 1.2 copy.32.wq
  5.4 126.0 %gather.1 = (f32[16,1024]{1,0:T(8,128)}, f32[4,2,1024]{2,1,0:T(2,128)}, s32[1024,128]{1,0:T(8,128)}, s32[8,1024]{1,0:T(8,128)}, f32[512,1]{1,0:T(8,128)}, /*inde...) custom-call(bf16[2048,256]{1,0:T(8,128)(2,1)} %tok.1, ...), custom_call_target="tpu_custom_call" | custom-call | tf_op jit(solution)/shard_map/gather/pallas_call | solution.py:454
  131.4 43.9 %mid.1 = (bf16[2048,256]{1,0:T(8,128)(2,1)}, bf16[1024,2048]{1,0:T(8,128)(2,1)}, bf16[1024,1024]{1,0:T(8,128)(2,1)}, bf16[1024,512]{1,0:T(8,128)(2,1)}, f32[512,...) custom-call(f32[512,1]{1,0:T(8,128)} %get-tuple-element.48.inverse, ...), custom_call_target="tpu_custom_call" | custom-call | tf_op jit(solution)/shard_map/mid/pallas_call | solution.py:713
  175.3 0.0 copy-start.1
  175.4 105.9 %back.1 = (f32[2048,256]{1,0:T(8,128)}, f32[16,256]{1,0:T(8,128)}, f32[128,768]{1,0:T(8,128)}, f32[256,128]{1,0:T(8,128)}, f32[128,1024]{1,0:T(8,128)}, /*index=5*/f32[1024,128]{1,0:T(8,128)}) custom-call(f32[4,2,1024]{2,1,0:T(2,128)} %get-tuple-element.62.lse, s32[1024,128]{1,0:T(8,128)} %get-tuple-element.63.segk, s32[8,1024]{1,0:T(8,128)} %get-tuple-element.64.segq, ...), custom_call_target="tpu_custom_call" | custom-call | tf_op jit(solution)/shard_map/back/pallas_call | solution.py:1045
  281.3 0.0 copy-start
  281.3 1.4 slice.24
  282.7 0.7 slice_bitcast_fusion
  283.4 1.5 fusion
  284.9 0.6 copy.35
  285.5 1.1 copy.33
  286.7 0.9 copy.34
  287.6 0.0 copy-done.1
  287.6 1.0 copy.41
  288.6 0.0 copy-done
  288.6 0.0 copy-start.4
  288.6 0.0 copy-start.3
  288.6 0.0 copy-start.2
  288.6 1.3 copy.42
  289.9 0.0 copy-done.4
  289.9 0.7 copy.43
  290.6 0.0 copy-done.3
  290.6 0.8 copy.44
  291.4 0.0 copy-done.2
  291.4 0.8 copy.45
  (4 shorter events, 0.0 us)
Async XLA Ops:
  175.3 112.3 %copy-start.1 = (bf16[2048,256]{1,0:T(8,128)(2,1)S(1)}, bf16[2048,256]{1,0:T(8,128)(2,1)}, u32[]{:S(2)}) copy-start(bf16[2048,256]{1,0:T(8,128)(2,1)} %get-tuple-element.136) | copy-start | bytes 3145732
  281.3 7.3 %copy-start = (f32[2048,256]{1,0:T(8,128)S(1)}, f32[2048,256]{1,0:T(8,128)}, u32[]{:S(2)}) copy-start(f32[2048,256]{1,0:T(8,128)} %get-tuple-element.137) | copy-start | bytes 6291460
  288.6 1.3 copy-start.4
  288.6 2.0 copy-start.3
  288.6 2.8 copy-start.2
